TPU v7x, 128 devices: a whole 4x4x4 slice. The times are simulated.
128 devices in a mesh: dp: 16 (over z, y), tensor: 8 (over x, core).
Axes of the slice: x: 4, y: 4, z: 4, core: 2. Of those that a mesh axis runs over, the one named last changes fastest.
Arguments:
- dense: bfloat16 [3072, 2048], P('dp'), may hold values from -8 to 8
- bottom_weight: bfloat16 [2048, 16384], P(None, 'tensor'), may hold values from -0.125 to 0.125
- bottom_bias: float32 [16384], P('tensor'), may hold values from -3 to 3
- cross_blocks: bfloat16 [80, 512, 512], P('tensor', 'dp'), may hold values from -0.25 to 0.25
- cross_bias: float32 [16384], P('tensor'), may hold values from -3 to 3
- cotangent: bfloat16 [3072, 16384], P('dp', 'tensor'), may hold values from -6 to 6
- in_blocks: int32 [8, 10], replicated, may hold values from 0 to 31, as said below
- out_blocks: int32 [8, 10], replicated, may hold values from 0 to 31, as said below
- live_slots: int32 [8], replicated, may hold values from 2 to 10, as said below
Outputs:
- cross_out: bfloat16 [3072, 16384], P('dp', 'tensor')
- grad_bottom: float32 [2048, 16384], P('dp', 'tensor')
- grad_bias_bottom: float32 [16384], P('tensor')
- grad_blocks: float32 [80, 512, 512], P('tensor', 'dp')
- grad_bias: float32 [16384], P('tensor')
Inputs may be any that keep to these rules, and one draw needn't show every extreme that they name: `in_blocks`: among the live slots of one tensor device, at most 2 have input blocks held by any one tensor device (blocks s * 16384 / (512 * 8) onward for device s), and this most is reached in every draw. `out_blocks`: among the live slots of one tensor device, at most 2 have output blocks held by any one tensor device, and this most is reached in every draw. `live_slots`: some tensor device has all 10 slots live.
All inputs are finite; a program needn't handle non-finite values.
Results may differ from a plain program's by a relative error of at most 0.014.
Values may be sent and summed in bfloat16 or wider, within the bound.
A program may use at most 128 MiB of HBM per device.

v0:
```python
import jax
import jax.numpy as jnp
from jax import lax
from jax.sharding import PartitionSpec as P

BLK = 512
SLOTS = 10


def slot_ranks(owner, alive):
    order = jnp.arange(owner.shape[1])
    earlier = order[None, :] < order[:, None]
    same = (owner[:, :, None] == owner[:, None, :]) & alive[:, None, :] & earlier[None, :, :]
    return jnp.sum(same.astype(jnp.int32), axis=2)


def post_table(owner_mine, rank_mine, alive_mine, groups, capacity):
    slot_count = owner_mine.shape[0]
    match = (
        (owner_mine[None, None, :] == jnp.arange(groups)[:, None, None])
        & (rank_mine[None, None, :] == jnp.arange(capacity)[None, :, None])
        & alive_mine[None, None, :]
    )
    chosen = jnp.sum(match.astype(jnp.int32) * jnp.arange(slot_count)[None, None, :], axis=2)
    filled = jnp.any(match, axis=2)
    return (chosen, filled)


def pack_parts(parts, chosen, filled):
    picked = jnp.take(parts, chosen.reshape(-1), axis=0) * filled.reshape(-1)[:, None, None].astype(
        parts.dtype
    )
    return picked.reshape(chosen.shape[0], chosen.shape[1] * parts.shape[1], parts.shape[2])


def collect_parts(received, owner, local, rank, alive, target, capacity, per_device):
    groups, span_rows, block_width = received.shape
    row_count = span_rows // capacity
    match = ((owner == target) & alive)[:, :, None] & (
        rank[:, :, None] == jnp.arange(capacity)[None, None, :]
    )
    matches = match[:, :, :, None] & (
        local[:, :, None, None] == jnp.arange(per_device)[None, None, None, :]
    )
    onehot = (
        jnp.sum(matches.astype(jnp.int32), axis=1)
        .reshape(groups * capacity, per_device)
        .astype(jnp.bfloat16)
    )
    flattened = received.reshape(groups * capacity, row_count, block_width)
    summed = jnp.einsum("irb,il->rlb", flattened, onehot, preferred_element_type=jnp.float32)
    return summed.reshape(row_count, per_device * block_width)


def ring_gather(x, axis, n):
    half = x.shape[0] // 2
    right = [(i, (i + 1) % n) for i in range(n)]
    left = [(i, (i - 1) % n) for i in range(n)]
    cur_a, cur_b = x[:half], x[half:]
    outs_a, outs_b = [cur_a], [cur_b]
    for _ in range(1, n):
        cur_a = lax.ppermute(cur_a, axis, right)
        cur_b = lax.ppermute(cur_b, axis, left)
        outs_a.append(cur_a)
        outs_b.append(cur_b)
    return jnp.stack(outs_a), jnp.stack(outs_b)


def take_blocks(stack_a, stack_b, owner, local, me, n):
    steps, half, width = stack_a.shape
    blocks_a = stack_a.reshape(steps, half, width // BLK, BLK)
    blocks_b = stack_b.reshape(steps, half, width // BLK, BLK)
    step_a = (me - owner) % n
    step_b = (owner - me) % n
    top = blocks_a[step_a, :, local, :]
    bottom = blocks_b[step_b, :, local, :]
    return jnp.concatenate([top, bottom], axis=1)


def on_device(
    dense,
    bottom_weight,
    bottom_bias,
    cross_blocks,
    cross_bias,
    cotangent,
    in_blocks,
    out_blocks,
    live_slots,
):
    groups = lax.axis_size("tensor")
    mine = lax.axis_index("tensor")
    row_count = dense.shape[0]
    local_width = bottom_weight.shape[1]
    per_device = local_width // BLK
    capacity = -(-SLOTS // groups)
    preact = jnp.dot(dense, bottom_weight, preferred_element_type=jnp.float32) + bottom_bias
    start = jax.nn.silu(preact).astype(jnp.bfloat16)
    start_wide = start.astype(jnp.float32)
    cot_wide = cotangent.astype(jnp.float32)
    grad_mixed = cot_wide * start_wide
    grad_mixed_low = grad_mixed.astype(jnp.bfloat16)
    alive = jnp.arange(SLOTS)[None, :] < live_slots[:, None]
    alive_mine = alive[mine]
    switch = alive_mine.astype(jnp.bfloat16)[:, None, None]
    in_owner = in_blocks // per_device
    in_local = in_blocks % per_device
    out_owner = out_blocks // per_device
    out_local = out_blocks % per_device
    in_rank = slot_ranks(in_owner, alive)
    out_rank = slot_ranks(out_owner, alive)
    combo = jnp.concatenate([start, grad_mixed_low], axis=1)
    stack_a, stack_b = ring_gather(combo, "tensor", groups)
    fetched = take_blocks(stack_a, stack_b, in_owner[mine], in_local[mine], mine, groups)
    taken = fetched
    product = jnp.einsum(
        "kri,kij->krj",
        taken,
        lax.all_gather(cross_blocks, "dp", axis=1, tiled=True),
        preferred_element_type=jnp.float32,
    )
    parts = product.astype(jnp.bfloat16) * switch
    chosen_out, filled_out = post_table(
        out_owner[mine], out_rank[mine], alive_mine, groups, capacity
    )
    arrived_parts = lax.all_to_all(
        pack_parts(parts, chosen_out, filled_out), "tensor", split_axis=0, concat_axis=0, tiled=True
    )
    mixed = (
        collect_parts(
            arrived_parts, out_owner, out_local, out_rank, alive, mine, capacity, per_device
        )
        + cross_bias
    )
    cross_out = (start_wide * mixed + start_wide).astype(jnp.bfloat16)
    upstream = take_blocks(
        stack_a, stack_b, out_owner[mine], out_local[mine] + per_device, mine, groups
    )
    upstream = upstream * switch
    backward = jnp.einsum(
        "krj,kij->kri",
        upstream,
        lax.all_gather(cross_blocks, "dp", axis=1, tiled=True),
        preferred_element_type=jnp.float32,
    )
    back_parts = backward.astype(jnp.bfloat16)
    chosen_in, filled_in = post_table(in_owner[mine], in_rank[mine], alive_mine, groups, capacity)
    arrived_back = lax.all_to_all(
        pack_parts(back_parts, chosen_in, filled_in),
        "tensor",
        split_axis=0,
        concat_axis=0,
        tiled=True,
    )
    grad_start = collect_parts(
        arrived_back, in_owner, in_local, in_rank, alive, mine, capacity, per_device
    )
    block_terms = jnp.einsum("kri,krj->kij", fetched, upstream, preferred_element_type=jnp.float32)
    grad_blocks = lax.psum_scatter(
        block_terms.astype(jnp.bfloat16), "dp", scatter_dimension=1, tiled=True
    ).astype(jnp.float32)
    grad_start = grad_start + cot_wide * mixed + cot_wide
    sigma = jax.nn.sigmoid(preact)
    grad_pre = grad_start * sigma * (1.0 + preact * (1.0 - sigma))
    grad_pre_low = grad_pre.astype(jnp.bfloat16)
    taken = dense
    grad_bottom = lax.psum_scatter(
        lax.dot_general(
            taken, grad_pre_low, (((0,), (0,)), ((), ())), preferred_element_type=jnp.float32
        ).astype(jnp.bfloat16),
        "dp",
        scatter_dimension=0,
        tiled=True,
    ).astype(jnp.float32)
    bias_sums = lax.psum((jnp.sum(grad_pre, axis=0), jnp.sum(grad_mixed, axis=0)), "dp")
    return (cross_out, grad_bottom, bias_sums[0], grad_blocks, bias_sums[1])


def solution(mesh):
    return jax.shard_map(
        on_device,
        mesh=mesh,
        in_specs=(
            P("dp", None),
            P(None, "tensor"),
            P("tensor"),
            P("tensor", "dp", None),
            P("tensor"),
            P("dp", "tensor"),
            P(),
            P(),
            P(),
        ),
        out_specs=(
            P("dp", "tensor"),
            P("dp", "tensor"),
            P("tensor"),
            P("tensor", "dp", None),
            P("tensor"),
        ),
        check_vma=False,
    )
```

profile of v0, /device:TPU:0, one launch (start us, length us, event | category | flops | bytes accessed | tf_op | source)
XLA Modules:
  0.0 354.9 jit_solution(3943194718781024249)
XLA Ops:
  8.3 7.5 %fusion.8 = (f32[2048]{0:T(1024)}, bf16[192,2048]{1,0:T(8,128)(2,1)S(1)}, f32[192,2048]{1,0:T(8,128)}) fusion(bf16[192,2048]{1,0:T(8,128)(2,1)} %param.16, f32[2048]{0:T(1024)} %param.13, bf16[192,2048]{1,0:T(8,128)(2,1)S(1)} %copy-done, bf16[2048,2048]{1,0:T(8,128)(2,1)} %param.12), kind=kOutput, calls=%fused_computation.30 | convolution fusion | flops 1614542848 | bytes 12337152 | tf_op jit(solution)/shard_map/dot_general | solution.py:97
  19.3 9.8 %collective-permute-done = bf16[96,4096]{1,0:T(8,128)(2,1)} collective-permute-done((bf16[96,4096]{1,0:T(8,128)(2,1)S(1)}, bf16[96,4096]{1,0:T(8,128)(2,1)}, u32[]{:S(2)}, u32[]{:S(2)}) %collective-permute-start) | collective-permute-done | bytes 786464 | tf_op jit(solution)/shard_map/ppermute | solution.py:62
  32.7 9.3 %collective-permute-done.1 = bf16[96,4096]{1,0:T(8,128)(2,1)} collective-permute-done((bf16[96,4096]{1,0:T(8,128)(2,1)}, bf16[96,4096]{1,0:T(8,128)(2,1)}, u32[]{:S(2)}, u32[]{:S(2)}) %collective-permute-start.1) | collective-permute-done | bytes 786464 | tf_op jit(solution)/shard_map/ppermute | solution.py:62
  42.0 3.0 collective-permute-start.9
  51.8 3.2 collective-permute-done.2
  55.0 3.2 collective-permute-start.10
  61.8 6.0 %collective-permute-done.3 = bf16[96,4096]{1,0:T(8,128)(2,1)S(1)} collective-permute-done((bf16[96,4096]{1,0:T(8,128)(2,1)}, bf16[96,4096]{1,0:T(8,128)(2,1)S(1)}, u32[]{:S(2)}, u32[]{:S(2)}) %collective-permute-start.3) | collective-permute-done | bytes 786464 | tf_op jit(solution)/shard_map/ppermute | solution.py:62
  68.0 3.2 collective-permute-start.11
  75.4 5.0 %collective-permute-done.4 = bf16[96,4096]{1,0:T(8,128)(2,1)S(1)} collective-permute-done((bf16[96,4096]{1,0:T(8,128)(2,1)S(1)}, bf16[96,4096]{1,0:T(8,128)(2,1)S(1)}, u32[]{:S(2)}, u32[]{:S(2)}) %collective-permute-start.4) | collective-permute-done | bytes 786464 | tf_op jit(solution)/shard_map/ppermute | solution.py:62
  80.8 3.1 collective-permute-start.12
  85.2 7.9 %collective-permute-done.5 = bf16[96,4096]{1,0:T(8,128)(2,1)S(1)} collective-permute-done((bf16[96,4096]{1,0:T(8,128)(2,1)S(1)}, bf16[96,4096]{1,0:T(8,128)(2,1)S(1)}, u32[]{:S(2)}, u32[]{:S(2)}) %collective-permute-start.5) | collective-permute-done | bytes 786464 | tf_op jit(solution)/shard_map/ppermute | solution.py:62
  93.4 3.1 collective-permute-start.13
  97.8 7.9 %collective-permute-done.6 = bf16[96,4096]{1,0:T(8,128)(2,1)S(1)} collective-permute-done((bf16[96,4096]{1,0:T(8,128)(2,1)S(1)}, bf16[96,4096]{1,0:T(8,128)(2,1)S(1)}, u32[]{:S(2)}, u32[]{:S(2)}) %collective-permute-start.6) | collective-permute-done | bytes 786464 | tf_op jit(solution)/shard_map/ppermute | solution.py:62
  109.2 3.4 gather_fusion
  112.6 4.4 %gather_fusion.2 = bf16[10,96,512]{2,1,0:T(8,128)(2,1)} fusion(bf16[8,96,8,512]{3,1,2,0:T(8,128)(2,1)} %copy-done.8, s32[10]{0:T(128)S(1)} %get-tuple-element.52), kind=kCustom, calls=%fused_computation.4 | custom fusion | bytes 1966160 | tf_op jit(solution)/shard_map/gather | solution.py:75
  118.1 3.4 gather_fusion.1
  121.6 4.4 %gather_fusion.3 = bf16[10,96,512]{2,1,0:T(8,128)(2,1)} fusion(bf16[8,96,8,512]{3,1,2,0:T(8,128)(2,1)} %copy_dynamic-update-slice_fusion, s32[10]{0:T(128)S(1)} %get-tuple-element.53), kind=kCustom, calls=%fused_computation.5 | custom fusion | bytes 1966160 | tf_op jit(solution)/shard_map/gather | solution.py:76
  128.1 4.1 %convolution_convert_fusion = bf16[10,512,512]{2,1,0:T(8,128)(2,1)} fusion(bf16[10,192,512]{2,1,0:T(8,128)(2,1)S(1)} %constant_dynamic-update-slice_fusion, bf16[10,96,512]{2,1,0:T(8,128)(2,1)S(1)} %copy-done.10, bf16[10,96,512]{2,1,0:T(8,128)(2,1)S(1)} %copy-done.9, bf16[10]{0:T(256)(128)(2,1)S(1)} %copy-done.19), kind=kOutput, calls=%fused_computation.13 | convolution fusion | flops 1015152640 | bytes 9175060 | tf_op jit(solution)/shard_map/kri,krj->kij/dot_general | solution.py:158
  138.4 4.3 %convert_multiply_fusion.2 = bf16[10,192,512]{2,1,0:T(8,128)(2,1)S(1)} fusion(bf16[10,192,512]{2,1,0:T(8,128)(2,1)} %copy-done.1, bf16[10,512,512]{2,1,0:T(8,128)(2,1)} %all-gather.2.cloned.1.call-done, bf16[10]{0:T(256)(128)(2,1)} %get-tuple-element.45), kind=kOutput, calls=%fused_computation.20 | convolution fusion | flops 1008599040 | bytes 9175060 | tf_op jit(solution)/shard_map/kri,kij->krj/dot_general | solution.py:116
  145.3 3.9 %select_multiply_fusion.1 = bf16[16,192,512]{2,1,0:T(8,128)(2,1)} fusion(bf16[16,192,512]{2,1,0:T(8,128)(2,1)} %gather_fusion.4, pred[16]{0:T(512)(128)(4,1)} %compare_and_fusion.3, bf16[16]{0:T(256)(128)(2,1)} %reshape.558), kind=kLoop, calls=%fused_computation.12 | loop fusion | flops 3145728 | bytes 6291504 | tf_op jit(solution)/shard_map/mul | solution.py:30
  149.2 4.6 %all-to-all-start = ((bf16[8,384,512]{2,1,0:T(8,128)(2,1)}), bf16[8,384,512]{2,1,0:T(8,128)(2,1)}, u32[]{:S(2)}, u32[]{:S(2)}) async-start(bf16[8,384,512]{2,1,0:T(8,128)(2,1)} %bitcast.135), calls=%async_computation | async-start | bytes 6291456 | tf_op jit(solution)/shard_map/all_to_all | solution.py:126
  155.8 5.3 %convolution_convert_fusion.1 = bf16[10,192,512]{2,1,0:T(8,128)(2,1)S(1)} fusion(bf16[10,512,512]{2,1,0:T(8,128)(2,1)} %all-gather.2.cloned.1.call-done, bf16[10,96,512]{2,1,0:T(8,128)(2,1)} %gather_fusion.3, bf16[10,96,512]{2,1,0:T(8,128)(2,1)} %gather_fusion.2, bf16[10]{0:T(256)(128)(2,1)} %get-tuple-element.45), kind=kOutput, calls=%fused_computation.21 | convolution fusion | flops 1013514240 | bytes 9175060 | tf_op jit(solution)/shard_map/krj,kij->kri/dot_general | solution.py:140
  163.7 4.0 %select_multiply_fusion = bf16[16,192,512]{2,1,0:T(8,128)(2,1)} fusion(bf16[16,192,512]{2,1,0:T(8,128)(2,1)} %gather_fusion.5, pred[16]{0:T(512)(128)(4,1)} %compare_and_fusion.2, bf16[16]{0:T(256)(128)(2,1)} %reshape.559), kind=kLoop, calls=%fused_computation.11 | loop fusion | flops 3145728 | bytes 6291504 | tf_op jit(solution)/shard_map/mul | solution.py:30
  167.7 24.5 %all-to-all-done = bf16[8,384,512]{2,1,0:T(8,128)(2,1)} async-done(((bf16[8,384,512]{2,1,0:T(8,128)(2,1)}), bf16[8,384,512]{2,1,0:T(8,128)(2,1)}, u32[]{:S(2)}, u32[]{:S(2)}) %all-to-all-start) | async-done | bytes 3145760 | tf_op jit(solution)/shard_map/all_to_all | solution.py:126
  192.3 4.6 %all-to-all-start.1 = ((bf16[8,384,512]{2,1,0:T(8,128)(2,1)}), bf16[8,384,512]{2,1,0:T(8,128)(2,1)}, u32[]{:S(2)}, u32[]{:S(2)}) async-start(bf16[8,384,512]{2,1,0:T(8,128)(2,1)} %bitcast.134), calls=%async_computation.1 | async-start | bytes 6291456 | tf_op jit(solution)/shard_map/all_to_all | solution.py:148
  197.8 3.8 %fusion.2 = f32[4,192,512]{2,0,1:T(4,128)S(1)} fusion(bf16[16,4,1]{1,0,2:T(8,128)(2,1)S(1)} %bitcast.166, bf16[16,192,512]{2,1,0:T(8,128)(2,1)} %bitcast.10), kind=kOutput, calls=%fused_computation.9 | convolution fusion | flops 12582912 | bytes 4718720 | tf_op jit(solution)/shard_map/irb,il->rlb/dot_general | solution.py:51
  202.2 33.1 %all-to-all-done.1 = bf16[8,384,512]{2,1,0:T(8,128)(2,1)} async-done(((bf16[8,384,512]{2,1,0:T(8,128)(2,1)}), bf16[8,384,512]{2,1,0:T(8,128)(2,1)}, u32[]{:S(2)}, u32[]{:S(2)}) %all-to-all-start.1) | async-done | bytes 3145760 | tf_op jit(solution)/shard_map/all_to_all | solution.py:148
  235.3 4.0 %fusion = f32[4,192,512]{2,0,1:T(4,128)S(1)} fusion(bf16[16,4,1]{1,0,2:T(8,128)(2,1)S(1)} %bitcast.167, bf16[16,192,512]{2,1,0:T(8,128)(2,1)} %bitcast.22), kind=kOutput, calls=%fused_computation.7 | convolution fusion | flops 12582912 | bytes 4718720 | tf_op jit(solution)/shard_map/irb,il->rlb/dot_general | solution.py:51
  241.8 5.6 %convert_bitcast_fusion = bf16[2048,2048]{0,1:T(8,128)(2,1)} fusion(bf16[192,2048]{1,0:T(8,128)(2,1)S(1)} %copy-done, bf16[192,2048]{1,0:T(8,128)(2,1)S(1)} %get-tuple-element.42), kind=kOutput, calls=%fused_computation.6 | convolution fusion | flops 1614807040 | bytes 9961472 | tf_op jit(solution)/shard_map/dot_general | solution.py:168
  247.4 12.4 %copy.125 = bf16[2048,2048]{1,0:T(8,128)(2,1)} copy(bf16[2048,2048]{0,1:T(8,128)(2,1)} %convert_bitcast_fusion) | data formatting | bytes 16777216
  260.5 76.5 %all-reduce = (f32[2048]{0:T(1024)}, f32[2048]{0:T(1024)}) all-reduce(f32[2048]{0:T(1024)S(1)} %get-tuple-element.41, f32[2048]{0:T(1024)S(1)} %copy-done.20), channel_id=1, replica_groups=mesh['dp'=16,'tensor'=8] {'dp'}, use_global_device_ids=true, to_apply=%region_10.12 | all-reduce | flops 4096 | bytes 32768 | tf_op jit(solution)/shard_map/psum | solution.py:175
  338.9 7.0 %reduce-scatter.7.cloned.1.call-done = bf16[128,2048]{1,0:T(8,128)(2,1)} async-done(((bf16[2048,2048]{1,0:T(8,128)(2,1)}), bf16[128,2048]{1,0:T(8,128)(2,1)}) %reduce-scatter.7.cloned.1.call-update) | async-done | bytes 524304
  (172 shorter events, 55.1 us)
Async XLA Ops:
  7.2 131.2 %all-gather.2.cloned.1.call-start = ((), (), s32[]{:S(2)}) async-start(), calls=%async_computation.4 | async-start | bytes 5570560 | tf_op jit(solution)/shard_map/all_gather | solution.py:119
  7.9 7.9 %copy-start.4 = (bf16[192,2048]{1,0:T(8,128)(2,1)S(1)}, bf16[192,2048]{1,0:T(8,128)(2,1)}, u32[]{:S(2)}) copy-start(bf16[192,2048]{1,0:T(8,128)(2,1)} %param.16) | copy-start | bytes 2359300
  7.9 329.0 %reduce-scatter.5.cloned.1.call-start = ((), (), s32[]{:S(2)}) async-start(), calls=%async_computation.5 | async-start | bytes 5570560 | tf_op jit(solution)/shard_map/reduce_scatter | solution.py:159
  15.9 16.2 %copy-start.17 = (s32[8,10]{1,0:T(8,128)S(1)}, s32[8,10]{1,0:T(8,128)}, u32[]{:S(2)}) copy-start(s32[8,10]{1,0:T(8,128)} %param.17) | copy-start | bytes 964
  15.9 16.2 %copy-start.18 = (s32[8,10]{1,0:T(8,128)S(1)}, s32[8,10]{1,0:T(8,128)}, u32[]{:S(2)}) copy-start(s32[8,10]{1,0:T(8,128)} %param.18) | copy-start | bytes 964
  15.9 16.2 %copy-start.28 = (s32[8]{0:T(128)S(1)}, s32[8]{0:T(128)}, u32[]{:S(2)}) copy-start(s32[8]{0:T(128)} %param.19) | copy-start | bytes 100
  16.3 28.7 %copy-start.3 = (bf16[96,4096]{1,0:T(8,128)(2,1)}, bf16[96,4096]{1,0:T(8,128)(2,1)S(1)}, u32[]{:S(2)}) copy-start(bf16[96,4096]{1,0:T(8,128)(2,1)S(1)} %get-tuple-element.51) | copy-start | bytes 2359300
  16.3 30.1 %copy-start.2 = (bf16[96,4096]{1,0:T(8,128)(2,1)}, bf16[96,4096]{1,0:T(8,128)(2,1)S(1)}, u32[]{:S(2)}) copy-start(bf16[96,4096]{1,0:T(8,128)(2,1)S(1)} %get-tuple-element.50) | copy-start | bytes 2359300
  16.3 12.7 %collective-permute-start = (bf16[96,4096]{1,0:T(8,128)(2,1)S(1)}, bf16[96,4096]{1,0:T(8,128)(2,1)}, u32[]{:S(2)}, u32[]{:S(2)}) collective-permute-start(bf16[96,4096]{1,0:T(8,128)(2,1)S(1)} %get-tuple-element.51), channel_id=1, source_target_pairs={{0,1},{1,2},{2,3},{3,4},{4,5},{5,6},{6,7},{7,0},{8,9},{9,10},{10,1... | collective-permute-start | bytes 2359304 | tf_op jit(solution)/shard_map/ppermute | solution.py:62
  16.3 12.7 %collective-permute-start.7 = (bf16[96,4096]{1,0:T(8,128)(2,1)S(1)}, bf16[96,4096]{1,0:T(8,128)(2,1)}, u32[]{:S(2)}, u32[]{:S(2)}) collective-permute-start(bf16[96,4096]{1,0:T(8,128)(2,1)S(1)} %get-tuple-element.50), channel_id=1, source_target_pairs={{0,7},{1,0},{2,1},{3,2},{4,3},{5,4},{6,5},{7,6},{8,15},{9,8},{10,9... | collective-permute-start | bytes 2359304 | tf_op jit(solution)/shard_map/ppermute | solution.py:63
  29.1 12.9 %collective-permute-start.1 = (bf16[96,4096]{1,0:T(8,128)(2,1)}, bf16[96,4096]{1,0:T(8,128)(2,1)}, u32[]{:S(2)}, u32[]{:S(2)}) collective-permute-start(bf16[96,4096]{1,0:T(8,128)(2,1)} %collective-permute-done), channel_id=1, source_target_pairs={{0,1},{1,2},{2,3},{3,4},{4,5},{5,6},{6,7},{7,0},{8,9},{9,10},{10,1... | collective-permute-start | bytes 2359304 | tf_op jit(solution)/shard_map/ppermute | solution.py:62
  29.1 12.9 %collective-permute-start.8 = (bf16[96,4096]{1,0:T(8,128)(2,1)}, bf16[96,4096]{1,0:T(8,128)(2,1)}, u32[]{:S(2)}, u32[]{:S(2)}) collective-permute-start(bf16[96,4096]{1,0:T(8,128)(2,1)} %collective-permute-done.7), channel_id=1, source_target_pairs={{0,7},{1,0},{2,1},{3,2},{4,3},{5,4},{6,5},{7,6},{8,15},{9,8},{10,9... | collective-permute-start | bytes 2359304 | tf_op jit(solution)/shard_map/ppermute | solution.py:63
  32.1 16.9 %copy-start.13 = (s32[8,10]{1,0:T(8,128)}, s32[8,10]{1,0:T(8,128)S(1)}, u32[]{:S(2)}) copy-start(s32[8,10]{1,0:T(8,128)S(1)} %add_select_fusion) | copy-start | bytes 964
  32.7 16.2 %copy-start.22 = (pred[8,10]{1,0:T(8,128)(4,1)}, pred[8,10]{1,0:T(8,128)(4,1)S(1)}, u32[]{:S(2)}) copy-start(pred[8,10]{1,0:T(8,128)(4,1)S(1)} %get-tuple-element.58) | copy-start | bytes 244
  32.7 99.4 %copy-start.12 = (s32[8,10]{1,0:T(8,128)}, s32[8,10]{1,0:T(8,128)S(1)}, u32[]{:S(2)}) copy-start(s32[8,10]{1,0:T(8,128)S(1)} %get-tuple-element.57) | copy-start | bytes 964
  32.7 99.5 %copy-start.11 = (s32[8,10]{1,0:T(8,128)}, s32[8,10]{1,0:T(8,128)S(1)}, u32[]{:S(2)}) copy-start(s32[8,10]{1,0:T(8,128)S(1)} %get-tuple-element.48) | copy-start | bytes 964
  42.0 12.9 %collective-permute-start.2 = (bf16[96,4096]{1,0:T(8,128)(2,1)}, bf16[96,4096]{1,0:T(8,128)(2,1)}, u32[]{:S(2)}, u32[]{:S(2)}) collective-permute-start(bf16[96,4096]{1,0:T(8,128)(2,1)} %collective-permute-done.1), channel_id=1, source_target_pairs={{0,1},{1,2},{2,3},{3,4},{4,5},{5,6},{6,7},{7,0},{8,9},{9,10},{10,1... | collective-permute-start | bytes 2359304 | tf_op jit(solution)/shard_map/ppermute | solution.py:62
  42.0 12.9 %collective-permute-start.9 = (bf16[96,4096]{1,0:T(8,128)(2,1)}, bf16[96,4096]{1,0:T(8,128)(2,1)}, u32[]{:S(2)}, u32[]{:S(2)}) collective-permute-start(bf16[96,4096]{1,0:T(8,128)(2,1)} %collective-permute-done.8), channel_id=1, source_target_pairs={{0,7},{1,0},{2,1},{3,2},{4,3},{5,4},{6,5},{7,6},{8,15},{9,8},{10,9... | collective-permute-start | bytes 2359304 | tf_op jit(solution)/shard_map/ppermute | solution.py:63
  54.9 12.8 %collective-permute-start.3 = (bf16[96,4096]{1,0:T(8,128)(2,1)}, bf16[96,4096]{1,0:T(8,128)(2,1)S(1)}, u32[]{:S(2)}, u32[]{:S(2)}) collective-permute-start(bf16[96,4096]{1,0:T(8,128)(2,1)} %collective-permute-done.2), channel_id=1, source_target_pairs={{0,1},{1,2},{2,3},{3,4},{4,5},{5,6},{6,7},{7,0},{8,9},{9,10},{10,1... | collective-permute-start | bytes 2359304 | tf_op jit(solution)/shard_map/ppermute | solution.py:62
  55.0 13.1 %collective-permute-start.10 = (bf16[96,4096]{1,0:T(8,128)(2,1)}, bf16[96,4096]{1,0:T(8,128)(2,1)S(1)}, u32[]{:S(2)}, u32[]{:S(2)}) collective-permute-start(bf16[96,4096]{1,0:T(8,128)(2,1)} %collective-permute-done.9), channel_id=1, source_target_pairs={{0,7},{1,0},{2,1},{3,2},{4,3},{5,4},{6,5},{7,6},{8,15},{9,8},{10,9... | collective-permute-start | bytes 2359304 | tf_op jit(solution)/shard_map/ppermute | solution.py:63
  67.8 12.6 %collective-permute-start.4 = (bf16[96,4096]{1,0:T(8,128)(2,1)S(1)}, bf16[96,4096]{1,0:T(8,128)(2,1)S(1)}, u32[]{:S(2)}, u32[]{:S(2)}) collective-permute-start(bf16[96,4096]{1,0:T(8,128)(2,1)S(1)} %collective-permute-done.3), channel_id=1, source_target_pairs={{0,1},{1,2},{2,3},{3,4},{4,5},{5,6},{6,7},{7,0},{8,9},{9,10},{10,1... | collective-permute-start | bytes 2359304 | tf_op jit(solution)/shard_map/ppermute | solution.py:62
  68.0 12.7 %collective-permute-start.11 = (bf16[96,4096]{1,0:T(8,128)(2,1)S(1)}, bf16[96,4096]{1,0:T(8,128)(2,1)S(1)}, u32[]{:S(2)}, u32[]{:S(2)}) collective-permute-start(bf16[96,4096]{1,0:T(8,128)(2,1)S(1)} %collective-permute-done.10), channel_id=1, source_target_pairs={{0,7},{1,0},{2,1},{3,2},{4,3},{5,4},{6,5},{7,6},{8,15},{9,8},{10,9... | collective-permute-start | bytes 2359304 | tf_op jit(solution)/shard_map/ppermute | solution.py:63
  80.4 12.6 %collective-permute-start.5 = (bf16[96,4096]{1,0:T(8,128)(2,1)S(1)}, bf16[96,4096]{1,0:T(8,128)(2,1)S(1)}, u32[]{:S(2)}, u32[]{:S(2)}) collective-permute-start(bf16[96,4096]{1,0:T(8,128)(2,1)S(1)} %collective-permute-done.4), channel_id=1, source_target_pairs={{0,1},{1,2},{2,3},{3,4},{4,5},{5,6},{6,7},{7,0},{8,9},{9,10},{10,1... | collective-permute-start | bytes 2359304 | tf_op jit(solution)/shard_map/ppermute | solution.py:62
  80.8 12.6 %collective-permute-start.12 = (bf16[96,4096]{1,0:T(8,128)(2,1)S(1)}, bf16[96,4096]{1,0:T(8,128)(2,1)S(1)}, u32[]{:S(2)}, u32[]{:S(2)}) collective-permute-start(bf16[96,4096]{1,0:T(8,128)(2,1)S(1)} %collective-permute-done.11), channel_id=1, source_target_pairs={{0,7},{1,0},{2,1},{3,2},{4,3},{5,4},{6,5},{7,6},{8,15},{9,8},{10,9... | collective-permute-start | bytes 2359304 | tf_op jit(solution)/shard_map/ppermute | solution.py:63
  93.0 12.6 %collective-permute-start.6 = (bf16[96,4096]{1,0:T(8,128)(2,1)S(1)}, bf16[96,4096]{1,0:T(8,128)(2,1)S(1)}, u32[]{:S(2)}, u32[]{:S(2)}) collective-permute-start(bf16[96,4096]{1,0:T(8,128)(2,1)S(1)} %collective-permute-done.5), channel_id=1, source_target_pairs={{0,1},{1,2},{2,3},{3,4},{4,5},{5,6},{6,7},{7,0},{8,9},{9,10},{10,1... | collective-permute-start | bytes 2359304 | tf_op jit(solution)/shard_map/ppermute | solution.py:62
  93.4 12.6 %collective-permute-start.13 = (bf16[96,4096]{1,0:T(8,128)(2,1)S(1)}, bf16[96,4096]{1,0:T(8,128)(2,1)S(1)}, u32[]{:S(2)}, u32[]{:S(2)}) collective-permute-start(bf16[96,4096]{1,0:T(8,128)(2,1)S(1)} %collective-permute-done.12), channel_id=1, source_target_pairs={{0,7},{1,0},{2,1},{3,2},{4,3},{5,4},{6,5},{7,6},{8,15},{9,8},{10,9... | collective-permute-start | bytes 2359304 | tf_op jit(solution)/shard_map/ppermute | solution.py:63
  97.8 8.7 %copy-start.7 = (bf16[8,96,8,512]{3,1,2,0:T(8,128)(2,1)}, bf16[8,96,8,512]{3,1,2,0:T(8,128)(2,1)S(1)}, u32[]{:S(2)}) copy-start(bf16[8,96,8,512]{3,1,2,0:T(8,128)(2,1)S(1)} %copy_dynamic-update-slice_fusion.1) | copy-start | bytes 18874372
  121.5 6.0 %copy-start.19 = (bf16[10]{0:T(256)(128)(2,1)S(1)}, bf16[10]{0:T(256)(128)(2,1)}, u32[]{:S(2)}) copy-start(bf16[10]{0:T(256)(128)(2,1)} %get-tuple-element.45) | copy-start | bytes 64
  149.2 43.1 %all-to-all-start = ((bf16[8,384,512]{2,1,0:T(8,128)(2,1)}), bf16[8,384,512]{2,1,0:T(8,128)(2,1)}, u32[]{:S(2)}, u32[]{:S(2)}) async-start(bf16[8,384,512]{2,1,0:T(8,128)(2,1)} %bitcast.135), calls=%async_computation | async-start | bytes 6291456 | tf_op jit(solution)/shard_map/all_to_all | solution.py:126
  192.3 5.2 %copy-start.14 = (s32[8,10]{1,0:T(8,128)S(1)}, s32[8,10]{1,0:T(8,128)}, u32[]{:S(2)}) copy-start(s32[8,10]{1,0:T(8,128)} %copy-done.13) | copy-start | bytes 964
  192.3 43.0 %all-to-all-start.1 = ((bf16[8,384,512]{2,1,0:T(8,128)(2,1)}), bf16[8,384,512]{2,1,0:T(8,128)(2,1)}, u32[]{:S(2)}, u32[]{:S(2)}) async-start(bf16[8,384,512]{2,1,0:T(8,128)(2,1)} %bitcast.134), calls=%async_computation.1 | async-start | bytes 6291456 | tf_op jit(solution)/shard_map/all_to_all | solution.py:148
  196.9 149.0 %reduce-scatter.7.cloned.1.call-start = ((), (), s32[]{:S(2)}) async-start(), calls=%async_computation.6 | async-start | bytes 8912896
  (17 other events, 54.5 us)
Sparse Core Ops, SparseCore 0:
  10.2 58.9 all-gather.1
  132.3 81.9 reduce-scatter.4
  259.9 85.9 reduce-scatter.6
where the time goes:
time: 356 us; the launch traced here: 355 us
  waiting for transfers between devices  115 us (32%)
  blocking collectives  76.5 us (21%)
  local copies, waits for them, and re-layouts  64.5 us (18%)
  matrix products  34.6 us (10%)
  starting transfers between devices  30.9 us (9%)
  other arithmetic  18.7 us (5%)
  between operations  14.3 us (4%)
    psum x1, blocking collectives, on_device(): lax.psum((jnp.sum(grad_pre, axis=0), jnp.sum(grad_mixed, axis=0)), 'dp')  76.5 us
    ppermute x7, waiting for transfers between devices, ring_gather(): cur_a = lax.ppermute(cur_a, axis, right)  49 us
    unnamed x96, local copies, waits for them, and re-layouts  38.9 us
    all_to_all x1, waiting for transfers between devices, on_device(): lax.all_to_all(pack_parts(back_parts, chosen_in, filled_in), 'tensor', sp...  33.1 us
    all_to_all x1, waiting for transfers between devices, on_device(): lax.all_to_all(pack_parts(parts, chosen_out, filled_out), 'tensor', split...  24.5 us
    ppermute x7, starting transfers between devices, ring_gather(): cur_b = lax.ppermute(cur_b, axis, left)  21.6 us
    mul x2, other arithmetic, pack_parts(): jnp.take(parts, chosen.reshape(-1), axis=0)  7.95 us
    gather x2, local copies, waits for them, and re-layouts, take_blocks(): top = blocks_a[step_a, :, local, :]  7.85 us
  transfers between devices with their start and end apart: 19, of which 14 were waited for; matrix products, arithmetic and copies ran while one was open for 31% of the time, Pallas kernels for 0%

commit v1 on v0

--- a/solution.py
+++ b/solution.py
@@ -163,15 +163,19 @@
     sigma = jax.nn.sigmoid(preact)
     grad_pre = grad_start * sigma * (1.0 + preact * (1.0 - sigma))
     grad_pre_low = grad_pre.astype(jnp.bfloat16)
-    taken = dense
-    grad_bottom = lax.psum_scatter(
-        lax.dot_general(
-            taken, grad_pre_low, (((0,), (0,)), ((), ())), preferred_element_type=jnp.float32
-        ).astype(jnp.bfloat16),
-        "dp",
-        scatter_dimension=0,
-        tiled=True,
-    ).astype(jnp.float32)
+    dp_size = lax.axis_size("dp")
+    split = local_width // 2
+    lead = lax.dot_general(
+        grad_pre_low[:, :split], dense, (((0,), (0,)), ((), ())), preferred_element_type=jnp.float32
+    ).astype(jnp.bfloat16)
+    lead = lax.psum_scatter(lead, "dp", scatter_dimension=1, tiled=True).astype(jnp.float32).T
+    rest = lax.dot_general(
+        dense, grad_pre_low[:, split:], (((0,), (0,)), ((), ())), preferred_element_type=jnp.float32
+    ).astype(jnp.bfloat16)
+    rest = rest.reshape(dp_size, rest.shape[0] // dp_size, rest.shape[1])
+    rest = lax.all_to_all(rest, "dp", split_axis=0, concat_axis=0, tiled=True)
+    rest = jnp.sum(rest.astype(jnp.float32), axis=0)
+    grad_bottom = jnp.concatenate([lead, rest], axis=1)
     bias_sums = lax.psum((jnp.sum(grad_pre, axis=0), jnp.sum(grad_mixed, axis=0)), "dp")
     return (cross_out, grad_bottom, bias_sums[0], grad_blocks, bias_sums[1])
 

time: 356 us -> 413 us (1.16)
  blocking collectives: 76.5 us -> 131 us
  starting transfers between devices: 30.9 us -> 39.4 us
  waiting for transfers between devices: 115 us -> 108 us
    psum x1, blocking collectives: 76.5 us -> 131 us  [on_device(): lax.psum((jnp.sum(grad_pre, axis=0), jnp.sum(grad_mixed, axis=0)), 'dp')]
    all_to_all x0 -> x1, starting transfers between devices: none -> 8.45 us  [on_device(): rest = lax.all_to_all(rest, 'dp', split_axis=0, concat_axis=0, tiled=True)]
    unnamed x4, waiting for transfers between devices: 7.74 us -> 0.73 us
    unnamed x96 -> x100, local copies, waits for them, and re-layouts: 38.9 us -> 34.2 us
  transfers between devices with their start and end apart: 19 -> 20, of which waited for: 14 -> 13; matrix products, arithmetic and copies ran while one was open for 31% -> 26% of each run, Pallas kernels for 0% -> 0%
where the time goes in v1:
time: 413 us; the launch traced here: 411 us
  blocking collectives  131 us (32%)
  waiting for transfers between devices  108 us (26%)
  local copies, waits for them, and re-layouts  62.9 us (15%)
  starting transfers between devices  39.4 us (10%)
  matrix products  33.8 us (8%)
  other arithmetic  21.8 us (5%)
  between operations  14.3 us (3%)
    psum x1, blocking collectives, on_device(): lax.psum((jnp.sum(grad_pre, axis=0), jnp.sum(grad_mixed, axis=0)), 'dp')  131 us
    ppermute x7, waiting for transfers between devices, ring_gather(): cur_a = lax.ppermute(cur_a, axis, right)  49 us
    unnamed x100, local copies, waits for them, and re-layouts  34.2 us
    all_to_all x1, waiting for transfers between devices, on_device(): lax.all_to_all(pack_parts(back_parts, chosen_in, filled_in), 'tensor', sp...  33.1 us
    all_to_all x1, waiting for transfers between devices, on_device(): lax.all_to_all(pack_parts(parts, chosen_out, filled_out), 'tensor', split...  24.4 us
    ppermute x7, starting transfers between devices, ring_gather(): cur_b = lax.ppermute(cur_b, axis, left)  21.6 us
    all_to_all x1, starting transfers between devices, on_device(): rest = lax.all_to_all(rest, 'dp', split_axis=0, concat_axis=0, tiled=True)  8.45 us
  transfers between devices with their start and end apart: 20, of which 13 were waited for; matrix products, arithmetic and copies ran while one was open for 26% of the time, Pallas kernels for 0%

profile of v1, /device:TPU:0, one launch (start us, length us, event | category | flops | bytes accessed | tf_op | source)
XLA Modules:
  0.0 411.3 jit_solution(8052514285744440589)
XLA Ops:
  8.3 7.5 %fusion.8 = (f32[2048]{0:T(1024)}, bf16[192,2048]{1,0:T(8,128)(2,1)S(1)}, f32[192,2048]{1,0:T(8,128)}) fusion(bf16[192,2048]{1,0:T(8,128)(2,1)} %param.16, f32[2048]{0:T(1024)} %param.13, bf16[192,2048]{1,0:T(8,128)(2,1)S(1)} %copy-done, bf16[2048,2048]{1,0:T(8,128)(2,1)} %param.12), kind=kOutput, calls=%fused_computation.33 | convolution fusion | flops 1614542848 | bytes 12337152 | tf_op jit(solution)/shard_map/dot_general | solution.py:97
  19.3 9.8 %collective-permute-done = bf16[96,4096]{1,0:T(8,128)(2,1)} collective-permute-done((bf16[96,4096]{1,0:T(8,128)(2,1)S(1)}, bf16[96,4096]{1,0:T(8,128)(2,1)}, u32[]{:S(2)}, u32[]{:S(2)}) %collective-permute-start) | collective-permute-done | bytes 786464 | tf_op jit(solution)/shard_map/ppermute | solution.py:62
  32.7 9.3 %collective-permute-done.1 = bf16[96,4096]{1,0:T(8,128)(2,1)} collective-permute-done((bf16[96,4096]{1,0:T(8,128)(2,1)}, bf16[96,4096]{1,0:T(8,128)(2,1)}, u32[]{:S(2)}, u32[]{:S(2)}) %collective-permute-start.1) | collective-permute-done | bytes 786464 | tf_op jit(solution)/shard_map/ppermute | solution.py:62
  51.8 3.1 collective-permute-done.2
  54.9 3.2 collective-permute-start.10
  61.7 6.0 %collective-permute-done.3 = bf16[96,4096]{1,0:T(8,128)(2,1)S(1)} collective-permute-done((bf16[96,4096]{1,0:T(8,128)(2,1)}, bf16[96,4096]{1,0:T(8,128)(2,1)S(1)}, u32[]{:S(2)}, u32[]{:S(2)}) %collective-permute-start.3) | collective-permute-done | bytes 786464 | tf_op jit(solution)/shard_map/ppermute | solution.py:62
  68.0 3.2 collective-permute-start.11
  75.4 5.0 %collective-permute-done.4 = bf16[96,4096]{1,0:T(8,128)(2,1)S(1)} collective-permute-done((bf16[96,4096]{1,0:T(8,128)(2,1)S(1)}, bf16[96,4096]{1,0:T(8,128)(2,1)S(1)}, u32[]{:S(2)}, u32[]{:S(2)}) %collective-permute-start.4) | collective-permute-done | bytes 786464 | tf_op jit(solution)/shard_map/ppermute | solution.py:62
  80.8 3.1 collective-permute-start.12
  85.2 7.9 %collective-permute-done.5 = bf16[96,4096]{1,0:T(8,128)(2,1)S(1)} collective-permute-done((bf16[96,4096]{1,0:T(8,128)(2,1)S(1)}, bf16[96,4096]{1,0:T(8,128)(2,1)S(1)}, u32[]{:S(2)}, u32[]{:S(2)}) %collective-permute-start.5) | collective-permute-done | bytes 786464 | tf_op jit(solution)/shard_map/ppermute | solution.py:62
  93.4 3.1 collective-permute-start.13
  97.8 7.9 %collective-permute-done.6 = bf16[96,4096]{1,0:T(8,128)(2,1)S(1)} collective-permute-done((bf16[96,4096]{1,0:T(8,128)(2,1)S(1)}, bf16[96,4096]{1,0:T(8,128)(2,1)S(1)}, u32[]{:S(2)}, u32[]{:S(2)}) %collective-permute-start.6) | collective-permute-done | bytes 786464 | tf_op jit(solution)/shard_map/ppermute | solution.py:62
  109.1 3.4 gather_fusion
  112.6 4.4 %gather_fusion.2 = bf16[10,96,512]{2,1,0:T(8,128)(2,1)} fusion(bf16[8,96,8,512]{3,1,2,0:T(8,128)(2,1)} %copy-done.10, s32[10]{0:T(128)S(1)} %get-tuple-element.52), kind=kCustom, calls=%fused_computation.4 | custom fusion | bytes 1966160 | tf_op jit(solution)/shard_map/gather | solution.py:75
  118.1 3.4 gather_fusion.1
  121.5 4.4 %gather_fusion.3 = bf16[10,96,512]{2,1,0:T(8,128)(2,1)} fusion(bf16[8,96,8,512]{3,1,2,0:T(8,128)(2,1)} %copy_dynamic-update-slice_fusion, s32[10]{0:T(128)S(1)} %get-tuple-element.53), kind=kCustom, calls=%fused_computation.5 | custom fusion | bytes 1966160 | tf_op jit(solution)/shard_map/gather | solution.py:76
  128.0 4.1 convolution_convert_fusion.1
  138.5 4.3 %convert_multiply_fusion.2 = bf16[10,192,512]{2,1,0:T(8,128)(2,1)S(1)} fusion(bf16[10,192,512]{2,1,0:T(8,128)(2,1)} %copy-done.1, bf16[10,512,512]{2,1,0:T(8,128)(2,1)} %all-gather.2.cloned.1.call-done, bf16[10]{0:T(256)(128)(2,1)} %get-tuple-element.45), kind=kOutput, calls=%fused_computation.23 | convolution fusion | flops 1008599040 | bytes 9175060 | tf_op jit(solution)/shard_map/kri,kij->krj/dot_general | solution.py:116
  145.3 4.0 select_multiply_fusion.1
  149.3 4.6 %all-to-all-start = ((bf16[8,384,512]{2,1,0:T(8,128)(2,1)}), bf16[8,384,512]{2,1,0:T(8,128)(2,1)}, u32[]{:S(2)}, u32[]{:S(2)}) async-start(bf16[8,384,512]{2,1,0:T(8,128)(2,1)} %bitcast.144), calls=%async_computation | async-start | bytes 6291456 | tf_op jit(solution)/shard_map/all_to_all | solution.py:126
  156.0 5.4 %convolution_convert_fusion.2 = bf16[10,192,512]{2,1,0:T(8,128)(2,1)S(1)} fusion(bf16[10,512,512]{2,1,0:T(8,128)(2,1)} %all-gather.2.cloned.1.call-done, bf16[10,96,512]{2,1,0:T(8,128)(2,1)} %gather_fusion.3, bf16[10,96,512]{2,1,0:T(8,128)(2,1)} %gather_fusion.2, bf16[10]{0:T(256)(128)(2,1)} %get-tuple-element.45), kind=kOutput, calls=%fused_computation.24 | convolution fusion | flops 1013514240 | bytes 9175060 | tf_op jit(solution)/shard_map/krj,kij->kri/dot_general | solution.py:140
  163.9 4.0 select_multiply_fusion
  168.0 24.4 %all-to-all-done = bf16[8,384,512]{2,1,0:T(8,128)(2,1)} async-done(((bf16[8,384,512]{2,1,0:T(8,128)(2,1)}), bf16[8,384,512]{2,1,0:T(8,128)(2,1)}, u32[]{:S(2)}, u32[]{:S(2)}) %all-to-all-start) | async-done | bytes 3145760 | tf_op jit(solution)/shard_map/all_to_all | solution.py:126
  192.4 4.6 %all-to-all-start.1 = ((bf16[8,384,512]{2,1,0:T(8,128)(2,1)}), bf16[8,384,512]{2,1,0:T(8,128)(2,1)}, u32[]{:S(2)}, u32[]{:S(2)}) async-start(bf16[8,384,512]{2,1,0:T(8,128)(2,1)} %bitcast.143), calls=%async_computation.1 | async-start | bytes 6291456 | tf_op jit(solution)/shard_map/all_to_all | solution.py:148
  197.9 3.8 fusion.2
  202.4 33.1 %all-to-all-done.1 = bf16[8,384,512]{2,1,0:T(8,128)(2,1)} async-done(((bf16[8,384,512]{2,1,0:T(8,128)(2,1)}), bf16[8,384,512]{2,1,0:T(8,128)(2,1)}, u32[]{:S(2)}, u32[]{:S(2)}) %all-to-all-start.1) | async-done | bytes 3145760 | tf_op jit(solution)/shard_map/all_to_all | solution.py:148
  235.4 4.0 fusion
  242.8 3.4 convolution_convert_fusion
  246.2 6.5 %copy.128 = bf16[1024,2048]{0,1:T(8,128)(2,1)} copy(bf16[1024,2048]{1,0:T(8,128)(2,1)} %convolution_convert_fusion) | data formatting | bytes 8388608
  255.1 3.1 copy.170
  258.1 8.5 %all-to-all-start.2 = ((bf16[16,128,1024]{1,2,0:T(8,128)(2,1)}), bf16[16,128,1024]{1,2,0:T(8,128)(2,1)}, u32[]{:S(2)}, u32[]{:S(2)}) async-start(bf16[16,128,1024]{1,2,0:T(8,128)(2,1)} %bitcast.142), calls=%async_computation.2 | async-start | bytes 8388608 | tf_op jit(solution)/shard_map/all_to_all | solution.py:176
  266.6 130.8 %all-reduce = (f32[2048]{0:T(1024)}, f32[2048]{0:T(1024)}) all-reduce(f32[2048]{0:T(1024)S(1)} %get-tuple-element.41, f32[2048]{0:T(1024)S(1)} %copy-done.22), channel_id=1, replica_groups=mesh['dp'=16,'tensor'=8] {'dp'}, use_global_device_ids=true, to_apply=%region_11.13 | all-reduce | flops 4096 | bytes 32768 | tf_op jit(solution)/shard_map/psum | solution.py:179
  (183 shorter events, 63.8 us)
Async XLA Ops:
  7.2 131.3 %all-gather.2.cloned.1.call-start = ((), (), s32[]{:S(2)}) async-start(), calls=%async_computation.5 | async-start | bytes 5570560 | tf_op jit(solution)/shard_map/all_gather | solution.py:119
  7.9 7.9 %copy-start.4 = (bf16[192,2048]{1,0:T(8,128)(2,1)S(1)}, bf16[192,2048]{1,0:T(8,128)(2,1)}, u32[]{:S(2)}) copy-start(bf16[192,2048]{1,0:T(8,128)(2,1)} %param.16) | copy-start | bytes 2359300
  7.9 389.5 %reduce-scatter.5.cloned.1.call-start = ((), (), s32[]{:S(2)}) async-start(), calls=%async_computation.6 | async-start | bytes 5570560 | tf_op jit(solution)/shard_map/reduce_scatter | solution.py:159
  15.8 16.2 %copy-start.19 = (s32[8,10]{1,0:T(8,128)S(1)}, s32[8,10]{1,0:T(8,128)}, u32[]{:S(2)}) copy-start(s32[8,10]{1,0:T(8,128)} %param.17) | copy-start | bytes 964
  15.8 16.2 %copy-start.20 = (s32[8,10]{1,0:T(8,128)S(1)}, s32[8,10]{1,0:T(8,128)}, u32[]{:S(2)}) copy-start(s32[8,10]{1,0:T(8,128)} %param.18) | copy-start | bytes 964
  15.9 16.2 %copy-start.30 = (s32[8]{0:T(128)S(1)}, s32[8]{0:T(128)}, u32[]{:S(2)}) copy-start(s32[8]{0:T(128)} %param.19) | copy-start | bytes 100
  16.3 28.7 %copy-start.3 = (bf16[96,4096]{1,0:T(8,128)(2,1)}, bf16[96,4096]{1,0:T(8,128)(2,1)S(1)}, u32[]{:S(2)}) copy-start(bf16[96,4096]{1,0:T(8,128)(2,1)S(1)} %get-tuple-element.51) | copy-start | bytes 2359300
  16.3 30.1 %copy-start.2 = (bf16[96,4096]{1,0:T(8,128)(2,1)}, bf16[96,4096]{1,0:T(8,128)(2,1)S(1)}, u32[]{:S(2)}) copy-start(bf16[96,4096]{1,0:T(8,128)(2,1)S(1)} %get-tuple-element.50) | copy-start | bytes 2359300
  16.3 12.7 %collective-permute-start = (bf16[96,4096]{1,0:T(8,128)(2,1)S(1)}, bf16[96,4096]{1,0:T(8,128)(2,1)}, u32[]{:S(2)}, u32[]{:S(2)}) collective-permute-start(bf16[96,4096]{1,0:T(8,128)(2,1)S(1)} %get-tuple-element.51), channel_id=1, source_target_pairs={{0,1},{1,2},{2,3},{3,4},{4,5},{5,6},{6,7},{7,0},{8,9},{9,10},{10,1... | collective-permute-start | bytes 2359304 | tf_op jit(solution)/shard_map/ppermute | solution.py:62
  16.3 12.7 %collective-permute-start.7 = (bf16[96,4096]{1,0:T(8,128)(2,1)S(1)}, bf16[96,4096]{1,0:T(8,128)(2,1)}, u32[]{:S(2)}, u32[]{:S(2)}) collective-permute-start(bf16[96,4096]{1,0:T(8,128)(2,1)S(1)} %get-tuple-element.50), channel_id=1, source_target_pairs={{0,7},{1,0},{2,1},{3,2},{4,3},{5,4},{6,5},{7,6},{8,15},{9,8},{10,9... | collective-permute-start | bytes 2359304 | tf_op jit(solution)/shard_map/ppermute | solution.py:63
  29.1 12.9 %collective-permute-start.1 = (bf16[96,4096]{1,0:T(8,128)(2,1)}, bf16[96,4096]{1,0:T(8,128)(2,1)}, u32[]{:S(2)}, u32[]{:S(2)}) collective-permute-start(bf16[96,4096]{1,0:T(8,128)(2,1)} %collective-permute-done), channel_id=1, source_target_pairs={{0,1},{1,2},{2,3},{3,4},{4,5},{5,6},{6,7},{7,0},{8,9},{9,10},{10,1... | collective-permute-start | bytes 2359304 | tf_op jit(solution)/shard_map/ppermute | solution.py:62
  29.1 12.9 %collective-permute-start.8 = (bf16[96,4096]{1,0:T(8,128)(2,1)}, bf16[96,4096]{1,0:T(8,128)(2,1)}, u32[]{:S(2)}, u32[]{:S(2)}) collective-permute-start(bf16[96,4096]{1,0:T(8,128)(2,1)} %collective-permute-done.7), channel_id=1, source_target_pairs={{0,7},{1,0},{2,1},{3,2},{4,3},{5,4},{6,5},{7,6},{8,15},{9,8},{10,9... | collective-permute-start | bytes 2359304 | tf_op jit(solution)/shard_map/ppermute | solution.py:63
  32.0 16.9 %copy-start.15 = (s32[8,10]{1,0:T(8,128)}, s32[8,10]{1,0:T(8,128)S(1)}, u32[]{:S(2)}) copy-start(s32[8,10]{1,0:T(8,128)S(1)} %add_select_fusion) | copy-start | bytes 964
  32.7 16.2 %copy-start.24 = (pred[8,10]{1,0:T(8,128)(4,1)}, pred[8,10]{1,0:T(8,128)(4,1)S(1)}, u32[]{:S(2)}) copy-start(pred[8,10]{1,0:T(8,128)(4,1)S(1)} %get-tuple-element.58) | copy-start | bytes 244
  32.7 99.4 %copy-start.14 = (s32[8,10]{1,0:T(8,128)}, s32[8,10]{1,0:T(8,128)S(1)}, u32[]{:S(2)}) copy-start(s32[8,10]{1,0:T(8,128)S(1)} %get-tuple-element.57) | copy-start | bytes 964
  32.7 99.5 %copy-start.13 = (s32[8,10]{1,0:T(8,128)}, s32[8,10]{1,0:T(8,128)S(1)}, u32[]{:S(2)}) copy-start(s32[8,10]{1,0:T(8,128)S(1)} %get-tuple-element.48) | copy-start | bytes 964
  42.0 12.9 %collective-permute-start.2 = (bf16[96,4096]{1,0:T(8,128)(2,1)}, bf16[96,4096]{1,0:T(8,128)(2,1)}, u32[]{:S(2)}, u32[]{:S(2)}) collective-permute-start(bf16[96,4096]{1,0:T(8,128)(2,1)} %collective-permute-done.1), channel_id=1, source_target_pairs={{0,1},{1,2},{2,3},{3,4},{4,5},{5,6},{6,7},{7,0},{8,9},{9,10},{10,1... | collective-permute-start | bytes 2359304 | tf_op jit(solution)/shard_map/ppermute | solution.py:62
  42.0 12.9 %collective-permute-start.9 = (bf16[96,4096]{1,0:T(8,128)(2,1)}, bf16[96,4096]{1,0:T(8,128)(2,1)}, u32[]{:S(2)}, u32[]{:S(2)}) collective-permute-start(bf16[96,4096]{1,0:T(8,128)(2,1)} %collective-permute-done.8), channel_id=1, source_target_pairs={{0,7},{1,0},{2,1},{3,2},{4,3},{5,4},{6,5},{7,6},{8,15},{9,8},{10,9... | collective-permute-start | bytes 2359304 | tf_op jit(solution)/shard_map/ppermute | solution.py:63
  54.9 12.8 %collective-permute-start.3 = (bf16[96,4096]{1,0:T(8,128)(2,1)}, bf16[96,4096]{1,0:T(8,128)(2,1)S(1)}, u32[]{:S(2)}, u32[]{:S(2)}) collective-permute-start(bf16[96,4096]{1,0:T(8,128)(2,1)} %collective-permute-done.2), channel_id=1, source_target_pairs={{0,1},{1,2},{2,3},{3,4},{4,5},{5,6},{6,7},{7,0},{8,9},{9,10},{10,1... | collective-permute-start | bytes 2359304 | tf_op jit(solution)/shard_map/ppermute | solution.py:62
  54.9 13.1 %collective-permute-start.10 = (bf16[96,4096]{1,0:T(8,128)(2,1)}, bf16[96,4096]{1,0:T(8,128)(2,1)S(1)}, u32[]{:S(2)}, u32[]{:S(2)}) collective-permute-start(bf16[96,4096]{1,0:T(8,128)(2,1)} %collective-permute-done.9), channel_id=1, source_target_pairs={{0,7},{1,0},{2,1},{3,2},{4,3},{5,4},{6,5},{7,6},{8,15},{9,8},{10,9... | collective-permute-start | bytes 2359304 | tf_op jit(solution)/shard_map/ppermute | solution.py:63
  67.8 12.6 %collective-permute-start.4 = (bf16[96,4096]{1,0:T(8,128)(2,1)S(1)}, bf16[96,4096]{1,0:T(8,128)(2,1)S(1)}, u32[]{:S(2)}, u32[]{:S(2)}) collective-permute-start(bf16[96,4096]{1,0:T(8,128)(2,1)S(1)} %collective-permute-done.3), channel_id=1, source_target_pairs={{0,1},{1,2},{2,3},{3,4},{4,5},{5,6},{6,7},{7,0},{8,9},{9,10},{10,1... | collective-permute-start | bytes 2359304 | tf_op jit(solution)/shard_map/ppermute | solution.py:62
  68.0 12.7 %collective-permute-start.11 = (bf16[96,4096]{1,0:T(8,128)(2,1)S(1)}, bf16[96,4096]{1,0:T(8,128)(2,1)S(1)}, u32[]{:S(2)}, u32[]{:S(2)}) collective-permute-start(bf16[96,4096]{1,0:T(8,128)(2,1)S(1)} %collective-permute-done.10), channel_id=1, source_target_pairs={{0,7},{1,0},{2,1},{3,2},{4,3},{5,4},{6,5},{7,6},{8,15},{9,8},{10,9... | collective-permute-start | bytes 2359304 | tf_op jit(solution)/shard_map/ppermute | solution.py:63
  80.4 12.6 %collective-permute-start.5 = (bf16[96,4096]{1,0:T(8,128)(2,1)S(1)}, bf16[96,4096]{1,0:T(8,128)(2,1)S(1)}, u32[]{:S(2)}, u32[]{:S(2)}) collective-permute-start(bf16[96,4096]{1,0:T(8,128)(2,1)S(1)} %collective-permute-done.4), channel_id=1, source_target_pairs={{0,1},{1,2},{2,3},{3,4},{4,5},{5,6},{6,7},{7,0},{8,9},{9,10},{10,1... | collective-permute-start | bytes 2359304 | tf_op jit(solution)/shard_map/ppermute | solution.py:62
  80.8 12.6 %collective-permute-start.12 = (bf16[96,4096]{1,0:T(8,128)(2,1)S(1)}, bf16[96,4096]{1,0:T(8,128)(2,1)S(1)}, u32[]{:S(2)}, u32[]{:S(2)}) collective-permute-start(bf16[96,4096]{1,0:T(8,128)(2,1)S(1)} %collective-permute-done.11), channel_id=1, source_target_pairs={{0,7},{1,0},{2,1},{3,2},{4,3},{5,4},{6,5},{7,6},{8,15},{9,8},{10,9... | collective-permute-start | bytes 2359304 | tf_op jit(solution)/shard_map/ppermute | solution.py:63
  93.0 12.6 %collective-permute-start.6 = (bf16[96,4096]{1,0:T(8,128)(2,1)S(1)}, bf16[96,4096]{1,0:T(8,128)(2,1)S(1)}, u32[]{:S(2)}, u32[]{:S(2)}) collective-permute-start(bf16[96,4096]{1,0:T(8,128)(2,1)S(1)} %collective-permute-done.5), channel_id=1, source_target_pairs={{0,1},{1,2},{2,3},{3,4},{4,5},{5,6},{6,7},{7,0},{8,9},{9,10},{10,1... | collective-permute-start | bytes 2359304 | tf_op jit(solution)/shard_map/ppermute | solution.py:62
  93.4 12.6 %collective-permute-start.13 = (bf16[96,4096]{1,0:T(8,128)(2,1)S(1)}, bf16[96,4096]{1,0:T(8,128)(2,1)S(1)}, u32[]{:S(2)}, u32[]{:S(2)}) collective-permute-start(bf16[96,4096]{1,0:T(8,128)(2,1)S(1)} %collective-permute-done.12), channel_id=1, source_target_pairs={{0,7},{1,0},{2,1},{3,2},{4,3},{5,4},{6,5},{7,6},{8,15},{9,8},{10,9... | collective-permute-start | bytes 2359304 | tf_op jit(solution)/shard_map/ppermute | solution.py:63
  97.8 8.7 %copy-start.9 = (bf16[8,96,8,512]{3,1,2,0:T(8,128)(2,1)}, bf16[8,96,8,512]{3,1,2,0:T(8,128)(2,1)S(1)}, u32[]{:S(2)}) copy-start(bf16[8,96,8,512]{3,1,2,0:T(8,128)(2,1)S(1)} %copy_dynamic-update-slice_fusion.1) | copy-start | bytes 18874372
  149.3 43.1 %all-to-all-start = ((bf16[8,384,512]{2,1,0:T(8,128)(2,1)}), bf16[8,384,512]{2,1,0:T(8,128)(2,1)}, u32[]{:S(2)}, u32[]{:S(2)}) async-start(bf16[8,384,512]{2,1,0:T(8,128)(2,1)} %bitcast.144), calls=%async_computation | async-start | bytes 6291456 | tf_op jit(solution)/shard_map/all_to_all | solution.py:126
  192.4 43.1 %all-to-all-start.1 = ((bf16[8,384,512]{2,1,0:T(8,128)(2,1)}), bf16[8,384,512]{2,1,0:T(8,128)(2,1)}, u32[]{:S(2)}, u32[]{:S(2)}) async-start(bf16[8,384,512]{2,1,0:T(8,128)(2,1)} %bitcast.143), calls=%async_computation.1 | async-start | bytes 6291456 | tf_op jit(solution)/shard_map/all_to_all | solution.py:148
  197.0 205.2 %reduce-scatter.7.cloned.1.call-start = ((), (), s32[]{:S(2)}) async-start(), calls=%async_computation.7 | async-start | bytes 4456448
  258.1 8.5 %copy-start.22 = (f32[2048]{0:T(1024)S(1)}, f32[2048]{0:T(1024)}, u32[]{:S(2)}) copy-start(f32[2048]{0:T(1024)} %get-tuple-element.39) | copy-start | bytes 24580
  258.1 141.2 %all-to-all-start.2 = ((bf16[16,128,1024]{1,2,0:T(8,128)(2,1)}), bf16[16,128,1024]{1,2,0:T(8,128)(2,1)}, u32[]{:S(2)}, u32[]{:S(2)}) async-start(bf16[16,128,1024]{1,2,0:T(8,128)(2,1)} %bitcast.142), calls=%async_computation.2 | async-start | bytes 8388608 | tf_op jit(solution)/shard_map/all_to_all | solution.py:176
  (20 other events, 67.2 us)
Sparse Core Ops, SparseCore 0:
  10.2 58.9 all-gather.1
  132.2 81.8 reduce-scatter.4
  252.8 124.0 reduce-scatter.6

commit v2 on v0

--- a/solution.py
+++ b/solution.py
@@ -52,30 +52,35 @@
     return summed.reshape(row_count, per_device * block_width)
 
 
-def ring_gather(x, axis, n):
+def chip_gather(x, axis, n):
+    me = lax.axis_index(axis)
+    core = me % 2
     half = x.shape[0] // 2
-    right = [(i, (i + 1) % n) for i in range(n)]
-    left = [(i, (i - 1) % n) for i in range(n)]
-    cur_a, cur_b = x[:half], x[half:]
-    outs_a, outs_b = [cur_a], [cur_b]
-    for _ in range(1, n):
-        cur_a = lax.ppermute(cur_a, axis, right)
-        cur_b = lax.ppermute(cur_b, axis, left)
-        outs_a.append(cur_a)
-        outs_b.append(cur_b)
-    return jnp.stack(outs_a), jnp.stack(outs_b)
-
-
-def take_blocks(stack_a, stack_b, owner, local, me, n):
-    steps, half, width = stack_a.shape
-    blocks_a = stack_a.reshape(steps, half, width // BLK, BLK)
-    blocks_b = stack_b.reshape(steps, half, width // BLK, BLK)
-    step_a = (me - owner) % n
-    step_b = (owner - me) % n
-    top = blocks_a[step_a, :, local, :]
-    bottom = blocks_b[step_b, :, local, :]
+    swap = [(i, i ^ 1) for i in range(n)]
+    ring = [(i, (i + 2) % n) if i % 2 == 0 else (i, (i - 2) % n) for i in range(n)]
+    partner = lax.ppermute(x, axis, swap)
+    both = jnp.stack([x, partner])
+    pair = jnp.take(both, jnp.stack([core, 1 - core]), axis=0)
+    cur = lax.dynamic_slice_in_dim(pair, core * half, half, axis=1)
+    other = lax.dynamic_slice_in_dim(pair, (1 - core) * half, half, axis=1)
+    mine_steps, other_steps = [cur], [other]
+    for _ in range(1, n // 2):
+        cur = lax.ppermute(cur, axis, ring)
+        mine_steps.append(cur)
+        other_steps.append(lax.ppermute(cur, axis, swap))
+    return jnp.stack([jnp.stack(mine_steps), jnp.stack(other_steps)])
+
+
+def take_blocks(stacks, owner, local, me, n):
+    sides, chips, cores, half, width = stacks.shape
+    blocks = stacks.reshape(sides, chips, cores, half, width // BLK, BLK)
+    core = me % 2
+    chip = me // 2
+    owner_chip = owner // 2
+    owner_core = owner % 2
+    top = blocks[core, (chip - owner_chip) % chips, owner_core, :, local, :]
+    bottom = blocks[1 - core, (owner_chip - chip) % chips, owner_core, :, local, :]
     return jnp.concatenate([top, bottom], axis=1)
-
 
 def on_device(
     dense,
@@ -110,8 +115,8 @@
     in_rank = slot_ranks(in_owner, alive)
     out_rank = slot_ranks(out_owner, alive)
     combo = jnp.concatenate([start, grad_mixed_low], axis=1)
-    stack_a, stack_b = ring_gather(combo, "tensor", groups)
-    fetched = take_blocks(stack_a, stack_b, in_owner[mine], in_local[mine], mine, groups)
+    stacks = chip_gather(combo, "tensor", groups)
+    fetched = take_blocks(stacks, in_owner[mine], in_local[mine], mine, groups)
     taken = fetched
     product = jnp.einsum(
         "kri,kij->krj",
@@ -133,9 +138,7 @@
         + cross_bias
     )
     cross_out = (start_wide * mixed + start_wide).astype(jnp.bfloat16)
-    upstream = take_blocks(
-        stack_a, stack_b, out_owner[mine], out_local[mine] + per_device, mine, groups
-    )
+    upstream = take_blocks(stacks, out_owner[mine], out_local[mine] + per_device, mine, groups)
     upstream = upstream * switch
     backward = jnp.einsum(
         "krj,kij->kri",

time: 356 us -> 379 us (1.065)
  starting transfers between devices: 30.9 us -> 12.2 us
  waiting for transfers between devices: 115 us -> 132 us
  local copies, waits for them, and re-layouts: 64.5 us -> 78 us
  other arithmetic: 18.7 us -> 30.7 us
    ppermute x14 -> x7, starting transfers between devices: 21.6 us -> 2.63 us  [the longest x3 1.93 us: chip_gather(): cur = lax.ppermute(cur, axis, ring)]
    ppermute x14 -> x7, waiting for transfers between devices: 50 us -> 66.5 us  [the longest x3 63 us: chip_gather(): cur = lax.ppermute(cur, axis, ring)]
    gather x4 -> x5, local copies, waits for them, and re-layouts: 15.6 us -> 27.3 us  [the longest x2 11.5 us: take_blocks(): top = blocks[core, (chip - owner_chip) % chips, owner_core, :, local, :]]
    another operation x0 -> x3, other arithmetic: none -> 9.95 us  [the longest x1 5.07 us: chip_gather(): return jnp.stack([jnp.stack(mine_steps), jnp.stack(other_steps)])]
    unnamed x96 -> x70, local copies, waits for them, and re-layouts: 38.9 us -> 37.7 us
  transfers between devices with their start and end apart: 19 -> 12, of which waited for: 14 -> 7; matrix products, arithmetic and copies ran while one was open for 31% -> 33% of each run, Pallas kernels for 0% -> 0%
where the time goes in v2:
time: 379 us; the launch traced here: 378 us
  waiting for transfers between devices  132 us (35%)
  local copies, waits for them, and re-layouts  78 us (21%)
  blocking collectives  76.7 us (20%)
  matrix products  34.3 us (9%)
  other arithmetic  30.7 us (8%)
  between operations  14.2 us (4%)
  starting transfers between devices  12.2 us (3%)
    psum x1, blocking collectives, on_device(): lax.psum((jnp.sum(grad_pre, axis=0), jnp.sum(grad_mixed, axis=0)), 'dp')  76.7 us
    ppermute x3, waiting for transfers between devices, chip_gather(): cur = lax.ppermute(cur, axis, ring)  63 us
    unnamed x70, local copies, waits for them, and re-layouts  37.7 us
    all_to_all x1, waiting for transfers between devices, on_device(): lax.all_to_all(pack_parts(back_parts, chosen_in, filled_in), 'tensor', sp...  32.8 us
    all_to_all x1, waiting for transfers between devices, on_device(): lax.all_to_all(pack_parts(parts, chosen_out, filled_out), 'tensor', split...  25.4 us
    gather x2, local copies, waits for them, and re-layouts, take_blocks(): top = blocks[core, (chip - owner_chip) % chips, owner_core, :, local, :]  11.5 us
    gather x2, local copies, waits for them, and re-layouts, take_blocks(): blocks[1 - core, (owner_chip - chip) % chips, owner_core, :, local, :]  11.4 us
    mul x2, other arithmetic, pack_parts(): jnp.take(parts, chosen.reshape(-1), axis=0)  7.95 us
  transfers between devices with their start and end apart: 12, of which 7 were waited for; matrix products, arithmetic and copies ran while one was open for 33% of the time, Pallas kernels for 0%

profile of v2, /device:TPU:0, one launch (start us, length us, event | category | flops | bytes accessed | tf_op | source)
XLA Modules:
  0.0 377.7 jit_solution(8037260523021417090)
XLA Ops:
  8.3 7.6 %fusion.8 = (f32[2048]{0:T(1024)}, bf16[192,2048]{1,0:T(8,128)(2,1)S(1)}, f32[192,2048]{1,0:T(8,128)}) fusion(bf16[192,2048]{1,0:T(8,128)(2,1)} %param.16, f32[2048]{0:T(1024)} %param.13, bf16[192,2048]{1,0:T(8,128)(2,1)S(1)} %copy-done, bf16[2048,2048]{1,0:T(8,128)(2,1)} %param.12), kind=kOutput, calls=%fused_computation.33 | convolution fusion | flops 1614542848 | bytes 12337152 | tf_op jit(solution)/shard_map/dot_general | solution.py:102
  18.0 3.5 collective-permute-done
  21.5 3.3 pad_maximum_fusion
  24.8 4.3 %gather_fusion = bf16[2,192,4096]{2,1,0:T(8,128)(2,1)} fusion(bf16[2,192,4096]{2,1,0:T(8,128)(2,1)} %pad_maximum_fusion, s32[1024]{0:T(1024)S(1)} %pad_clamp_fusion.2), kind=kCustom, calls=%fused_computation.2 | custom fusion | bytes 6291464 | tf_op jit(solution)/shard_map/jit(_take)/gather | solution.py:63
  29.2 2.4 broadcast_select_fusion
  34.6 20.2 %collective-permute-done.1 = bf16[2,96,4096]{2,1,0:T(8,128)(2,1)} collective-permute-done((bf16[2,96,4096]{2,1,0:T(8,128)(2,1)S(1)}, bf16[2,96,4096]{2,1,0:T(8,128)(2,1)}, u32[]{:S(2)}, u32[]{:S(2)}) %collective-permute-start.1) | collective-permute-done | bytes 1572896 | tf_op jit(solution)/shard_map/ppermute | solution.py:68
  55.1 21.6 %collective-permute-done.2 = bf16[2,96,4096]{2,1,0:T(8,128)(2,1)} collective-permute-done((bf16[2,96,4096]{2,1,0:T(8,128)(2,1)}, bf16[2,96,4096]{2,1,0:T(8,128)(2,1)}, u32[]{:S(2)}, u32[]{:S(2)}) %collective-permute-start.2) | collective-permute-done | bytes 1572896 | tf_op jit(solution)/shard_map/ppermute | solution.py:68
  77.4 21.2 %collective-permute-done.3 = bf16[2,96,4096]{2,1,0:T(8,128)(2,1)} collective-permute-done((bf16[2,96,4096]{2,1,0:T(8,128)(2,1)}, bf16[2,96,4096]{2,1,0:T(8,128)(2,1)}, u32[]{:S(2)}, u32[]{:S(2)}) %collective-permute-start.3) | collective-permute-done | bytes 1572896 | tf_op jit(solution)/shard_map/ppermute | solution.py:68
  100.1 2.1 copy.106
  103.9 2.1 copy.107
  119.3 5.1 %maximum_maximum_fusion = bf16[2,4,2,96,8,512]{5,3,4,2,1,0:T(8,128)(2,1)} fusion(bf16[1,1,2,96,8,512]{5,3,4,2,1,0:T(8,128)(2,1)S(1)} %copy.88, bf16[1,1,2,96,8,512]{5,3,4,2,1,0:T(8,128)(2,1)S(1)} %copy.87, bf16[1,1,2,96,8,512]{5,3,4,2,1,0:T(8,128)(2,1)S(1)} %copy.86, bf16[1,1,2,96,8,512]{5,3,4,2,1,0:T(8,128)(2,1)S(1)} %copy.85, ...), kind=kLoop, calls=%fused_computation.7 | loop fusion | flops 44040192 | bytes 25165824 | tf_op jit(solution)/shard_map/stack | solution.py:71
  124.4 5.2 %gather_fusion.1 = bf16[10,96,512]{2,1,0:T(8,128)(2,1)S(1)} fusion(bf16[2,4,2,96,8,512]{5,3,4,2,1,0:T(8,128)(2,1)} %maximum_maximum_fusion, s32[10]{0:T(128)S(1)} %fusion.57), kind=kCustom, calls=%fused_computation.3 | custom fusion | bytes 1966240 | tf_op jit(solution)/shard_map/gather | solution.py:81
  129.6 5.2 %gather_fusion.2 = bf16[10,96,512]{2,1,0:T(8,128)(2,1)S(1)} fusion(bf16[2,4,2,96,8,512]{5,3,4,2,1,0:T(8,128)(2,1)} %maximum_maximum_fusion, s32[10]{0:T(128)S(1)} %get-tuple-element.54), kind=kCustom, calls=%fused_computation.4 | custom fusion | bytes 1966240 | tf_op jit(solution)/shard_map/gather | solution.py:82
  134.8 6.3 %gather_fusion.3 = bf16[10,96,512]{2,1,0:T(8,128)(2,1)} fusion(bf16[2,4,2,96,8,512]{5,3,4,2,1,0:T(8,128)(2,1)} %maximum_maximum_fusion, s32[10]{0:T(128)S(1)} %get-tuple-element.48), kind=kCustom, calls=%fused_computation.5 | custom fusion | bytes 1966240 | tf_op jit(solution)/shard_map/gather | solution.py:81
  141.1 6.2 %gather_fusion.4 = bf16[10,96,512]{2,1,0:T(8,128)(2,1)} fusion(bf16[2,4,2,96,8,512]{5,3,4,2,1,0:T(8,128)(2,1)} %maximum_maximum_fusion, s32[10]{0:T(128)S(1)} %fusion.54), kind=kCustom, calls=%fused_computation.6 | custom fusion | bytes 1966240 | tf_op jit(solution)/shard_map/gather | solution.py:82
  149.5 4.1 %convolution_convert_fusion = bf16[10,512,512]{2,1,0:T(8,128)(2,1)} fusion(bf16[10,192,512]{2,1,0:T(8,128)(2,1)S(1)} %constant_dynamic-update-slice_fusion, bf16[10,96,512]{2,1,0:T(8,128)(2,1)S(1)} %copy-done.7, bf16[10,96,512]{2,1,0:T(8,128)(2,1)S(1)} %copy-done.6, bf16[10]{0:T(256)(128)(2,1)S(1)} %copy-done.17), kind=kOutput, calls=%fused_computation.17 | convolution fusion | flops 1015152640 | bytes 9175060 | tf_op jit(solution)/shard_map/kri,krj->kij/dot_general | solution.py:161
  160.3 4.3 %convert_multiply_fusion.2 = bf16[10,192,512]{2,1,0:T(8,128)(2,1)S(1)} fusion(bf16[10,192,512]{2,1,0:T(8,128)(2,1)} %copy-done.1, bf16[10,512,512]{2,1,0:T(8,128)(2,1)} %all-gather.2.cloned.1.call-done, bf16[10]{0:T(256)(128)(2,1)} %get-tuple-element.52), kind=kOutput, calls=%fused_computation.24 | convolution fusion | flops 1008599040 | bytes 9175060 | tf_op jit(solution)/shard_map/kri,kij->krj/dot_general | solution.py:121
  164.6 2.6 gather_fusion.5
  167.2 4.0 %select_multiply_fusion.1 = bf16[16,192,512]{2,1,0:T(8,128)(2,1)} fusion(bf16[16,192,512]{2,1,0:T(8,128)(2,1)} %gather_fusion.5, pred[16]{0:T(512)(128)(4,1)} %get-tuple-element.72, bf16[16]{0:T(256)(128)(2,1)} %reshape.853), kind=kLoop, calls=%fused_computation.15 | loop fusion | flops 3145728 | bytes 6291504 | tf_op jit(solution)/shard_map/mul | solution.py:30
  171.2 4.6 %all-to-all-start = ((bf16[8,384,512]{2,1,0:T(8,128)(2,1)}), bf16[8,384,512]{2,1,0:T(8,128)(2,1)}, u32[]{:S(2)}, u32[]{:S(2)}) async-start(bf16[8,384,512]{2,1,0:T(8,128)(2,1)} %bitcast.148), calls=%async_computation | async-start | bytes 6291456 | tf_op jit(solution)/shard_map/all_to_all | solution.py:131
  177.1 5.0 %convolution_convert_fusion.1 = bf16[10,192,512]{2,1,0:T(8,128)(2,1)S(1)} fusion(bf16[10,512,512]{2,1,0:T(8,128)(2,1)} %all-gather.2.cloned.1.call-done, bf16[10,96,512]{2,1,0:T(8,128)(2,1)} %gather_fusion.4, bf16[10,96,512]{2,1,0:T(8,128)(2,1)} %gather_fusion.3, bf16[10]{0:T(256)(128)(2,1)} %get-tuple-element.52), kind=kOutput, calls=%fused_computation.25 | convolution fusion | flops 1013514240 | bytes 9175060 | tf_op jit(solution)/shard_map/krj,kij->kri/dot_general | solution.py:143
  182.2 2.6 gather_fusion.6
  184.8 4.0 %select_multiply_fusion = bf16[16,192,512]{2,1,0:T(8,128)(2,1)} fusion(bf16[16,192,512]{2,1,0:T(8,128)(2,1)} %gather_fusion.6, pred[16]{0:T(512)(128)(4,1)} %get-tuple-element.71, bf16[16]{0:T(256)(128)(2,1)} %reshape.854), kind=kLoop, calls=%fused_computation.14 | loop fusion | flops 3145728 | bytes 6291504 | tf_op jit(solution)/shard_map/mul | solution.py:30
  188.7 25.4 %all-to-all-done = bf16[8,384,512]{2,1,0:T(8,128)(2,1)} async-done(((bf16[8,384,512]{2,1,0:T(8,128)(2,1)}), bf16[8,384,512]{2,1,0:T(8,128)(2,1)}, u32[]{:S(2)}, u32[]{:S(2)}) %all-to-all-start) | async-done | bytes 3145760 | tf_op jit(solution)/shard_map/all_to_all | solution.py:131
  214.2 4.6 %all-to-all-start.1 = ((bf16[8,384,512]{2,1,0:T(8,128)(2,1)}), bf16[8,384,512]{2,1,0:T(8,128)(2,1)}, u32[]{:S(2)}, u32[]{:S(2)}) async-start(bf16[8,384,512]{2,1,0:T(8,128)(2,1)} %bitcast.147), calls=%async_computation.1 | async-start | bytes 6291456 | tf_op jit(solution)/shard_map/all_to_all | solution.py:151
  220.0 3.8 %fusion.2 = f32[4,192,512]{2,0,1:T(4,128)S(1)} fusion(bf16[16,4,1]{1,0,2:T(8,128)(2,1)S(1)} %bitcast.163, bf16[16,192,512]{2,1,0:T(8,128)(2,1)} %bitcast.16), kind=kOutput, calls=%fused_computation.12 | convolution fusion | flops 12582912 | bytes 4718720 | tf_op jit(solution)/shard_map/irb,il->rlb/dot_general | solution.py:51
  224.5 32.8 %all-to-all-done.1 = bf16[8,384,512]{2,1,0:T(8,128)(2,1)} async-done(((bf16[8,384,512]{2,1,0:T(8,128)(2,1)}), bf16[8,384,512]{2,1,0:T(8,128)(2,1)}, u32[]{:S(2)}, u32[]{:S(2)}) %all-to-all-start.1) | async-done | bytes 3145760 | tf_op jit(solution)/shard_map/all_to_all | solution.py:151
  257.3 3.8 %fusion = f32[4,192,512]{2,0,1:T(4,128)S(1)} fusion(bf16[16,4,1]{1,0,2:T(8,128)(2,1)S(1)} %bitcast.164, bf16[16,192,512]{2,1,0:T(8,128)(2,1)} %bitcast.27), kind=kOutput, calls=%fused_computation.10 | convolution fusion | flops 12582912 | bytes 4718720 | tf_op jit(solution)/shard_map/irb,il->rlb/dot_general | solution.py:51
  264.6 5.6 %convert_bitcast_fusion = bf16[2048,2048]{0,1:T(8,128)(2,1)} fusion(bf16[192,2048]{1,0:T(8,128)(2,1)S(1)} %copy-done, bf16[192,2048]{1,0:T(8,128)(2,1)S(1)} %get-tuple-element.47), kind=kOutput, calls=%fused_computation.8 | convolution fusion | flops 1614807040 | bytes 9961472 | tf_op jit(solution)/shard_map/dot_general | solution.py:171
  270.2 12.4 %copy.104 = bf16[2048,2048]{1,0:T(8,128)(2,1)} copy(bf16[2048,2048]{0,1:T(8,128)(2,1)} %convert_bitcast_fusion) | data formatting | bytes 16777216
  283.3 76.7 %all-reduce = (f32[2048]{0:T(1024)}, f32[2048]{0:T(1024)}) all-reduce(f32[2048]{0:T(1024)S(1)} %get-tuple-element.46, f32[2048]{0:T(1024)S(1)} %copy-done.18), channel_id=1, replica_groups=mesh['dp'=16,'tensor'=8] {'dp'}, use_global_device_ids=true, to_apply=%region_10.12 | all-reduce | flops 4096 | bytes 32768 | tf_op jit(solution)/shard_map/psum | solution.py:178
  361.9 6.8 %reduce-scatter.7.cloned.1.call-done = bf16[128,2048]{1,0:T(8,128)(2,1)} async-done(((bf16[2048,2048]{1,0:T(8,128)(2,1)}), bf16[128,2048]{1,0:T(8,128)(2,1)}) %reduce-scatter.7.cloned.1.call-update) | async-done | bytes 524304
  (148 shorter events, 44.1 us)
Async XLA Ops:
  7.2 8.7 %copy-start.3 = (bf16[192,2048]{1,0:T(8,128)(2,1)S(1)}, bf16[192,2048]{1,0:T(8,128)(2,1)}, u32[]{:S(2)}) copy-start(bf16[192,2048]{1,0:T(8,128)(2,1)} %param.16) | copy-start | bytes 2359300
  7.2 153.1 %all-gather.2.cloned.1.call-start = ((), (), s32[]{:S(2)}) async-start(), calls=%async_computation.4 | async-start | bytes 5570560 | tf_op jit(solution)/shard_map/all_gather | solution.py:124
  17.7 3.8 collective-permute-start
  17.8 342.2 %reduce-scatter.5.cloned.1.call-start = ((), (), s32[]{:S(2)}) async-start(), calls=%async_computation.5 | async-start | bytes 5570560 | tf_op jit(solution)/shard_map/reduce_scatter | solution.py:162
  31.6 67.1 %copy-start.15 = (s32[8,10]{1,0:T(8,128)S(1)}, s32[8,10]{1,0:T(8,128)}, u32[]{:S(2)}) copy-start(s32[8,10]{1,0:T(8,128)} %param.17) | copy-start | bytes 964
  31.6 67.1 %copy-start.16 = (s32[8,10]{1,0:T(8,128)S(1)}, s32[8,10]{1,0:T(8,128)}, u32[]{:S(2)}) copy-start(s32[8,10]{1,0:T(8,128)} %param.18) | copy-start | bytes 964
  31.6 67.1 %copy-start.26 = (s32[8]{0:T(128)S(1)}, s32[8]{0:T(128)}, u32[]{:S(2)}) copy-start(s32[8]{0:T(128)} %param.19) | copy-start | bytes 100
  33.0 21.7 %collective-permute-start.1 = (bf16[2,96,4096]{2,1,0:T(8,128)(2,1)S(1)}, bf16[2,96,4096]{2,1,0:T(8,128)(2,1)}, u32[]{:S(2)}, u32[]{:S(2)}) collective-permute-start(bf16[2,96,4096]{2,1,0:T(8,128)(2,1)S(1)} %get-tuple-element.59), channel_id=1, source_target_pairs={{0,2},{1,7},{2,4},{3,1},{4,6},{5,3},{6,0},{7,5},{8,10},{9,15},{10,... | collective-permute-start | bytes 4718600 | tf_op jit(solution)/shard_map/ppermute | solution.py:68
  54.8 21.9 %collective-permute-start.2 = (bf16[2,96,4096]{2,1,0:T(8,128)(2,1)}, bf16[2,96,4096]{2,1,0:T(8,128)(2,1)}, u32[]{:S(2)}, u32[]{:S(2)}) collective-permute-start(bf16[2,96,4096]{2,1,0:T(8,128)(2,1)} %collective-permute-done.1), channel_id=1, source_target_pairs={{0,2},{1,7},{2,4},{3,1},{4,6},{5,3},{6,0},{7,5},{8,10},{9,15},{10,... | collective-permute-start | bytes 4718600 | tf_op jit(solution)/shard_map/ppermute | solution.py:68
  76.7 21.9 %collective-permute-start.3 = (bf16[2,96,4096]{2,1,0:T(8,128)(2,1)}, bf16[2,96,4096]{2,1,0:T(8,128)(2,1)}, u32[]{:S(2)}, u32[]{:S(2)}) collective-permute-start(bf16[2,96,4096]{2,1,0:T(8,128)(2,1)} %collective-permute-done.2), channel_id=1, source_target_pairs={{0,2},{1,7},{2,4},{3,1},{4,6},{5,3},{6,0},{7,5},{8,10},{9,15},{10,... | collective-permute-start | bytes 4718600 | tf_op jit(solution)/shard_map/ppermute | solution.py:68
  76.7 32.3 %collective-permute-start.4 = (bf16[2,96,4096]{2,1,0:T(8,128)(2,1)}, bf16[2,96,4096]{2,1,0:T(8,128)(2,1)}, u32[]{:S(2)}, u32[]{:S(2)}) collective-permute-start(bf16[2,96,4096]{2,1,0:T(8,128)(2,1)} %collective-permute-done.1), channel_id=1, source_target_pairs={{0,1},{1,0},{2,3},{3,2},{4,5},{5,4},{6,7},{7,6},{8,9},{9,8},{10,11... | collective-permute-start | bytes 4718600 | tf_op jit(solution)/shard_map/ppermute | solution.py:70
  77.4 36.7 %collective-permute-start.5 = (bf16[2,96,4096]{2,1,0:T(8,128)(2,1)}, bf16[2,96,4096]{2,1,0:T(8,128)(2,1)}, u32[]{:S(2)}, u32[]{:S(2)}) collective-permute-start(bf16[2,96,4096]{2,1,0:T(8,128)(2,1)} %collective-permute-done.2), channel_id=1, source_target_pairs={{0,1},{1,0},{2,3},{3,2},{4,5},{5,4},{6,7},{7,6},{8,9},{9,8},{10,11... | collective-permute-start | bytes 4718600 | tf_op jit(solution)/shard_map/ppermute | solution.py:70
  98.6 18.1 %collective-permute-start.6 = (bf16[2,96,4096]{2,1,0:T(8,128)(2,1)}, bf16[2,96,4096]{2,1,0:T(8,128)(2,1)}, u32[]{:S(2)}, u32[]{:S(2)}) collective-permute-start(bf16[2,96,4096]{2,1,0:T(8,128)(2,1)} %collective-permute-done.3), channel_id=1, source_target_pairs={{0,1},{1,0},{2,3},{3,2},{4,5},{5,4},{6,7},{7,6},{8,9},{9,8},{10,11... | collective-permute-start | bytes 4718600 | tf_op jit(solution)/shard_map/ppermute | solution.py:70
  98.7 4.0 %copy-start.11 = (s32[8,10]{1,0:T(8,128)}, s32[8,10]{1,0:T(8,128)S(1)}, u32[]{:S(2)}) copy-start(s32[8,10]{1,0:T(8,128)S(1)} %get-tuple-element.67) | copy-start | bytes 964
  98.7 4.0 %copy-start.13 = (s32[8,10]{1,0:T(8,128)}, s32[8,10]{1,0:T(8,128)S(1)}, u32[]{:S(2)}) copy-start(s32[8,10]{1,0:T(8,128)S(1)} %get-tuple-element.68) | copy-start | bytes 964
  99.4 3.3 copy-start.20
  99.4 54.3 %copy-start.8 = (s32[8,10]{1,0:T(8,128)}, s32[8,10]{1,0:T(8,128)S(1)}, u32[]{:S(2)}) copy-start(s32[8,10]{1,0:T(8,128)S(1)} %get-tuple-element.57) | copy-start | bytes 964
  147.3 1.5 copy-start.6
  147.3 2.2 copy-start.7
  147.3 2.2 copy-start.17
  153.6 3.1 copy-start.22
  171.2 4.6 %copy-start.27 = (pred[8,2]{0,1:T(4,128)(4,1)S(1)}, pred[8,2]{0,1:T(4,128)(4,1)}, u32[]{:S(2)}) copy-start(pred[8,2]{0,1:T(4,128)(4,1)} %get-tuple-element.38) | copy-start | bytes 52
  171.2 5.4 %copy-start.25 = (s32[16]{0:T(128)S(1)}, s32[16]{0:T(128)}, u32[]{:S(2)}) copy-start(s32[16]{0:T(128)} %get-tuple-element.69) | copy-start | bytes 196
  171.2 43.0 %all-to-all-start = ((bf16[8,384,512]{2,1,0:T(8,128)(2,1)}), bf16[8,384,512]{2,1,0:T(8,128)(2,1)}, u32[]{:S(2)}, u32[]{:S(2)}) async-start(bf16[8,384,512]{2,1,0:T(8,128)(2,1)} %bitcast.148), calls=%async_computation | async-start | bytes 6291456 | tf_op jit(solution)/shard_map/all_to_all | solution.py:131
  214.2 5.1 %copy-start.14 = (s32[8,10]{1,0:T(8,128)S(1)}, s32[8,10]{1,0:T(8,128)}, u32[]{:S(2)}) copy-start(s32[8,10]{1,0:T(8,128)} %copy-done.13) | copy-start | bytes 964
  214.2 5.1 %copy-start.23 = (pred[8,10]{1,0:T(8,128)(4,1)S(1)}, pred[8,10]{1,0:T(8,128)(4,1)}, u32[]{:S(2)}) copy-start(pred[8,10]{1,0:T(8,128)(4,1)} %get-tuple-element.56) | copy-start | bytes 244
  214.2 5.1 %copy-start.24 = (pred[8,10]{1,0:T(8,128)(4,1)S(1)}, pred[8,10]{1,0:T(8,128)(4,1)}, u32[]{:S(2)}) copy-start(pred[8,10]{1,0:T(8,128)(4,1)} %get-tuple-element.63) | copy-start | bytes 244
  214.2 5.5 %copy-start.12 = (s32[8,10]{1,0:T(8,128)S(1)}, s32[8,10]{1,0:T(8,128)}, u32[]{:S(2)}) copy-start(s32[8,10]{1,0:T(8,128)} %copy-done.11) | copy-start | bytes 964
  214.2 43.1 %all-to-all-start.1 = ((bf16[8,384,512]{2,1,0:T(8,128)(2,1)}), bf16[8,384,512]{2,1,0:T(8,128)(2,1)}, u32[]{:S(2)}, u32[]{:S(2)}) async-start(bf16[8,384,512]{2,1,0:T(8,128)(2,1)} %bitcast.147), calls=%async_computation.1 | async-start | bytes 6291456 | tf_op jit(solution)/shard_map/all_to_all | solution.py:151
  218.8 149.8 %reduce-scatter.7.cloned.1.call-start = ((), (), s32[]{:S(2)}) async-start(), calls=%async_computation.6 | async-start | bytes 8912896
  261.1 1.7 copy-start.5
  261.1 1.6 copy-start.19
  (8 other events, 7.6 us)
Sparse Core Ops, SparseCore 0:
  17.9 59.0 all-gather.1
  153.8 79.3 reduce-scatter.4
  282.7 85.8 reduce-scatter.6

commit v3 on v0

--- a/solution.py
+++ b/solution.py
@@ -2,6 +2,8 @@
 import jax.numpy as jnp
 from jax import lax
 from jax.sharding import PartitionSpec as P
+from jax.experimental import pallas as pl
+from jax.experimental.pallas import tpu as pltpu
 
 BLK = 512
 SLOTS = 10
@@ -75,6 +77,68 @@
     top = blocks_a[step_a, :, local, :]
     bottom = blocks_b[step_b, :, local, :]
     return jnp.concatenate([top, bottom], axis=1)
+
+
+def slot_kernel(sa_i, sb_i, bi, sa_o, sb_o, bo, live, fa, fb, ua, ub, w, part_ref, back_ref, term_ref):
+    k = pl.program_id(0)
+    on = live[k] > 0
+    half = fa.shape[1]
+    wk = w[0]
+    top_in, bottom_in = fa[0], fb[0]
+    top_up, bottom_up = ua[0], ub[0]
+    nt = (((1,), (1,)), ((), ()))
+    tn = (((0,), (0,)), ((), ()))
+    for rows, src in ((slice(0, half), top_in), (slice(half, 2 * half), bottom_in)):
+        value = jnp.dot(src, wk, preferred_element_type=jnp.float32)
+        part_ref[0, rows, :] = jnp.where(on, value, 0.0).astype(part_ref.dtype)
+    for rows, src in ((slice(0, half), top_up), (slice(half, 2 * half), bottom_up)):
+        value = lax.dot_general(src, wk, nt, preferred_element_type=jnp.float32)
+        back_ref[0, rows, :] = jnp.where(on, value, 0.0).astype(back_ref.dtype)
+    term = lax.dot_general(top_in, top_up, tn, preferred_element_type=jnp.float32)
+    term = term + lax.dot_general(bottom_in, bottom_up, tn, preferred_element_type=jnp.float32)
+    term_ref[0] = jnp.where(on, term, 0.0).astype(term_ref.dtype)
+
+
+def slot_products(stack_a, stack_b, weights, tables):
+    slots, size, _ = weights.shape
+    steps, half, width = stack_a.shape
+    rows = 2 * half
+
+    def block(step_ref, blk_ref):
+        return pl.BlockSpec(
+            (1, half, BLK), lambda k, *t: (t[step_ref][k], 0, t[blk_ref][k])
+        )
+
+    grid_spec = pltpu.PrefetchScalarGridSpec(
+        num_scalar_prefetch=len(tables),
+        grid=(slots,),
+        in_specs=[
+            block(0, 2),
+            block(1, 2),
+            block(3, 5),
+            block(4, 5),
+            pl.BlockSpec((1, size, size), lambda k, *t: (k, 0, 0)),
+        ],
+        out_specs=[
+            pl.BlockSpec((1, rows, BLK), lambda k, *t: (k, 0, 0)),
+            pl.BlockSpec((1, rows, BLK), lambda k, *t: (k, 0, 0)),
+            pl.BlockSpec((1, size, size), lambda k, *t: (k, 0, 0)),
+        ],
+    )
+    return pl.pallas_call(
+        slot_kernel,
+        grid_spec=grid_spec,
+        out_shape=[
+            jax.ShapeDtypeStruct((slots, rows, BLK), jnp.bfloat16),
+            jax.ShapeDtypeStruct((slots, rows, BLK), jnp.bfloat16),
+            jax.ShapeDtypeStruct((slots, size, size), jnp.bfloat16),
+        ],
+        cost_estimate=pl.CostEstimate(
+            flops=6 * slots * rows * size * size,
+            bytes_accessed=slots * (4 * rows * BLK + 2 * size * size) * 2,
+            transcendentals=0,
+        ),
+    )(*tables, stack_a, stack_b, stack_a, stack_b, weights)
 
 
 def on_device(
@@ -102,7 +166,6 @@
     grad_mixed_low = grad_mixed.astype(jnp.bfloat16)
     alive = jnp.arange(SLOTS)[None, :] < live_slots[:, None]
     alive_mine = alive[mine]
-    switch = alive_mine.astype(jnp.bfloat16)[:, None, None]
     in_owner = in_blocks // per_device
     in_local = in_blocks % per_device
     out_owner = out_blocks // per_device
@@ -111,15 +174,24 @@
     out_rank = slot_ranks(out_owner, alive)
     combo = jnp.concatenate([start, grad_mixed_low], axis=1)
     stack_a, stack_b = ring_gather(combo, "tensor", groups)
-    fetched = take_blocks(stack_a, stack_b, in_owner[mine], in_local[mine], mine, groups)
-    taken = fetched
-    product = jnp.einsum(
-        "kri,kij->krj",
-        taken,
-        lax.all_gather(cross_blocks, "dp", axis=1, tiled=True),
-        preferred_element_type=jnp.float32,
-    )
-    parts = product.astype(jnp.bfloat16) * switch
+    step_a = lambda owner: (mine - owner) % groups
+    step_b = lambda owner: (owner - mine) % groups
+    tables = (
+        step_a(in_owner[mine]),
+        step_b(in_owner[mine]),
+        in_local[mine],
+        step_a(out_owner[mine]),
+        step_b(out_owner[mine]),
+        out_local[mine] + per_device,
+        alive_mine.astype(jnp.int32),
+    )
+    weights = lax.all_gather(cross_blocks, "dp", axis=1, tiled=True)
+    parts, back_parts, block_terms = slot_products(
+        stack_a.reshape(groups, -1, 2 * local_width),
+        stack_b.reshape(groups, -1, 2 * local_width),
+        weights,
+        tuple(t.astype(jnp.int32) for t in tables),
+    )
     chosen_out, filled_out = post_table(
         out_owner[mine], out_rank[mine], alive_mine, groups, capacity
     )
@@ -133,17 +205,6 @@
         + cross_bias
     )
     cross_out = (start_wide * mixed + start_wide).astype(jnp.bfloat16)
-    upstream = take_blocks(
-        stack_a, stack_b, out_owner[mine], out_local[mine] + per_device, mine, groups
-    )
-    upstream = upstream * switch
-    backward = jnp.einsum(
-        "krj,kij->kri",
-        upstream,
-        lax.all_gather(cross_blocks, "dp", axis=1, tiled=True),
-        preferred_element_type=jnp.float32,
-    )
-    back_parts = backward.astype(jnp.bfloat16)
     chosen_in, filled_in = post_table(in_owner[mine], in_rank[mine], alive_mine, groups, capacity)
     arrived_back = lax.all_to_all(
         pack_parts(back_parts, chosen_in, filled_in),
@@ -155,10 +216,9 @@
     grad_start = collect_parts(
         arrived_back, in_owner, in_local, in_rank, alive, mine, capacity, per_device
     )
-    block_terms = jnp.einsum("kri,krj->kij", fetched, upstream, preferred_element_type=jnp.float32)
-    grad_blocks = lax.psum_scatter(
-        block_terms.astype(jnp.bfloat16), "dp", scatter_dimension=1, tiled=True
-    ).astype(jnp.float32)
+    grad_blocks = lax.psum_scatter(block_terms, "dp", scatter_dimension=1, tiled=True).astype(
+        jnp.float32
+    )
     grad_start = grad_start + cot_wide * mixed + cot_wide
     sigma = jax.nn.sigmoid(preact)
     grad_pre = grad_start * sigma * (1.0 + preact * (1.0 - sigma))

time: 356 us -> 355 us (level)
  local copies, waits for them, and re-layouts: 64.5 us -> 50.1 us
  Pallas kernels: 0 us -> 14.1 us
  matrix products: 34.6 us -> 21.2 us
  other arithmetic: 18.7 us -> 29.2 us
    ppermute x7, waiting for transfers between devices: 1.05 us -> 41.6 us  [ring_gather(): cur_b = lax.ppermute(cur_b, axis, left)]
    ppermute x7, waiting for transfers between devices: 49 us -> 11.9 us  [ring_gather(): cur_a = lax.ppermute(cur_a, axis, right)]
    gather x4 -> x0, local copies, waits for them, and re-layouts: 15.6 us -> none  [the longest x2 7.85 us: take_blocks(): top = blocks_a[step_a, :, local, :]]
    pallas_call x0 -> x1, Pallas kernels: none -> 14.1 us  [slot_products(): pl.pallas_call(slot_kernel, grid_spec=grid_spec, out_shape=[jax.ShapeDtyp...]
    dot_general x3 -> x0, matrix products: 13.7 us -> none  [the longest x1 5.29 us: on_device(): jnp.einsum('krj,kij->kri', upstream, lax.all_gather(cross_blocks, 'dp', a...]
    unnamed x96 -> x69, local copies, waits for them, and re-layouts: 38.9 us -> 30.9 us
    convert_element_type x4, local copies, waits for them, and re-layouts: 1.49 us -> 5.14 us  [pack_parts(): filled.reshape(-1)[:, None, None].astype(parts.dtype)]
  transfers between devices with their start and end apart: 19 -> 19, of which waited for: 14 -> 16; matrix products, arithmetic and copies ran while one was open for 31% -> 27% of each run, Pallas kernels for 0% -> 0%
where the time goes in v3:
time: 355 us; the launch traced here: 353 us
  waiting for transfers between devices  117 us (33%)
  blocking collectives  76.6 us (22%)
  local copies, waits for them, and re-layouts  50.1 us (14%)
  starting transfers between devices  30.9 us (9%)
  other arithmetic  29.2 us (8%)
  matrix products  21.2 us (6%)
  Pallas kernels  14.1 us (4%)
  between operations  14 us (4%)
    psum x1, blocking collectives, on_device(): lax.psum((jnp.sum(grad_pre, axis=0), jnp.sum(grad_mixed, axis=0)), 'dp')  76.6 us
    ppermute x7, waiting for transfers between devices, ring_gather(): cur_b = lax.ppermute(cur_b, axis, left)  41.6 us
    all_to_all x1, waiting for transfers between devices, on_device(): lax.all_to_all(pack_parts(back_parts, chosen_in, filled_in), 'tensor', sp...  32.8 us
    unnamed x69, local copies, waits for them, and re-layouts  30.9 us
    all_to_all x1, waiting for transfers between devices, on_device(): lax.all_to_all(pack_parts(parts, chosen_out, filled_out), 'tensor', split...  23.2 us
    ppermute x7, starting transfers between devices, ring_gather(): cur_b = lax.ppermute(cur_b, axis, left)  21.4 us
    pallas_call x1, Pallas kernels, slot_products(): pl.pallas_call(slot_kernel, grid_spec=grid_spec, out_shape=[jax.ShapeDtyp...  14.1 us
    ppermute x7, waiting for transfers between devices, ring_gather(): cur_a = lax.ppermute(cur_a, axis, right)  11.9 us
  transfers between devices with their start and end apart: 19, of which 16 were waited for; matrix products, arithmetic and copies ran while one was open for 27% of the time, Pallas kernels for 0%

profile of v3, /device:TPU:0, one launch (start us, length us, event | category | flops | bytes accessed | tf_op | source)
XLA Modules:
  0.0 353.0 jit_solution(204277031771747655)
XLA Ops:
  8.3 7.6 %fusion.8 = (f32[2048]{0:T(1024)}, bf16[192,2048]{1,0:T(8,128)(2,1)S(1)}, f32[192,2048]{1,0:T(8,128)}) fusion(bf16[192,2048]{1,0:T(8,128)(2,1)} %param.16, f32[2048]{0:T(1024)} %param.13, bf16[192,2048]{1,0:T(8,128)(2,1)S(1)} %copy-done, bf16[2048,2048]{1,0:T(8,128)(2,1)} %param.12), kind=kOutput, calls=%fused_computation.22 | convolution fusion | flops 1614542848 | bytes 12337152 | tf_op jit(solution)/shard_map/dot_general | solution.py:161
  17.8 2.3 collective-permute-start.7
  23.5 6.0 %collective-permute-done.7 = bf16[96,4096]{1,0:T(8,128)(2,1)} collective-permute-done((bf16[96,4096]{1,0:T(8,128)(2,1)S(1)}, bf16[96,4096]{1,0:T(8,128)(2,1)}, u32[]{:S(2)}, u32[]{:S(2)}) %collective-permute-start.7) | collective-permute-done | bytes 786464 | tf_op jit(solution)/shard_map/ppermute | solution.py:65
  29.6 3.2 collective-permute-start.8
  34.9 2.1 bitcast_dynamic-update-slice_fusion.14
  37.0 5.6 %collective-permute-done.8 = bf16[96,4096]{1,0:T(8,128)(2,1)S(1)} collective-permute-done((bf16[96,4096]{1,0:T(8,128)(2,1)}, bf16[96,4096]{1,0:T(8,128)(2,1)S(1)}, u32[]{:S(2)}, u32[]{:S(2)}) %collective-permute-start.8) | collective-permute-done | bytes 786464 | tf_op jit(solution)/shard_map/ppermute | solution.py:65
  42.6 3.0 collective-permute-start.9
  48.7 6.4 %collective-permute-done.9 = bf16[96,4096]{1,0:T(8,128)(2,1)S(1)} collective-permute-done((bf16[96,4096]{1,0:T(8,128)(2,1)S(1)}, bf16[96,4096]{1,0:T(8,128)(2,1)S(1)}, u32[]{:S(2)}, u32[]{:S(2)}) %collective-permute-start.9) | collective-permute-done | bytes 786464 | tf_op jit(solution)/shard_map/ppermute | solution.py:65
  55.1 3.5 collective-permute-start.10
  62.3 5.9 %collective-permute-done.10 = bf16[96,4096]{1,0:T(8,128)(2,1)S(1)} collective-permute-done((bf16[96,4096]{1,0:T(8,128)(2,1)S(1)}, bf16[96,4096]{1,0:T(8,128)(2,1)S(1)}, u32[]{:S(2)}, u32[]{:S(2)}) %collective-permute-start.10) | collective-permute-done | bytes 786464 | tf_op jit(solution)/shard_map/ppermute | solution.py:65
  68.2 3.1 collective-permute-start.11
  74.9 5.9 %collective-permute-done.11 = bf16[96,4096]{1,0:T(8,128)(2,1)S(1)} collective-permute-done((bf16[96,4096]{1,0:T(8,128)(2,1)S(1)}, bf16[96,4096]{1,0:T(8,128)(2,1)S(1)}, u32[]{:S(2)}, u32[]{:S(2)}) %collective-permute-start.11) | collective-permute-done | bytes 786464 | tf_op jit(solution)/shard_map/ppermute | solution.py:65
  80.8 3.1 collective-permute-start.12
  87.5 5.9 %collective-permute-done.12 = bf16[96,4096]{1,0:T(8,128)(2,1)S(1)} collective-permute-done((bf16[96,4096]{1,0:T(8,128)(2,1)S(1)}, bf16[96,4096]{1,0:T(8,128)(2,1)S(1)}, u32[]{:S(2)}, u32[]{:S(2)}) %collective-permute-start.12) | collective-permute-done | bytes 786464 | tf_op jit(solution)/shard_map/ppermute | solution.py:65
  93.4 3.1 collective-permute-start.13
  100.2 5.8 %collective-permute-done.13 = bf16[96,4096]{1,0:T(8,128)(2,1)S(1)} collective-permute-done((bf16[96,4096]{1,0:T(8,128)(2,1)S(1)}, bf16[96,4096]{1,0:T(8,128)(2,1)S(1)}, u32[]{:S(2)}, u32[]{:S(2)}) %collective-permute-start.13) | collective-permute-done | bytes 786464 | tf_op jit(solution)/shard_map/ppermute | solution.py:65
  107.0 3.9 %collective-permute-done.6 = bf16[96,4096]{1,0:T(8,128)(2,1)S(1)} collective-permute-done((bf16[96,4096]{1,0:T(8,128)(2,1)S(1)}, bf16[96,4096]{1,0:T(8,128)(2,1)S(1)}, u32[]{:S(2)}, u32[]{:S(2)}) %collective-permute-start.6) | collective-permute-done | bytes 786464 | tf_op jit(solution)/shard_map/ppermute | solution.py:64
  111.8 14.1 %shard_map.128 = (bf16[10,192,512]{2,1,0:T(8,128)(2,1)}, bf16[10,192,512]{2,1,0:T(8,128)(2,1)}, bf16[10,512,512]{2,1,0:T(8,128)(2,1)}) custom-call(s32[10]{0:T(128)} %and_select_fusion.3.sa_i, s32[10]{0:T(128)} %get-tuple-element.70.sb_i, s32[10]{0:T(128)} %get-tuple-element.76.bi, s32[10]{0:T(128)} %and_select_fusion.1.sa_o, s32[10]{0:T(128)} %get-tuple-element.57.sb_o, ...), custom_call_target="tpu_custom_call" | custom-call | flops 3019898880 | bytes 18350080 | tf_op jit(solution)/shard_map/pallas_call | solution.py:128
  140.8 2.5 gather_fusion
  143.4 3.9 %select_multiply_fusion.1 = bf16[16,192,512]{2,1,0:T(8,128)(2,1)} fusion(bf16[16,192,512]{2,1,0:T(8,128)(2,1)} %gather_fusion, pred[16]{0:T(512)(128)(4,1)} %compare_and_fusion.3, bf16[16]{0:T(256)(128)(2,1)} %reshape.246), kind=kLoop, calls=%fused_computation.8 | loop fusion | flops 3145728 | bytes 6291504 | tf_op jit(solution)/shard_map/mul | solution.py:32
  147.3 4.6 %all-to-all-start = ((bf16[8,384,512]{2,1,0:T(8,128)(2,1)}), bf16[8,384,512]{2,1,0:T(8,128)(2,1)}, u32[]{:S(2)}, u32[]{:S(2)}) async-start(bf16[8,384,512]{2,1,0:T(8,128)(2,1)} %bitcast.71), calls=%async_computation | async-start | bytes 6291456 | tf_op jit(solution)/shard_map/all_to_all | solution.py:198
  160.6 2.5 gather_fusion.1
  163.1 4.0 %select_multiply_fusion = bf16[16,192,512]{2,1,0:T(8,128)(2,1)} fusion(bf16[16,192,512]{2,1,0:T(8,128)(2,1)} %gather_fusion.1, pred[16]{0:T(512)(128)(4,1)} %compare_and_fusion.2, bf16[16]{0:T(256)(128)(2,1)} %reshape.247), kind=kLoop, calls=%fused_computation.7 | loop fusion | flops 3145728 | bytes 6291504 | tf_op jit(solution)/shard_map/mul | solution.py:32
  167.1 23.2 %all-to-all-done = bf16[8,384,512]{2,1,0:T(8,128)(2,1)} async-done(((bf16[8,384,512]{2,1,0:T(8,128)(2,1)}), bf16[8,384,512]{2,1,0:T(8,128)(2,1)}, u32[]{:S(2)}, u32[]{:S(2)}) %all-to-all-start) | async-done | bytes 3145760 | tf_op jit(solution)/shard_map/all_to_all | solution.py:198
  190.4 4.6 %all-to-all-start.1 = ((bf16[8,384,512]{2,1,0:T(8,128)(2,1)}), bf16[8,384,512]{2,1,0:T(8,128)(2,1)}, u32[]{:S(2)}, u32[]{:S(2)}) async-start(bf16[8,384,512]{2,1,0:T(8,128)(2,1)} %bitcast.70), calls=%async_computation.1 | async-start | bytes 6291456 | tf_op jit(solution)/shard_map/all_to_all | solution.py:209
  196.1 3.9 %fusion.2 = f32[4,192,512]{2,0,1:T(4,128)S(1)} fusion(bf16[16,4,1]{1,0,2:T(8,128)(2,1)S(1)} %bitcast.77, bf16[16,192,512]{2,1,0:T(8,128)(2,1)} %bitcast.24), kind=kOutput, calls=%fused_computation.5 | convolution fusion | flops 12582912 | bytes 4718720 | tf_op jit(solution)/shard_map/irb,il->rlb/dot_general | solution.py:53
  200.6 32.8 %all-to-all-done.1 = bf16[8,384,512]{2,1,0:T(8,128)(2,1)} async-done(((bf16[8,384,512]{2,1,0:T(8,128)(2,1)}), bf16[8,384,512]{2,1,0:T(8,128)(2,1)}, u32[]{:S(2)}, u32[]{:S(2)}) %all-to-all-start.1) | async-done | bytes 3145760 | tf_op jit(solution)/shard_map/all_to_all | solution.py:209
  233.4 4.0 %fusion = f32[4,192,512]{2,0,1:T(4,128)S(1)} fusion(bf16[16,4,1]{1,0,2:T(8,128)(2,1)S(1)} %bitcast.76, bf16[16,192,512]{2,1,0:T(8,128)(2,1)} %bitcast.29), kind=kOutput, calls=%fused_computation.3 | convolution fusion | flops 12582912 | bytes 4718720 | tf_op jit(solution)/shard_map/irb,il->rlb/dot_general | solution.py:53
  239.9 5.7 %convert_bitcast_fusion = bf16[2048,2048]{0,1:T(8,128)(2,1)} fusion(bf16[192,2048]{1,0:T(8,128)(2,1)S(1)} %copy-done, bf16[192,2048]{1,0:T(8,128)(2,1)S(1)} %get-tuple-element.48), kind=kOutput, calls=%fused_computation.2 | convolution fusion | flops 1614807040 | bytes 9961472 | tf_op jit(solution)/shard_map/dot_general | solution.py:228
  245.7 12.4 %copy.61 = bf16[2048,2048]{1,0:T(8,128)(2,1)} copy(bf16[2048,2048]{0,1:T(8,128)(2,1)} %convert_bitcast_fusion) | data formatting | bytes 16777216
  258.7 76.6 %all-reduce = (f32[2048]{0:T(1024)}, f32[2048]{0:T(1024)}) all-reduce(f32[2048]{0:T(1024)S(1)} %get-tuple-element.47, f32[2048]{0:T(1024)S(1)} %copy-done.14), channel_id=1, replica_groups=mesh['dp'=16,'tensor'=8] {'dp'}, use_global_device_ids=true, to_apply=%region_10.12 | all-reduce | flops 4096 | bytes 32768 | tf_op jit(solution)/shard_map/psum | solution.py:235
  337.2 6.8 %reduce-scatter.7.cloned.1.call-done = bf16[128,2048]{1,0:T(8,128)(2,1)} async-done(((bf16[2048,2048]{1,0:T(8,128)(2,1)}), bf16[128,2048]{1,0:T(8,128)(2,1)}) %reduce-scatter.7.cloned.1.call-update) | async-done | bytes 524304
  (140 shorter events, 60.8 us)
Async XLA Ops:
  7.2 104.6 %all-gather.2.cloned.1.call-start = ((), (), s32[]{:S(2)}) async-start(), calls=%async_computation.4 | async-start | bytes 5570560 | tf_op jit(solution)/shard_map/all_gather | solution.py:188
  7.9 8.0 %copy-start.3 = (bf16[192,2048]{1,0:T(8,128)(2,1)S(1)}, bf16[192,2048]{1,0:T(8,128)(2,1)}, u32[]{:S(2)}) copy-start(bf16[192,2048]{1,0:T(8,128)(2,1)} %param.16) | copy-start | bytes 2359300
  7.9 327.4 %reduce-scatter.5.cloned.1.call-start = ((), (), s32[]{:S(2)}) async-start(), calls=%async_computation.5 | async-start | bytes 5570560 | tf_op jit(solution)/shard_map/reduce_scatter | solution.py:219
  17.8 11.8 %collective-permute-start.7 = (bf16[96,4096]{1,0:T(8,128)(2,1)S(1)}, bf16[96,4096]{1,0:T(8,128)(2,1)}, u32[]{:S(2)}, u32[]{:S(2)}) collective-permute-start(bf16[96,4096]{1,0:T(8,128)(2,1)S(1)} %get-tuple-element.52), channel_id=1, source_target_pairs={{0,7},{1,0},{2,1},{3,2},{4,3},{5,4},{6,5},{7,6},{8,15},{9,8},{10,9... | collective-permute-start | bytes 2359304 | tf_op jit(solution)/shard_map/ppermute | solution.py:65
  20.1 14.8 %collective-permute-start = (bf16[96,4096]{1,0:T(8,128)(2,1)S(1)}, bf16[96,4096]{1,0:T(8,128)(2,1)}, u32[]{:S(2)}, u32[]{:S(2)}) collective-permute-start(bf16[96,4096]{1,0:T(8,128)(2,1)S(1)} %get-tuple-element.65), channel_id=1, source_target_pairs={{0,1},{1,2},{2,3},{3,4},{4,5},{5,6},{6,7},{7,0},{8,9},{9,10},{10,1... | collective-permute-start | bytes 2359304 | tf_op jit(solution)/shard_map/ppermute | solution.py:64
  20.1 28.6 %copy-start.8 = (s32[8,10]{1,0:T(8,128)}, s32[8,10]{1,0:T(8,128)S(1)}, u32[]{:S(2)}) copy-start(s32[8,10]{1,0:T(8,128)S(1)} %add_select_fusion) | copy-start | bytes 964
  20.8 27.9 %copy-start.16 = (pred[8,10]{1,0:T(8,128)(4,1)}, pred[8,10]{1,0:T(8,128)(4,1)S(1)}, u32[]{:S(2)}) copy-start(pred[8,10]{1,0:T(8,128)(4,1)S(1)} %get-tuple-element.68) | copy-start | bytes 244
  20.8 105.1 %copy-start.6 = (s32[8,10]{1,0:T(8,128)}, s32[8,10]{1,0:T(8,128)S(1)}, u32[]{:S(2)}) copy-start(s32[8,10]{1,0:T(8,128)S(1)} %get-tuple-element.62) | copy-start | bytes 964
  20.8 105.8 %copy-start.7 = (s32[8,10]{1,0:T(8,128)}, s32[8,10]{1,0:T(8,128)S(1)}, u32[]{:S(2)}) copy-start(s32[8,10]{1,0:T(8,128)S(1)} %get-tuple-element.67) | copy-start | bytes 964
  20.8 27.9 %copy-start.10 = (s32[8,10]{1,0:T(8,128)}, s32[8,10]{1,0:T(8,128)S(1)}, u32[]{:S(2)}) copy-start(s32[8,10]{1,0:T(8,128)S(1)} %add_select_fusion.2) | copy-start | bytes 964
  22.5 26.2 %copy-start.24 = (s32[10]{0:T(128)}, s32[10]{0:T(128)S(1)}, u32[]{:S(2)}) copy-start(s32[10]{0:T(128)S(1)} %get-tuple-element.58) | copy-start | bytes 124
  22.5 26.2 %copy-start.25 = (s32[10]{0:T(128)}, s32[10]{0:T(128)S(1)}, u32[]{:S(2)}) copy-start(s32[10]{0:T(128)S(1)} %get-tuple-element.71) | copy-start | bytes 124
  29.6 13.0 %collective-permute-start.8 = (bf16[96,4096]{1,0:T(8,128)(2,1)}, bf16[96,4096]{1,0:T(8,128)(2,1)S(1)}, u32[]{:S(2)}, u32[]{:S(2)}) collective-permute-start(bf16[96,4096]{1,0:T(8,128)(2,1)} %collective-permute-done.7), channel_id=1, source_target_pairs={{0,7},{1,0},{2,1},{3,2},{4,3},{5,4},{6,5},{7,6},{8,15},{9,8},{10,9... | collective-permute-start | bytes 2359304 | tf_op jit(solution)/shard_map/ppermute | solution.py:65
  34.9 12.8 %collective-permute-start.1 = (bf16[96,4096]{1,0:T(8,128)(2,1)}, bf16[96,4096]{1,0:T(8,128)(2,1)S(1)}, u32[]{:S(2)}, u32[]{:S(2)}) collective-permute-start(bf16[96,4096]{1,0:T(8,128)(2,1)} %collective-permute-done), channel_id=1, source_target_pairs={{0,1},{1,2},{2,3},{3,4},{4,5},{5,6},{6,7},{7,0},{8,9},{9,10},{10,1... | collective-permute-start | bytes 2359304 | tf_op jit(solution)/shard_map/ppermute | solution.py:64
  42.6 12.5 %collective-permute-start.9 = (bf16[96,4096]{1,0:T(8,128)(2,1)S(1)}, bf16[96,4096]{1,0:T(8,128)(2,1)S(1)}, u32[]{:S(2)}, u32[]{:S(2)}) collective-permute-start(bf16[96,4096]{1,0:T(8,128)(2,1)S(1)} %collective-permute-done.8), channel_id=1, source_target_pairs={{0,7},{1,0},{2,1},{3,2},{4,3},{5,4},{6,5},{7,6},{8,15},{9,8},{10,9... | collective-permute-start | bytes 2359304 | tf_op jit(solution)/shard_map/ppermute | solution.py:65
  47.7 12.6 %collective-permute-start.2 = (bf16[96,4096]{1,0:T(8,128)(2,1)S(1)}, bf16[96,4096]{1,0:T(8,128)(2,1)S(1)}, u32[]{:S(2)}, u32[]{:S(2)}) collective-permute-start(bf16[96,4096]{1,0:T(8,128)(2,1)S(1)} %collective-permute-done.1), channel_id=1, source_target_pairs={{0,1},{1,2},{2,3},{3,4},{4,5},{5,6},{6,7},{7,0},{8,9},{9,10},{10,1... | collective-permute-start | bytes 2359304 | tf_op jit(solution)/shard_map/ppermute | solution.py:64
  55.1 13.0 %collective-permute-start.10 = (bf16[96,4096]{1,0:T(8,128)(2,1)S(1)}, bf16[96,4096]{1,0:T(8,128)(2,1)S(1)}, u32[]{:S(2)}, u32[]{:S(2)}) collective-permute-start(bf16[96,4096]{1,0:T(8,128)(2,1)S(1)} %collective-permute-done.9), channel_id=1, source_target_pairs={{0,7},{1,0},{2,1},{3,2},{4,3},{5,4},{6,5},{7,6},{8,15},{9,8},{10,9... | collective-permute-start | bytes 2359304 | tf_op jit(solution)/shard_map/ppermute | solution.py:65
  60.4 12.6 %collective-permute-start.3 = (bf16[96,4096]{1,0:T(8,128)(2,1)S(1)}, bf16[96,4096]{1,0:T(8,128)(2,1)S(1)}, u32[]{:S(2)}, u32[]{:S(2)}) collective-permute-start(bf16[96,4096]{1,0:T(8,128)(2,1)S(1)} %collective-permute-done.2), channel_id=1, source_target_pairs={{0,1},{1,2},{2,3},{3,4},{4,5},{5,6},{6,7},{7,0},{8,9},{9,10},{10,1... | collective-permute-start | bytes 2359304 | tf_op jit(solution)/shard_map/ppermute | solution.py:64
  68.2 12.6 %collective-permute-start.11 = (bf16[96,4096]{1,0:T(8,128)(2,1)S(1)}, bf16[96,4096]{1,0:T(8,128)(2,1)S(1)}, u32[]{:S(2)}, u32[]{:S(2)}) collective-permute-start(bf16[96,4096]{1,0:T(8,128)(2,1)S(1)} %collective-permute-done.10), channel_id=1, source_target_pairs={{0,7},{1,0},{2,1},{3,2},{4,3},{5,4},{6,5},{7,6},{8,15},{9,8},{10,9... | collective-permute-start | bytes 2359304 | tf_op jit(solution)/shard_map/ppermute | solution.py:65
  73.0 12.6 %collective-permute-start.4 = (bf16[96,4096]{1,0:T(8,128)(2,1)S(1)}, bf16[96,4096]{1,0:T(8,128)(2,1)S(1)}, u32[]{:S(2)}, u32[]{:S(2)}) collective-permute-start(bf16[96,4096]{1,0:T(8,128)(2,1)S(1)} %collective-permute-done.3), channel_id=1, source_target_pairs={{0,1},{1,2},{2,3},{3,4},{4,5},{5,6},{6,7},{7,0},{8,9},{9,10},{10,1... | collective-permute-start | bytes 2359304 | tf_op jit(solution)/shard_map/ppermute | solution.py:64
  80.8 12.6 %collective-permute-start.12 = (bf16[96,4096]{1,0:T(8,128)(2,1)S(1)}, bf16[96,4096]{1,0:T(8,128)(2,1)S(1)}, u32[]{:S(2)}, u32[]{:S(2)}) collective-permute-start(bf16[96,4096]{1,0:T(8,128)(2,1)S(1)} %collective-permute-done.11), channel_id=1, source_target_pairs={{0,7},{1,0},{2,1},{3,2},{4,3},{5,4},{6,5},{7,6},{8,15},{9,8},{10,9... | collective-permute-start | bytes 2359304 | tf_op jit(solution)/shard_map/ppermute | solution.py:65
  85.6 12.6 %collective-permute-start.5 = (bf16[96,4096]{1,0:T(8,128)(2,1)S(1)}, bf16[96,4096]{1,0:T(8,128)(2,1)S(1)}, u32[]{:S(2)}, u32[]{:S(2)}) collective-permute-start(bf16[96,4096]{1,0:T(8,128)(2,1)S(1)} %collective-permute-done.4), channel_id=1, source_target_pairs={{0,1},{1,2},{2,3},{3,4},{4,5},{5,6},{6,7},{7,0},{8,9},{9,10},{10,1... | collective-permute-start | bytes 2359304 | tf_op jit(solution)/shard_map/ppermute | solution.py:64
  93.4 12.6 %collective-permute-start.13 = (bf16[96,4096]{1,0:T(8,128)(2,1)S(1)}, bf16[96,4096]{1,0:T(8,128)(2,1)S(1)}, u32[]{:S(2)}, u32[]{:S(2)}) collective-permute-start(bf16[96,4096]{1,0:T(8,128)(2,1)S(1)} %collective-permute-done.12), channel_id=1, source_target_pairs={{0,7},{1,0},{2,1},{3,2},{4,3},{5,4},{6,5},{7,6},{8,15},{9,8},{10,9... | collective-permute-start | bytes 2359304 | tf_op jit(solution)/shard_map/ppermute | solution.py:65
  98.2 12.6 %collective-permute-start.6 = (bf16[96,4096]{1,0:T(8,128)(2,1)S(1)}, bf16[96,4096]{1,0:T(8,128)(2,1)S(1)}, u32[]{:S(2)}, u32[]{:S(2)}) collective-permute-start(bf16[96,4096]{1,0:T(8,128)(2,1)S(1)} %collective-permute-done.5), channel_id=1, source_target_pairs={{0,1},{1,2},{2,3},{3,4},{4,5},{5,6},{6,7},{7,0},{8,9},{9,10},{10,1... | collective-permute-start | bytes 2359304 | tf_op jit(solution)/shard_map/ppermute | solution.py:64
  125.9 14.9 %copy-start.2 = (bf16[10,192,512]{2,1,0:T(8,128)(2,1)S(1)}, bf16[10,192,512]{2,1,0:T(8,128)(2,1)}, u32[]{:S(2)}) copy-start(bf16[10,192,512]{2,1,0:T(8,128)(2,1)} %get-tuple-element.9) | copy-start | bytes 5898244
  147.3 13.3 %copy-start.1 = (bf16[10,192,512]{2,1,0:T(8,128)(2,1)S(1)}, bf16[10,192,512]{2,1,0:T(8,128)(2,1)}, u32[]{:S(2)}) copy-start(bf16[10,192,512]{2,1,0:T(8,128)(2,1)} %get-tuple-element.10) | copy-start | bytes 5898244
  147.3 43.0 %all-to-all-start = ((bf16[8,384,512]{2,1,0:T(8,128)(2,1)}), bf16[8,384,512]{2,1,0:T(8,128)(2,1)}, u32[]{:S(2)}, u32[]{:S(2)}) async-start(bf16[8,384,512]{2,1,0:T(8,128)(2,1)} %bitcast.71), calls=%async_computation | async-start | bytes 6291456 | tf_op jit(solution)/shard_map/all_to_all | solution.py:198
  190.4 5.0 %copy-start.17 = (pred[8,10]{1,0:T(8,128)(4,1)S(1)}, pred[8,10]{1,0:T(8,128)(4,1)}, u32[]{:S(2)}) copy-start(pred[8,10]{1,0:T(8,128)(4,1)} %get-tuple-element.61) | copy-start | bytes 244
  190.4 5.0 %copy-start.18 = (pred[8,10]{1,0:T(8,128)(4,1)S(1)}, pred[8,10]{1,0:T(8,128)(4,1)}, u32[]{:S(2)}) copy-start(pred[8,10]{1,0:T(8,128)(4,1)} %get-tuple-element.66) | copy-start | bytes 244
  190.4 5.3 %copy-start.9 = (s32[8,10]{1,0:T(8,128)S(1)}, s32[8,10]{1,0:T(8,128)}, u32[]{:S(2)}) copy-start(s32[8,10]{1,0:T(8,128)} %copy-done.8) | copy-start | bytes 964
  190.4 43.1 %all-to-all-start.1 = ((bf16[8,384,512]{2,1,0:T(8,128)(2,1)}), bf16[8,384,512]{2,1,0:T(8,128)(2,1)}, u32[]{:S(2)}, u32[]{:S(2)}) async-start(bf16[8,384,512]{2,1,0:T(8,128)(2,1)} %bitcast.70), calls=%async_computation.1 | async-start | bytes 6291456 | tf_op jit(solution)/shard_map/all_to_all | solution.py:209
  195.0 149.0 %reduce-scatter.7.cloned.1.call-start = ((), (), s32[]{:S(2)}) async-start(), calls=%async_computation.6 | async-start | bytes 8912896
  (13 other events, 40.4 us)
Sparse Core Ops, SparseCore 0:
  10.2 58.9 all-gather.1
  126.0 79.0 reduce-scatter.4
  258.2 85.7 reduce-scatter.6

commit v4 on v3

--- a/solution.py
+++ b/solution.py
@@ -139,6 +139,30 @@
             transcendentals=0,
         ),
     )(*tables, stack_a, stack_b, stack_a, stack_b, weights)
+
+
+def outer_kernel(left, right, out):
+    out[...] = lax.dot_general(
+        left[...], right[...], (((0,), (0,)), ((), ())), preferred_element_type=jnp.float32
+    ).astype(out.dtype)
+
+
+def group_outer(left, right, tile_m=512, tile_n=1024):
+    rows, m = left.shape
+    n = right.shape[1]
+    return pl.pallas_call(
+        outer_kernel,
+        grid=(m // tile_m, n // tile_n),
+        in_specs=[
+            pl.BlockSpec((rows, tile_m), lambda i, j: (0, i)),
+            pl.BlockSpec((rows, tile_n), lambda i, j: (0, j)),
+        ],
+        out_specs=pl.BlockSpec((tile_m, tile_n), lambda i, j: (i, j)),
+        out_shape=jax.ShapeDtypeStruct((m, n), jnp.bfloat16),
+        cost_estimate=pl.CostEstimate(
+            flops=2 * rows * m * n, bytes_accessed=2 * (rows * (m + n) + m * n), transcendentals=0
+        ),
+    )(left, right)
 
 
 def on_device(
@@ -225,9 +249,7 @@
     grad_pre_low = grad_pre.astype(jnp.bfloat16)
     taken = dense
     grad_bottom = lax.psum_scatter(
-        lax.dot_general(
-            taken, grad_pre_low, (((0,), (0,)), ((), ())), preferred_element_type=jnp.float32
-        ).astype(jnp.bfloat16),
+        group_outer(taken, grad_pre_low),
         "dp",
         scatter_dimension=0,
         tiled=True,

time: 355 us -> 327 us (0.921)
  local copies, waits for them, and re-layouts: 50.1 us -> 22.3 us
  other arithmetic: 29.2 us -> 18.1 us
  waiting for transfers between devices: 117 us -> 128 us
  Pallas kernels: 14.1 us -> 23.4 us
  matrix products: 21.2 us -> 13 us
    unnamed x69 -> x32, local copies, waits for them, and re-layouts: 30.9 us -> 12.7 us
    pallas_call x0 -> x1, Pallas kernels: none -> 9.38 us  [group_outer(): pl.pallas_call(outer_kernel, grid=(m // tile_m, n // tile_n), in_specs=[p...]
    ppermute x7, waiting for transfers between devices: 41.6 us -> 51 us  [ring_gather(): cur_b = lax.ppermute(cur_b, axis, left)]
    ppermute x7, waiting for transfers between devices: 11.9 us -> 3.7 us  [ring_gather(): cur_a = lax.ppermute(cur_a, axis, right)]
    reduce_scatter x0 -> x1, waiting for transfers between devices: none -> 7.6 us  [on_device(): lax.psum_scatter(group_outer(taken, grad_pre_low), 'dp', scatter_dimensio...]
    unnamed x4 -> x3, waiting for transfers between devices: 7.49 us -> 0.71 us
    all_to_all x1, waiting for transfers between devices: 23.2 us -> 30 us  [on_device(): lax.all_to_all(pack_parts(parts, chosen_out, filled_out), 'tensor', split...]
    dot_general x1 -> x0, matrix products: 5.75 us -> none  [on_device(): lax.dot_general(taken, grad_pre_low, (((0,), (0,)), ((), ())), preferred_...]
  transfers between devices with their start and end apart: 19 -> 19, of which waited for: 16 -> 15; matrix products, arithmetic and copies ran while one was open for 27% -> 16% of each run, Pallas kernels for 0% -> 3%
where the time goes in v4:
time: 327 us; the launch traced here: 326 us
  waiting for transfers between devices  128 us (39%)
  blocking collectives  77 us (24%)
  starting transfers between devices  30.2 us (9%)
  Pallas kernels  23.4 us (7%)
  local copies, waits for them, and re-layouts  22.3 us (7%)
  other arithmetic  18.1 us (6%)
  between operations  14 us (4%)
  matrix products  13 us (4%)
    psum x1, blocking collectives, on_device(): lax.psum((jnp.sum(grad_pre, axis=0), jnp.sum(grad_mixed, axis=0)), 'dp')  77 us
    ppermute x7, waiting for transfers between devices, ring_gather(): cur_b = lax.ppermute(cur_b, axis, left)  51 us
    all_to_all x1, waiting for transfers between devices, on_device(): lax.all_to_all(pack_parts(back_parts, chosen_in, filled_in), 'tensor', sp...  34.8 us
    all_to_all x1, waiting for transfers between devices, on_device(): lax.all_to_all(pack_parts(parts, chosen_out, filled_out), 'tensor', split...  30 us
    ppermute x7, starting transfers between devices, ring_gather(): cur_b = lax.ppermute(cur_b, axis, left)  21.8 us
    pallas_call x1, Pallas kernels, slot_products(): pl.pallas_call(slot_kernel, grid_spec=grid_spec, out_shape=[jax.ShapeDtyp...  14.1 us
    unnamed x32, local copies, waits for them, and re-layouts  12.7 us
    pallas_call x1, Pallas kernels, group_outer(): pl.pallas_call(outer_kernel, grid=(m // tile_m, n // tile_n), in_specs=[p...  9.38 us
  transfers between devices with their start and end apart: 19, of which 15 were waited for; matrix products, arithmetic and copies ran while one was open for 16% of the time, Pallas kernels for 3%

profile of v4, /device:TPU:0, one launch (start us, length us, event | category | flops | bytes accessed | tf_op | source)
XLA Modules:
  0.0 325.8 jit_solution(14210500710864195669)
XLA Ops:
  8.0 7.1 %fusion.8 = (f32[2048]{0:T(1024)S(1)}, bf16[192,2048]{1,0:T(8,128)(2,1)S(1)}, f32[192,2048]{1,0:T(8,128)}) fusion(bf16[192,2048]{1,0:T(8,128)(2,1)} %param.16, f32[2048]{0:T(1024)} %param.13, bf16[192,2048]{1,0:T(8,128)(2,1)} %left.1, bf16[2048,2048]{1,0:T(8,128)(2,1)} %param.12), kind=kOutput, calls=%fused_computation.21 | convolution fusion | flops 1614542848 | bytes 12337152 | tf_op jit(solution)/shard_map/dot_general | solution.py:185
  17.0 2.3 collective-permute-start.7
  22.0 6.7 %collective-permute-done.7 = bf16[96,4096]{1,0:T(8,128)(2,1)S(1)} collective-permute-done((bf16[96,4096]{1,0:T(8,128)(2,1)S(1)}, bf16[96,4096]{1,0:T(8,128)(2,1)S(1)}, u32[]{:S(2)}, u32[]{:S(2)}) %collective-permute-start.7) | collective-permute-done | bytes 786464 | tf_op jit(solution)/shard_map/ppermute | solution.py:65
  28.8 3.1 collective-permute-start.8
  33.7 7.6 %collective-permute-done.8 = bf16[96,4096]{1,0:T(8,128)(2,1)S(1)} collective-permute-done((bf16[96,4096]{1,0:T(8,128)(2,1)S(1)}, bf16[96,4096]{1,0:T(8,128)(2,1)S(1)}, u32[]{:S(2)}, u32[]{:S(2)}) %collective-permute-start.8) | collective-permute-done | bytes 786464 | tf_op jit(solution)/shard_map/ppermute | solution.py:65
  41.4 3.1 collective-permute-start.9
  46.5 7.5 %collective-permute-done.9 = bf16[96,4096]{1,0:T(8,128)(2,1)S(1)} collective-permute-done((bf16[96,4096]{1,0:T(8,128)(2,1)S(1)}, bf16[96,4096]{1,0:T(8,128)(2,1)S(1)}, u32[]{:S(2)}, u32[]{:S(2)}) %collective-permute-start.9) | collective-permute-done | bytes 786464 | tf_op jit(solution)/shard_map/ppermute | solution.py:65
  54.0 3.5 %collective-permute-start.10 = (bf16[96,4096]{1,0:T(8,128)(2,1)S(1)}, bf16[96,4096]{1,0:T(8,128)(2,1)S(1)}, u32[]{:S(2)}, u32[]{:S(2)}) collective-permute-start(bf16[96,4096]{1,0:T(8,128)(2,1)S(1)} %collective-permute-done.9), channel_id=1, source_target_pairs={{0,7},{1,0},{2,1},{3,2},{4,3},{5,4},{6,5},{7,6},{8,15},{9,8},{10,9... | collective-permute-start | bytes 2359304 | tf_op jit(solution)/shard_map/ppermute | solution.py:65
  60.1 6.9 %collective-permute-done.10 = bf16[96,4096]{1,0:T(8,128)(2,1)S(1)} collective-permute-done((bf16[96,4096]{1,0:T(8,128)(2,1)S(1)}, bf16[96,4096]{1,0:T(8,128)(2,1)S(1)}, u32[]{:S(2)}, u32[]{:S(2)}) %collective-permute-start.10) | collective-permute-done | bytes 786464 | tf_op jit(solution)/shard_map/ppermute | solution.py:65
  67.0 3.5 %collective-permute-start.11 = (bf16[96,4096]{1,0:T(8,128)(2,1)S(1)}, bf16[96,4096]{1,0:T(8,128)(2,1)S(1)}, u32[]{:S(2)}, u32[]{:S(2)}) collective-permute-start(bf16[96,4096]{1,0:T(8,128)(2,1)S(1)} %collective-permute-done.10), channel_id=1, source_target_pairs={{0,7},{1,0},{2,1},{3,2},{4,3},{5,4},{6,5},{7,6},{8,15},{9,8},{10,9... | collective-permute-start | bytes 2359304 | tf_op jit(solution)/shard_map/ppermute | solution.py:65
  72.6 7.4 %collective-permute-done.11 = bf16[96,4096]{1,0:T(8,128)(2,1)S(1)} collective-permute-done((bf16[96,4096]{1,0:T(8,128)(2,1)S(1)}, bf16[96,4096]{1,0:T(8,128)(2,1)S(1)}, u32[]{:S(2)}, u32[]{:S(2)}) %collective-permute-start.11) | collective-permute-done | bytes 786464 | tf_op jit(solution)/shard_map/ppermute | solution.py:65
  80.1 3.1 collective-permute-start.12
  85.3 7.4 %collective-permute-done.12 = bf16[96,4096]{1,0:T(8,128)(2,1)S(1)} collective-permute-done((bf16[96,4096]{1,0:T(8,128)(2,1)S(1)}, bf16[96,4096]{1,0:T(8,128)(2,1)S(1)}, u32[]{:S(2)}, u32[]{:S(2)}) %collective-permute-start.12) | collective-permute-done | bytes 786464 | tf_op jit(solution)/shard_map/ppermute | solution.py:65
  92.7 3.1 collective-permute-start.13
  97.9 7.4 %collective-permute-done.13 = bf16[96,4096]{1,0:T(8,128)(2,1)S(1)} collective-permute-done((bf16[96,4096]{1,0:T(8,128)(2,1)S(1)}, bf16[96,4096]{1,0:T(8,128)(2,1)S(1)}, u32[]{:S(2)}, u32[]{:S(2)}) %collective-permute-start.13) | collective-permute-done | bytes 786464 | tf_op jit(solution)/shard_map/ppermute | solution.py:65
  106.3 2.4 collective-permute-done.6
  109.6 14.1 %shard_map.128 = (bf16[10,192,512]{2,1,0:T(8,128)(2,1)}, bf16[10,192,512]{2,1,0:T(8,128)(2,1)}, bf16[10,512,512]{2,1,0:T(8,128)(2,1)}) custom-call(s32[10]{0:T(128)} %and_select_fusion.3.sa_i, s32[10]{0:T(128)} %get-tuple-element.45.sb_i, s32[10]{0:T(128)} %get-tuple-element.51.bi, s32[10]{0:T(128)} %and_select_fusion.1.sa_o, s32[10]{0:T(128)} %get-tuple-element.32.sb_o, ...), custom_call_target="tpu_custom_call" | custom-call | flops 3019898880 | bytes 18350080 | tf_op jit(solution)/shard_map/pallas_call | solution.py:128
  125.3 2.3 gather_fusion
  127.6 2.0 select_multiply_fusion.1
  129.6 3.6 %all-to-all-start = ((bf16[8,384,512]{2,1,0:T(8,128)(2,1)}), bf16[8,384,512]{2,1,0:T(8,128)(2,1)S(1)}, u32[]{:S(2)}, u32[]{:S(2)}) async-start(bf16[8,384,512]{2,1,0:T(8,128)(2,1)} %bitcast.67), calls=%async_computation | async-start | bytes 6291456 | tf_op jit(solution)/shard_map/all_to_all | solution.py:222
  133.7 4.0 %gather_fusion.1 = bf16[16,192,512]{2,1,0:T(8,128)(2,1)} fusion(bf16[10,192,512]{2,1,0:T(8,128)(2,1)} %get-tuple-element.10, s32[1024]{0:T(1024)S(1)} %pad_clamp_fusion), kind=kCustom, calls=%fused_computation.1.clone | custom fusion | bytes 6291520 | tf_op jit(solution)/shard_map/jit(_take)/gather | solution.py:32
  137.7 4.0 %select_multiply_fusion = bf16[16,192,512]{2,1,0:T(8,128)(2,1)} fusion(bf16[16,192,512]{2,1,0:T(8,128)(2,1)} %gather_fusion.1, pred[16]{0:T(512)(128)(4,1)S(1)} %compare_and_fusion.2, bf16[16]{0:T(256)(128)(2,1)S(1)} %reshape.247), kind=kLoop, calls=%fused_computation.6 | loop fusion | flops 3145728 | bytes 6291504 | tf_op jit(solution)/shard_map/mul | solution.py:32
  141.6 30.0 %all-to-all-done = bf16[8,384,512]{2,1,0:T(8,128)(2,1)S(1)} async-done(((bf16[8,384,512]{2,1,0:T(8,128)(2,1)}), bf16[8,384,512]{2,1,0:T(8,128)(2,1)S(1)}, u32[]{:S(2)}, u32[]{:S(2)}) %all-to-all-start) | async-done | bytes 3145760 | tf_op jit(solution)/shard_map/all_to_all | solution.py:222
  171.6 4.4 %all-to-all-start.1 = ((bf16[8,384,512]{2,1,0:T(8,128)(2,1)}), bf16[8,384,512]{2,1,0:T(8,128)(2,1)}, u32[]{:S(2)}, u32[]{:S(2)}) async-start(bf16[8,384,512]{2,1,0:T(8,128)(2,1)} %bitcast.66), calls=%async_computation.1 | async-start | bytes 6291456 | tf_op jit(solution)/shard_map/all_to_all | solution.py:233
  177.2 1.9 fusion.2
  179.7 34.8 %all-to-all-done.1 = bf16[8,384,512]{2,1,0:T(8,128)(2,1)} async-done(((bf16[8,384,512]{2,1,0:T(8,128)(2,1)}), bf16[8,384,512]{2,1,0:T(8,128)(2,1)}, u32[]{:S(2)}, u32[]{:S(2)}) %all-to-all-start.1) | async-done | bytes 3145760 | tf_op jit(solution)/shard_map/all_to_all | solution.py:233
  214.5 4.0 %fusion = f32[4,192,512]{2,0,1:T(4,128)S(1)} fusion(bf16[16,4,1]{1,0,2:T(8,128)(2,1)S(1)} %bitcast.72, bf16[16,192,512]{2,1,0:T(8,128)(2,1)} %bitcast.29), kind=kOutput, calls=%fused_computation.2 | convolution fusion | flops 12582912 | bytes 4718720 | tf_op jit(solution)/shard_map/irb,il->rlb/dot_general | solution.py:53
  219.1 2.1 fusion.28
  221.3 9.4 %shard_map.129 = bf16[2048,2048]{1,0:T(8,128)(2,1)} custom-call(bf16[192,2048]{1,0:T(8,128)(2,1)} %left.1, bf16[192,2048]{1,0:T(8,128)(2,1)} %get-tuple-element.23.right), custom_call_target="tpu_custom_call" | custom-call | flops 1610612736 | bytes 9961472 | tf_op jit(solution)/shard_map/pallas_call | solution.py:153
  230.7 77.0 %all-reduce = (f32[2048]{0:T(1024)}, f32[2048]{0:T(1024)}) all-reduce(f32[2048]{0:T(1024)S(1)} %get-tuple-element.22, f32[2048]{0:T(1024)S(1)} %get-tuple-element.20), channel_id=1, replica_groups=mesh['dp'=16,'tensor'=8] {'dp'}, use_global_device_ids=true, to_apply=%region_10.12 | all-reduce | flops 4096 | bytes 32768 | tf_op jit(solution)/shard_map/psum | solution.py:257
  309.5 7.6 %reduce-scatter.3.cloned.1.call-done = bf16[128,2048]{1,0:T(8,128)(2,1)} async-done(((bf16[2048,2048]{1,0:T(8,128)(2,1)}), bf16[128,2048]{1,0:T(8,128)(2,1)}) %reduce-scatter.3.cloned.1.call-update) | async-done | bytes 524304 | tf_op jit(solution)/shard_map/reduce_scatter | solution.py:251
  317.1 2.1 convert_element_type.106
  (104 shorter events, 26.2 us)
Async XLA Ops:
  7.2 102.4 %all-gather.2.cloned.1.call-start = ((), (), s32[]{:S(2)}) async-start(), calls=%async_computation.4 | async-start | bytes 5570560 | tf_op jit(solution)/shard_map/all_gather | solution.py:212
  7.9 7.2 %copy-start.2 = (bf16[192,2048]{1,0:T(8,128)(2,1)S(1)}, bf16[192,2048]{1,0:T(8,128)(2,1)}, u32[]{:S(2)}) copy-start(bf16[192,2048]{1,0:T(8,128)(2,1)} %param.16) | copy-start | bytes 2359300
  7.9 299.7 %reduce-scatter.5.cloned.1.call-start = ((), (), s32[]{:S(2)}) async-start(), calls=%async_computation.6 | async-start | bytes 5570560 | tf_op jit(solution)/shard_map/reduce_scatter | solution.py:243
  15.1 1.9 copy-start
  15.1 4.2 %copy-start.5 = (s32[8,10]{1,0:T(8,128)S(1)}, s32[8,10]{1,0:T(8,128)}, u32[]{:S(2)}) copy-start(s32[8,10]{1,0:T(8,128)} %param.17) | copy-start | bytes 964
  15.1 4.2 %copy-start.6 = (s32[8,10]{1,0:T(8,128)S(1)}, s32[8,10]{1,0:T(8,128)}, u32[]{:S(2)}) copy-start(s32[8,10]{1,0:T(8,128)} %param.18) | copy-start | bytes 964
  15.1 4.2 %copy-start.8 = (s32[8]{0:T(128)S(1)}, s32[8]{0:T(128)}, u32[]{:S(2)}) copy-start(s32[8]{0:T(128)} %param.19) | copy-start | bytes 100
  17.0 11.8 %collective-permute-start.7 = (bf16[96,4096]{1,0:T(8,128)(2,1)S(1)}, bf16[96,4096]{1,0:T(8,128)(2,1)S(1)}, u32[]{:S(2)}, u32[]{:S(2)}) collective-permute-start(bf16[96,4096]{1,0:T(8,128)(2,1)S(1)} %get-tuple-element.27), channel_id=1, source_target_pairs={{0,7},{1,0},{2,1},{3,2},{4,3},{5,4},{6,5},{7,6},{8,15},{9,8},{10,9... | collective-permute-start | bytes 2359304 | tf_op jit(solution)/shard_map/ppermute | solution.py:65
  19.2 13.6 %collective-permute-start = (bf16[96,4096]{1,0:T(8,128)(2,1)S(1)}, bf16[96,4096]{1,0:T(8,128)(2,1)S(1)}, u32[]{:S(2)}, u32[]{:S(2)}) collective-permute-start(bf16[96,4096]{1,0:T(8,128)(2,1)S(1)} %get-tuple-element.40), channel_id=1, source_target_pairs={{0,1},{1,2},{2,3},{3,4},{4,5},{5,6},{6,7},{7,0},{8,9},{9,10},{10,1... | collective-permute-start | bytes 2359304 | tf_op jit(solution)/shard_map/ppermute | solution.py:64
  28.8 12.6 %collective-permute-start.8 = (bf16[96,4096]{1,0:T(8,128)(2,1)S(1)}, bf16[96,4096]{1,0:T(8,128)(2,1)S(1)}, u32[]{:S(2)}, u32[]{:S(2)}) collective-permute-start(bf16[96,4096]{1,0:T(8,128)(2,1)S(1)} %collective-permute-done.7), channel_id=1, source_target_pairs={{0,7},{1,0},{2,1},{3,2},{4,3},{5,4},{6,5},{7,6},{8,15},{9,8},{10,9... | collective-permute-start | bytes 2359304 | tf_op jit(solution)/shard_map/ppermute | solution.py:65
  32.8 12.7 %collective-permute-start.1 = (bf16[96,4096]{1,0:T(8,128)(2,1)S(1)}, bf16[96,4096]{1,0:T(8,128)(2,1)S(1)}, u32[]{:S(2)}, u32[]{:S(2)}) collective-permute-start(bf16[96,4096]{1,0:T(8,128)(2,1)S(1)} %collective-permute-done), channel_id=1, source_target_pairs={{0,1},{1,2},{2,3},{3,4},{4,5},{5,6},{6,7},{7,0},{8,9},{9,10},{10,1... | collective-permute-start | bytes 2359304 | tf_op jit(solution)/shard_map/ppermute | solution.py:64
  41.4 12.6 %collective-permute-start.9 = (bf16[96,4096]{1,0:T(8,128)(2,1)S(1)}, bf16[96,4096]{1,0:T(8,128)(2,1)S(1)}, u32[]{:S(2)}, u32[]{:S(2)}) collective-permute-start(bf16[96,4096]{1,0:T(8,128)(2,1)S(1)} %collective-permute-done.8), channel_id=1, source_target_pairs={{0,7},{1,0},{2,1},{3,2},{4,3},{5,4},{6,5},{7,6},{8,15},{9,8},{10,9... | collective-permute-start | bytes 2359304 | tf_op jit(solution)/shard_map/ppermute | solution.py:65
  45.5 12.6 %collective-permute-start.2 = (bf16[96,4096]{1,0:T(8,128)(2,1)S(1)}, bf16[96,4096]{1,0:T(8,128)(2,1)S(1)}, u32[]{:S(2)}, u32[]{:S(2)}) collective-permute-start(bf16[96,4096]{1,0:T(8,128)(2,1)S(1)} %collective-permute-done.1), channel_id=1, source_target_pairs={{0,1},{1,2},{2,3},{3,4},{4,5},{5,6},{6,7},{7,0},{8,9},{9,10},{10,1... | collective-permute-start | bytes 2359304 | tf_op jit(solution)/shard_map/ppermute | solution.py:64
  54.0 13.0 %collective-permute-start.10 = (bf16[96,4096]{1,0:T(8,128)(2,1)S(1)}, bf16[96,4096]{1,0:T(8,128)(2,1)S(1)}, u32[]{:S(2)}, u32[]{:S(2)}) collective-permute-start(bf16[96,4096]{1,0:T(8,128)(2,1)S(1)} %collective-permute-done.9), channel_id=1, source_target_pairs={{0,7},{1,0},{2,1},{3,2},{4,3},{5,4},{6,5},{7,6},{8,15},{9,8},{10,9... | collective-permute-start | bytes 2359304 | tf_op jit(solution)/shard_map/ppermute | solution.py:65
  58.1 12.6 %collective-permute-start.3 = (bf16[96,4096]{1,0:T(8,128)(2,1)S(1)}, bf16[96,4096]{1,0:T(8,128)(2,1)S(1)}, u32[]{:S(2)}, u32[]{:S(2)}) collective-permute-start(bf16[96,4096]{1,0:T(8,128)(2,1)S(1)} %collective-permute-done.2), channel_id=1, source_target_pairs={{0,1},{1,2},{2,3},{3,4},{4,5},{5,6},{6,7},{7,0},{8,9},{9,10},{10,1... | collective-permute-start | bytes 2359304 | tf_op jit(solution)/shard_map/ppermute | solution.py:64
  67.0 13.0 %collective-permute-start.11 = (bf16[96,4096]{1,0:T(8,128)(2,1)S(1)}, bf16[96,4096]{1,0:T(8,128)(2,1)S(1)}, u32[]{:S(2)}, u32[]{:S(2)}) collective-permute-start(bf16[96,4096]{1,0:T(8,128)(2,1)S(1)} %collective-permute-done.10), channel_id=1, source_target_pairs={{0,7},{1,0},{2,1},{3,2},{4,3},{5,4},{6,5},{7,6},{8,15},{9,8},{10,9... | collective-permute-start | bytes 2359304 | tf_op jit(solution)/shard_map/ppermute | solution.py:65
  70.8 12.6 %collective-permute-start.4 = (bf16[96,4096]{1,0:T(8,128)(2,1)S(1)}, bf16[96,4096]{1,0:T(8,128)(2,1)S(1)}, u32[]{:S(2)}, u32[]{:S(2)}) collective-permute-start(bf16[96,4096]{1,0:T(8,128)(2,1)S(1)} %collective-permute-done.3), channel_id=1, source_target_pairs={{0,1},{1,2},{2,3},{3,4},{4,5},{5,6},{6,7},{7,0},{8,9},{9,10},{10,1... | collective-permute-start | bytes 2359304 | tf_op jit(solution)/shard_map/ppermute | solution.py:64
  80.1 12.6 %collective-permute-start.12 = (bf16[96,4096]{1,0:T(8,128)(2,1)S(1)}, bf16[96,4096]{1,0:T(8,128)(2,1)S(1)}, u32[]{:S(2)}, u32[]{:S(2)}) collective-permute-start(bf16[96,4096]{1,0:T(8,128)(2,1)S(1)} %collective-permute-done.11), channel_id=1, source_target_pairs={{0,7},{1,0},{2,1},{3,2},{4,3},{5,4},{6,5},{7,6},{8,15},{9,8},{10,9... | collective-permute-start | bytes 2359304 | tf_op jit(solution)/shard_map/ppermute | solution.py:65
  83.4 12.6 %collective-permute-start.5 = (bf16[96,4096]{1,0:T(8,128)(2,1)S(1)}, bf16[96,4096]{1,0:T(8,128)(2,1)S(1)}, u32[]{:S(2)}, u32[]{:S(2)}) collective-permute-start(bf16[96,4096]{1,0:T(8,128)(2,1)S(1)} %collective-permute-done.4), channel_id=1, source_target_pairs={{0,1},{1,2},{2,3},{3,4},{4,5},{5,6},{6,7},{7,0},{8,9},{9,10},{10,1... | collective-permute-start | bytes 2359304 | tf_op jit(solution)/shard_map/ppermute | solution.py:64
  92.7 12.6 %collective-permute-start.13 = (bf16[96,4096]{1,0:T(8,128)(2,1)S(1)}, bf16[96,4096]{1,0:T(8,128)(2,1)S(1)}, u32[]{:S(2)}, u32[]{:S(2)}) collective-permute-start(bf16[96,4096]{1,0:T(8,128)(2,1)S(1)} %collective-permute-done.12), channel_id=1, source_target_pairs={{0,7},{1,0},{2,1},{3,2},{4,3},{5,4},{6,5},{7,6},{8,15},{9,8},{10,9... | collective-permute-start | bytes 2359304 | tf_op jit(solution)/shard_map/ppermute | solution.py:65
  96.0 12.6 %collective-permute-start.6 = (bf16[96,4096]{1,0:T(8,128)(2,1)S(1)}, bf16[96,4096]{1,0:T(8,128)(2,1)S(1)}, u32[]{:S(2)}, u32[]{:S(2)}) collective-permute-start(bf16[96,4096]{1,0:T(8,128)(2,1)S(1)} %collective-permute-done.5), channel_id=1, source_target_pairs={{0,1},{1,2},{2,3},{3,4},{4,5},{5,6},{6,7},{7,0},{8,9},{9,10},{10,1... | collective-permute-start | bytes 2359304 | tf_op jit(solution)/shard_map/ppermute | solution.py:64
  129.6 42.0 %all-to-all-start = ((bf16[8,384,512]{2,1,0:T(8,128)(2,1)}), bf16[8,384,512]{2,1,0:T(8,128)(2,1)S(1)}, u32[]{:S(2)}, u32[]{:S(2)}) async-start(bf16[8,384,512]{2,1,0:T(8,128)(2,1)} %bitcast.67), calls=%async_computation | async-start | bytes 6291456 | tf_op jit(solution)/shard_map/all_to_all | solution.py:222
  171.6 42.9 %all-to-all-start.1 = ((bf16[8,384,512]{2,1,0:T(8,128)(2,1)}), bf16[8,384,512]{2,1,0:T(8,128)(2,1)}, u32[]{:S(2)}, u32[]{:S(2)}) async-start(bf16[8,384,512]{2,1,0:T(8,128)(2,1)} %bitcast.66), calls=%async_computation.1 | async-start | bytes 6291456 | tf_op jit(solution)/shard_map/all_to_all | solution.py:233
  176.1 141.1 %reduce-scatter.3.cloned.1.call-start = ((), (), s32[]{:S(2)}) async-start(), calls=%async_computation.5 | async-start | bytes 8912896 | tf_op jit(solution)/shard_map/reduce_scatter | solution.py:251
  214.5 4.6 %copy-start.1 = (bf16[192,2048]{1,0:T(8,128)(2,1)S(1)}, bf16[192,2048]{1,0:T(8,128)(2,1)}, u32[]{:S(2)}) copy-start(bf16[192,2048]{1,0:T(8,128)(2,1)} %copy-done) | copy-start | bytes 2359300
  214.5 4.6 %copy-start.3 = (bf16[192,2048]{1,0:T(8,128)(2,1)S(1)}, bf16[192,2048]{1,0:T(8,128)(2,1)}, u32[]{:S(2)}) copy-start(bf16[192,2048]{1,0:T(8,128)(2,1)} %param.16) | copy-start | bytes 2359300
  214.5 4.6 %copy-start.4 = (f32[192,2048]{1,0:T(8,128)S(1)}, f32[192,2048]{1,0:T(8,128)}, u32[]{:S(2)}) copy-start(f32[192,2048]{1,0:T(8,128)} %get-tuple-element.44) | copy-start | bytes 4718596
  214.5 4.6 %copy-start.7 = (f32[2048]{0:T(1024)S(1)}, f32[2048]{0:T(1024)}, u32[]{:S(2)}) copy-start(f32[2048]{0:T(1024)} %param.15) | copy-start | bytes 24580
Sparse Core Ops, SparseCore 0:
  10.1 58.9 all-gather.1
  123.8 79.4 reduce-scatter.4
  230.8 86.2 reduce-scatter.2

commit v5 on v4

--- a/solution.py
+++ b/solution.py
@@ -1,3 +1,5 @@
+import functools
+
 import jax
 import jax.numpy as jnp
 from jax import lax
@@ -53,19 +55,68 @@
     summed = jnp.einsum("irb,il->rlb", flattened, onehot, preferred_element_type=jnp.float32)
     return summed.reshape(row_count, per_device * block_width)
 
+def ring_kernel(n, top, bottom, out_a, out_b, own_sem, send_sem, recv_sem):
+    me = lax.axis_index("tensor")
+    row = lax.axis_index("dp")
+    right = lax.rem(me + 1, n)
+    left = lax.rem(me + n - 1, n)
+    mesh_ids = pl.DeviceIdType.MESH
+    barrier = pltpu.get_barrier_semaphore()
+    for neighbour in (left, right):
+        pl.semaphore_signal(barrier, inc=1, device_id=(row, neighbour), device_id_type=mesh_ids)
+    pl.semaphore_wait(barrier, 2)
+    own_a = pltpu.make_async_copy(top, out_a.at[0], own_sem.at[0])
+    own_b = pltpu.make_async_copy(bottom, out_b.at[0], own_sem.at[1])
+    own_a.start()
+    own_b.start()
+
+    def link(out, side, step, target, src=None):
+        return pltpu.make_async_remote_copy(
+            src_ref=out.at[step] if src is None else src,
+            dst_ref=out.at[step],
+            send_sem=send_sem.at[side, step],
+            recv_sem=recv_sem.at[side, step],
+            device_id=(row, target),
+            device_id_type=mesh_ids,
+        )
+
+    sends = []
+    for step in range(1, n):
+        if step == 1:
+            src_a, src_b = top, bottom
+        else:
+            link(out_a, 0, step - 1, right).wait_recv()
+            link(out_b, 1, step - 1, left).wait_recv()
+            src_a, src_b = out_a.at[step - 1], out_b.at[step - 1]
+        copy_a = link(out_a, 0, step, right, src_a)
+        copy_b = link(out_b, 1, step, left, src_b)
+        copy_a.start()
+        copy_b.start()
+        sends += [copy_a, copy_b]
+    link(out_a, 0, n - 1, right).wait_recv()
+    link(out_b, 1, n - 1, left).wait_recv()
+    for copy in sends:
+        copy.wait_send()
+    own_a.wait()
+    own_b.wait()
+
 
 def ring_gather(x, axis, n):
     half = x.shape[0] // 2
-    right = [(i, (i + 1) % n) for i in range(n)]
-    left = [(i, (i - 1) % n) for i in range(n)]
-    cur_a, cur_b = x[:half], x[half:]
-    outs_a, outs_b = [cur_a], [cur_b]
-    for _ in range(1, n):
-        cur_a = lax.ppermute(cur_a, axis, right)
-        cur_b = lax.ppermute(cur_b, axis, left)
-        outs_a.append(cur_a)
-        outs_b.append(cur_b)
-    return jnp.stack(outs_a), jnp.stack(outs_b)
+    shape = jax.ShapeDtypeStruct((n, half, x.shape[1]), x.dtype)
+    anywhere = pl.BlockSpec(memory_space=pl.ANY)
+    return pl.pallas_call(
+        functools.partial(ring_kernel, n),
+        out_shape=[shape, shape],
+        in_specs=[anywhere, anywhere],
+        out_specs=[anywhere, anywhere],
+        scratch_shapes=[
+            pltpu.SemaphoreType.DMA((2,)),
+            pltpu.SemaphoreType.DMA((2, n)),
+            pltpu.SemaphoreType.DMA((2, n)),
+        ],
+        compiler_params=pltpu.CompilerParams(collective_id=0, has_side_effects=True),
+    )(x[:half], x[half:])
 
 
 def take_blocks(stack_a, stack_b, owner, local, me, n):

time: 327 us -> 320 us (0.979)
  Pallas kernels: 23.4 us -> 106 us
  waiting for transfers between devices: 128 us -> 73 us
  starting transfers between devices: 30.2 us -> 8.38 us
  local copies, waits for them, and re-layouts: 22.3 us -> 10.2 us
    pallas_call x0 -> x1, Pallas kernels: none -> 82.4 us  [ring_gather(): pl.pallas_call(functools.partial(ring_kernel, n), out_shape=[shape, shape...]
    ppermute x14 -> x0, waiting for transfers between devices: 54.7 us -> none  [the longest x7 51 us: ring_gather(): cur_b = lax.ppermute(cur_b, axis, left)]
    ppermute x14 -> x0, starting transfers between devices: 21.8 us -> none  [the longest x7 21.8 us: ring_gather(): cur_b = lax.ppermute(cur_b, axis, left)]
    unnamed x32 -> x20, local copies, waits for them, and re-layouts: 12.7 us -> 2.49 us
  transfers between devices with their start and end apart: 19 -> 5, of which waited for: 15 -> 3; matrix products, arithmetic and copies ran while one was open for 16% -> 12% of each run, Pallas kernels for 3% -> 29%
where the time goes in v5:
time: 320 us; the launch traced here: 319 us
  Pallas kernels  106 us (33%)
  blocking collectives  76.7 us (24%)
  waiting for transfers between devices  73 us (23%)
  other arithmetic  17.8 us (6%)
  between operations  14 us (4%)
  matrix products  12.9 us (4%)
  local copies, waits for them, and re-layouts  10.2 us (3%)
  starting transfers between devices  8.38 us (3%)
    pallas_call x1, Pallas kernels, ring_gather(): pl.pallas_call(functools.partial(ring_kernel, n), out_shape=[shape, shape...  82.4 us
    psum x1, blocking collectives, on_device(): lax.psum((jnp.sum(grad_pre, axis=0), jnp.sum(grad_mixed, axis=0)), 'dp')  76.7 us
    all_to_all x1, waiting for transfers between devices, on_device(): lax.all_to_all(pack_parts(back_parts, chosen_in, filled_in), 'tensor', sp...  34.8 us
    all_to_all x1, waiting for transfers between devices, on_device(): lax.all_to_all(pack_parts(parts, chosen_out, filled_out), 'tensor', split...  30 us
    pallas_call x1, Pallas kernels, slot_products(): pl.pallas_call(slot_kernel, grid_spec=grid_spec, out_shape=[jax.ShapeDtyp...  14.1 us
    pallas_call x1, Pallas kernels, group_outer(): pl.pallas_call(outer_kernel, grid=(m // tile_m, n // tile_n), in_specs=[p...  9.38 us
    reduce_scatter x1, waiting for transfers between devices, on_device(): lax.psum_scatter(group_outer(taken, grad_pre_low), 'dp', scatter_dimensio...  7.49 us
    dot_general x1, matrix products, on_device(): jnp.dot(dense, bottom_weight, preferred_element_type=jnp.float32)  7.13 us
  transfers between devices with their start and end apart: 5, of which 3 were waited for; matrix products, arithmetic and copies ran while one was open for 12% of the time, Pallas kernels for 29%

profile of v5, /device:TPU:0, one launch (start us, length us, event | category | flops | bytes accessed | tf_op | source)
XLA Modules:
  0.0 318.8 jit_solution(16819065974442716097)
XLA Ops:
  7.2 0.7 all-gather.2.cloned.1.call-update
  8.0 7.1 %fusion.8 = (f32[2048]{0:T(1024)S(1)}, bf16[192,2048]{1,0:T(8,128)(2,1)S(1)}, f32[192,2048]{1,0:T(8,128)}) fusion(bf16[192,2048]{1,0:T(8,128)(2,1)} %param.16, f32[2048]{0:T(1024)} %param.13, bf16[192,2048]{1,0:T(8,128)(2,1)} %left.1, bf16[2048,2048]{1,0:T(8,128)(2,1)} %param.12), kind=kOutput, calls=%fused_computation.21 | convolution fusion | flops 1614542848 | bytes 12337152 | tf_op jit(solution)/shard_map/dot_general | solution.py:236
  15.1 0.3 fusion.9
  15.4 1.3 pad_maximum_fusion
  16.7 82.4 %shard_map.128 = (bf16[8,96,4096]{2,1,0:T(8,128)(2,1)}, bf16[8,96,4096]{2,1,0:T(8,128)(2,1)}) custom-call(bf16[96,4096]{1,0:T(8,128)(2,1)} %get-tuple-element.40.top, bf16[96,4096]{1,0:T(8,128)(2,1)} %get-tuple-element.39.bottom), custom_call_target="tpu_custom_call" | custom-call | tf_op jit(solution)/shard_map/pallas_call | solution.py:108
  99.1 0.5 fusion.30
  99.7 0.5 fusion.20
  100.2 0.5 and_select_fusion
  100.8 0.6 and_select_fusion.1.sa_o
  101.3 0.5 and_select_fusion.3.sa_i
  101.9 14.1 %shard_map.129 = (bf16[10,192,512]{2,1,0:T(8,128)(2,1)}, bf16[10,192,512]{2,1,0:T(8,128)(2,1)}, bf16[10,512,512]{2,1,0:T(8,128)(2,1)}) custom-call(s32[10]{0:T(128)} %and_select_fusion.3.sa_i, s32[10]{0:T(128)} %get-tuple-element.45.sb_i, s32[10]{0:T(128)} %get-tuple-element.51.bi, s32[10]{0:T(128)} %and_select_fusion.1.sa_o, s32[10]{0:T(128)} %get-tuple-element.32.sb_o, ...), custom_call_target="tpu_custom_call" | custom-call | flops 3019898880 | bytes 18350080 | tf_op jit(solution)/shard_map/pallas_call | solution.py:179
  116.1 0.5 convert_reduce_fusion
  117.6 2.3 gather_fusion
  119.9 2.0 select_multiply_fusion.1
  121.9 3.6 %all-to-all-start = ((bf16[8,384,512]{2,1,0:T(8,128)(2,1)}), bf16[8,384,512]{2,1,0:T(8,128)(2,1)S(1)}, u32[]{:S(2)}, u32[]{:S(2)}) async-start(bf16[8,384,512]{2,1,0:T(8,128)(2,1)} %bitcast.35), calls=%async_computation | async-start | bytes 6291456 | tf_op jit(solution)/shard_map/all_to_all | solution.py:273
  126.0 4.0 %gather_fusion.1 = bf16[16,192,512]{2,1,0:T(8,128)(2,1)} fusion(bf16[10,192,512]{2,1,0:T(8,128)(2,1)} %get-tuple-element.14, s32[1024]{0:T(1024)S(1)} %pad_clamp_fusion), kind=kCustom, calls=%fused_computation.1.clone | custom fusion | bytes 6291520 | tf_op jit(solution)/shard_map/jit(_take)/gather | solution.py:34
  130.0 4.0 %select_multiply_fusion = bf16[16,192,512]{2,1,0:T(8,128)(2,1)} fusion(bf16[16,192,512]{2,1,0:T(8,128)(2,1)} %gather_fusion.1, pred[16]{0:T(512)(128)(4,1)S(1)} %compare_and_fusion.2, bf16[16]{0:T(256)(128)(2,1)S(1)} %reshape.247), kind=kLoop, calls=%fused_computation.6 | loop fusion | flops 3145728 | bytes 6291504 | tf_op jit(solution)/shard_map/mul | solution.py:34
  133.9 30.0 %all-to-all-done = bf16[8,384,512]{2,1,0:T(8,128)(2,1)S(1)} async-done(((bf16[8,384,512]{2,1,0:T(8,128)(2,1)}), bf16[8,384,512]{2,1,0:T(8,128)(2,1)S(1)}, u32[]{:S(2)}, u32[]{:S(2)}) %all-to-all-start) | async-done | bytes 3145760 | tf_op jit(solution)/shard_map/all_to_all | solution.py:273
  163.9 4.4 %all-to-all-start.1 = ((bf16[8,384,512]{2,1,0:T(8,128)(2,1)}), bf16[8,384,512]{2,1,0:T(8,128)(2,1)}, u32[]{:S(2)}, u32[]{:S(2)}) async-start(bf16[8,384,512]{2,1,0:T(8,128)(2,1)} %bitcast.34), calls=%async_computation.1 | async-start | bytes 6291456 | tf_op jit(solution)/shard_map/all_to_all | solution.py:284
  169.4 1.9 fusion.2
  171.4 0.6 copy.52
  172.0 34.8 %all-to-all-done.1 = bf16[8,384,512]{2,1,0:T(8,128)(2,1)} async-done(((bf16[8,384,512]{2,1,0:T(8,128)(2,1)}), bf16[8,384,512]{2,1,0:T(8,128)(2,1)}, u32[]{:S(2)}, u32[]{:S(2)}) %all-to-all-start.1) | async-done | bytes 3145760 | tf_op jit(solution)/shard_map/all_to_all | solution.py:284
  206.8 3.8 %fusion = f32[4,192,512]{2,0,1:T(4,128)S(1)} fusion(bf16[16,4,1]{1,0,2:T(8,128)(2,1)S(1)} %bitcast.40, bf16[16,192,512]{2,1,0:T(8,128)(2,1)} %bitcast.13), kind=kOutput, calls=%fused_computation.2 | convolution fusion | flops 12582912 | bytes 4718720 | tf_op jit(solution)/shard_map/irb,il->rlb/dot_general | solution.py:55
  210.7 0.6 copy.53
  211.3 0.5 copy-done.1
  212.0 0.5 copy-done.4
  212.5 2.1 fusion.28
  214.6 9.4 %shard_map.130 = bf16[2048,2048]{1,0:T(8,128)(2,1)} custom-call(bf16[192,2048]{1,0:T(8,128)(2,1)} %left.1, bf16[192,2048]{1,0:T(8,128)(2,1)} %get-tuple-element.27.right), custom_call_target="tpu_custom_call" | custom-call | flops 1610612736 | bytes 9961472 | tf_op jit(solution)/shard_map/pallas_call | solution.py:204
  224.0 76.7 %all-reduce = (f32[2048]{0:T(1024)}, f32[2048]{0:T(1024)}) all-reduce(f32[2048]{0:T(1024)S(1)} %get-tuple-element.26, f32[2048]{0:T(1024)S(1)} %get-tuple-element.24), channel_id=1, replica_groups=mesh['dp'=16,'tensor'=8] {'dp'}, use_global_device_ids=true, to_apply=%region_10.12 | all-reduce | flops 4096 | bytes 32768 | tf_op jit(solution)/shard_map/psum | solution.py:308
  300.7 1.9 convert_element_type.107
  302.6 7.5 %reduce-scatter.3.cloned.1.call-done = bf16[128,2048]{1,0:T(8,128)(2,1)} async-done(((bf16[2048,2048]{1,0:T(8,128)(2,1)}), bf16[128,2048]{1,0:T(8,128)(2,1)}) %reduce-scatter.3.cloned.1.call-update) | async-done | bytes 524304 | tf_op jit(solution)/shard_map/reduce_scatter | solution.py:302
  310.1 2.1 convert_element_type.106
  (63 shorter events, 3.0 us)
Async XLA Ops:
  7.2 94.7 %all-gather.2.cloned.1.call-start = ((), (), s32[]{:S(2)}) async-start(), calls=%async_computation.4 | async-start | bytes 5570560 | tf_op jit(solution)/shard_map/all_gather | solution.py:263
  7.9 292.8 %reduce-scatter.5.cloned.1.call-start = ((), (), s32[]{:S(2)}) async-start(), calls=%async_computation.6 | async-start | bytes 5570560 | tf_op jit(solution)/shard_map/reduce_scatter | solution.py:294
  8.0 7.2 %copy-start.2 = (bf16[192,2048]{1,0:T(8,128)(2,1)S(1)}, bf16[192,2048]{1,0:T(8,128)(2,1)}, u32[]{:S(2)}) copy-start(bf16[192,2048]{1,0:T(8,128)(2,1)} %param.16) | copy-start | bytes 2359300
  15.1 1.5 copy-start
  16.6 82.4 %copy-start.5 = (s32[8,10]{1,0:T(8,128)S(1)}, s32[8,10]{1,0:T(8,128)}, u32[]{:S(2)}) copy-start(s32[8,10]{1,0:T(8,128)} %param.17) | copy-start | bytes 964
  16.6 82.4 %copy-start.6 = (s32[8,10]{1,0:T(8,128)S(1)}, s32[8,10]{1,0:T(8,128)}, u32[]{:S(2)}) copy-start(s32[8,10]{1,0:T(8,128)} %param.18) | copy-start | bytes 964
  16.6 82.4 %copy-start.8 = (s32[8]{0:T(128)S(1)}, s32[8]{0:T(128)}, u32[]{:S(2)}) copy-start(s32[8]{0:T(128)} %param.19) | copy-start | bytes 100
  121.9 42.0 %all-to-all-start = ((bf16[8,384,512]{2,1,0:T(8,128)(2,1)}), bf16[8,384,512]{2,1,0:T(8,128)(2,1)S(1)}, u32[]{:S(2)}, u32[]{:S(2)}) async-start(bf16[8,384,512]{2,1,0:T(8,128)(2,1)} %bitcast.35), calls=%async_computation | async-start | bytes 6291456 | tf_op jit(solution)/shard_map/all_to_all | solution.py:273
  163.9 42.9 %all-to-all-start.1 = ((bf16[8,384,512]{2,1,0:T(8,128)(2,1)}), bf16[8,384,512]{2,1,0:T(8,128)(2,1)}, u32[]{:S(2)}, u32[]{:S(2)}) async-start(bf16[8,384,512]{2,1,0:T(8,128)(2,1)} %bitcast.34), calls=%async_computation.1 | async-start | bytes 6291456 | tf_op jit(solution)/shard_map/all_to_all | solution.py:284
  168.4 141.8 %reduce-scatter.3.cloned.1.call-start = ((), (), s32[]{:S(2)}) async-start(), calls=%async_computation.5 | async-start | bytes 8912896 | tf_op jit(solution)/shard_map/reduce_scatter | solution.py:302
  206.8 4.5 %copy-start.7 = (f32[2048]{0:T(1024)S(1)}, f32[2048]{0:T(1024)}, u32[]{:S(2)}) copy-start(f32[2048]{0:T(1024)} %param.15) | copy-start | bytes 24580
  210.6 1.1 copy-start.1
  210.6 1.4 copy-start.3
  210.7 1.9 copy-start.4
Sparse Core Ops, SparseCore 0:
  10.1 58.9 all-gather.1
  116.1 81.2 reduce-scatter.4
  224.2 85.9 reduce-scatter.2

commit v6 on v5

--- a/solution.py
+++ b/solution.py
@@ -9,6 +9,7 @@
 
 BLK = 512
 SLOTS = 10
+RING_CHUNKS = 4
 
 
 def slot_ranks(owner, alive):
@@ -70,31 +71,39 @@
     own_a.start()
     own_b.start()
 
-    def link(out, side, step, target, src=None):
+    chunks = send_sem.shape[2]
+    rows = top.shape[0] // chunks
+
+    def piece(ref, c):
+        return ref.at[pl.ds(c * rows, rows)]
+
+    def link(out, side, step, c, target, src=None):
         return pltpu.make_async_remote_copy(
-            src_ref=out.at[step] if src is None else src,
-            dst_ref=out.at[step],
-            send_sem=send_sem.at[side, step],
-            recv_sem=recv_sem.at[side, step],
+            src_ref=piece(out.at[step] if src is None else src, c),
+            dst_ref=piece(out.at[step], c),
+            send_sem=send_sem.at[side, step, c],
+            recv_sem=recv_sem.at[side, step, c],
             device_id=(row, target),
             device_id_type=mesh_ids,
         )
 
     sends = []
     for step in range(1, n):
-        if step == 1:
-            src_a, src_b = top, bottom
-        else:
-            link(out_a, 0, step - 1, right).wait_recv()
-            link(out_b, 1, step - 1, left).wait_recv()
-            src_a, src_b = out_a.at[step - 1], out_b.at[step - 1]
-        copy_a = link(out_a, 0, step, right, src_a)
-        copy_b = link(out_b, 1, step, left, src_b)
-        copy_a.start()
-        copy_b.start()
-        sends += [copy_a, copy_b]
-    link(out_a, 0, n - 1, right).wait_recv()
-    link(out_b, 1, n - 1, left).wait_recv()
+        for c in range(chunks):
+            if step == 1:
+                src_a, src_b = top, bottom
+            else:
+                link(out_a, 0, step - 1, c, right).wait_recv()
+                link(out_b, 1, step - 1, c, left).wait_recv()
+                src_a, src_b = out_a.at[step - 1], out_b.at[step - 1]
+            copy_a = link(out_a, 0, step, c, right, src_a)
+            copy_b = link(out_b, 1, step, c, left, src_b)
+            copy_a.start()
+            copy_b.start()
+            sends += [copy_a, copy_b]
+    for c in range(chunks):
+        link(out_a, 0, n - 1, c, right).wait_recv()
+        link(out_b, 1, n - 1, c, left).wait_recv()
     for copy in sends:
         copy.wait_send()
     own_a.wait()
@@ -112,8 +121,8 @@
         out_specs=[anywhere, anywhere],
         scratch_shapes=[
             pltpu.SemaphoreType.DMA((2,)),
-            pltpu.SemaphoreType.DMA((2, n)),
-            pltpu.SemaphoreType.DMA((2, n)),
+            pltpu.SemaphoreType.DMA((2, n, RING_CHUNKS)),
+            pltpu.SemaphoreType.DMA((2, n, RING_CHUNKS)),
         ],
         compiler_params=pltpu.CompilerParams(collective_id=0, has_side_effects=True),
     )(x[:half], x[half:])

time: 320 us -> 302 us (0.944)
  Pallas kernels: 106 us -> 88.2 us
    pallas_call x1, Pallas kernels: 82.4 us -> 64.8 us  [ring_gather(): pl.pallas_call(functools.partial(ring_kernel, n), out_shape=[shape, shape...]
  transfers between devices with their start and end apart: 5 -> 5, of which waited for: 3 -> 3; matrix products, arithmetic and copies ran while one was open for 12% -> 13% of each run, Pallas kernels for 29% -> 25%
where the time goes in v6:
time: 302 us; the launch traced here: 301 us
  Pallas kernels  88.2 us (29%)
  blocking collectives  76.5 us (25%)
  waiting for transfers between devices  73 us (24%)
  other arithmetic  17.8 us (6%)
  between operations  14 us (5%)
  matrix products  12.9 us (4%)
  local copies, waits for them, and re-layouts  10.4 us (3%)
  starting transfers between devices  8.38 us (3%)
    psum x1, blocking collectives, on_device(): lax.psum((jnp.sum(grad_pre, axis=0), jnp.sum(grad_mixed, axis=0)), 'dp')  76.5 us
    pallas_call x1, Pallas kernels, ring_gather(): pl.pallas_call(functools.partial(ring_kernel, n), out_shape=[shape, shape...  64.8 us
    all_to_all x1, waiting for transfers between devices, on_device(): lax.all_to_all(pack_parts(back_parts, chosen_in, filled_in), 'tensor', sp...  34.8 us
    all_to_all x1, waiting for transfers between devices, on_device(): lax.all_to_all(pack_parts(parts, chosen_out, filled_out), 'tensor', split...  29.8 us
    pallas_call x1, Pallas kernels, slot_products(): pl.pallas_call(slot_kernel, grid_spec=grid_spec, out_shape=[jax.ShapeDtyp...  14.1 us
    pallas_call x1, Pallas kernels, group_outer(): pl.pallas_call(outer_kernel, grid=(m // tile_m, n // tile_n), in_specs=[p...  9.38 us
    reduce_scatter x1, waiting for transfers between devices, on_device(): lax.psum_scatter(group_outer(taken, grad_pre_low), 'dp', scatter_dimensio...  7.68 us
    dot_general x1, matrix products, on_device(): jnp.dot(dense, bottom_weight, preferred_element_type=jnp.float32)  7.13 us
  transfers between devices with their start and end apart: 5, of which 3 were waited for; matrix products, arithmetic and copies ran while one was open for 13% of the time, Pallas kernels for 25%

profile of v6, /device:TPU:0, one launch (start us, length us, event | category | flops | bytes accessed | tf_op | source)
XLA Modules:
  0.0 301.2 jit_solution(15478271869368383847)
XLA Ops:
  7.2 0.7 all-gather.2.cloned.1.call-update
  8.0 7.1 %fusion.8 = (f32[2048]{0:T(1024)S(1)}, bf16[192,2048]{1,0:T(8,128)(2,1)S(1)}, f32[192,2048]{1,0:T(8,128)}) fusion(bf16[192,2048]{1,0:T(8,128)(2,1)} %param.16, f32[2048]{0:T(1024)} %param.13, bf16[192,2048]{1,0:T(8,128)(2,1)} %left.1, bf16[2048,2048]{1,0:T(8,128)(2,1)} %param.12), kind=kOutput, calls=%fused_computation.21 | convolution fusion | flops 1614542848 | bytes 12337152 | tf_op jit(solution)/shard_map/dot_general | solution.py:245
  15.1 0.3 fusion.9
  15.4 1.3 pad_maximum_fusion
  16.7 64.8 %shard_map.128 = (bf16[8,96,4096]{2,1,0:T(8,128)(2,1)}, bf16[8,96,4096]{2,1,0:T(8,128)(2,1)}) custom-call(bf16[96,4096]{1,0:T(8,128)(2,1)} %get-tuple-element.40.top, bf16[96,4096]{1,0:T(8,128)(2,1)} %get-tuple-element.39.bottom), custom_call_target="tpu_custom_call" | custom-call | tf_op jit(solution)/shard_map/pallas_call | solution.py:117
  81.6 0.5 fusion.30
  82.1 0.5 fusion.20
  82.6 0.5 and_select_fusion
  83.2 0.6 and_select_fusion.1.sa_o
  83.8 0.5 and_select_fusion.3.sa_i
  84.3 14.1 %shard_map.129 = (bf16[10,192,512]{2,1,0:T(8,128)(2,1)}, bf16[10,192,512]{2,1,0:T(8,128)(2,1)}, bf16[10,512,512]{2,1,0:T(8,128)(2,1)}) custom-call(s32[10]{0:T(128)} %and_select_fusion.3.sa_i, s32[10]{0:T(128)} %get-tuple-element.45.sb_i, s32[10]{0:T(128)} %get-tuple-element.51.bi, s32[10]{0:T(128)} %and_select_fusion.1.sa_o, s32[10]{0:T(128)} %get-tuple-element.32.sb_o, ...), custom_call_target="tpu_custom_call" | custom-call | flops 3019898880 | bytes 18350080 | tf_op jit(solution)/shard_map/pallas_call | solution.py:188
  98.6 0.5 convert_reduce_fusion
  100.0 2.3 gather_fusion
  102.3 2.0 select_multiply_fusion.1
  104.3 3.6 %all-to-all-start = ((bf16[8,384,512]{2,1,0:T(8,128)(2,1)}), bf16[8,384,512]{2,1,0:T(8,128)(2,1)S(1)}, u32[]{:S(2)}, u32[]{:S(2)}) async-start(bf16[8,384,512]{2,1,0:T(8,128)(2,1)} %bitcast.35), calls=%async_computation | async-start | bytes 6291456 | tf_op jit(solution)/shard_map/all_to_all | solution.py:282
  108.4 4.2 %gather_fusion.1 = bf16[16,192,512]{2,1,0:T(8,128)(2,1)} fusion(bf16[10,192,512]{2,1,0:T(8,128)(2,1)} %get-tuple-element.14, s32[1024]{0:T(1024)S(1)} %pad_clamp_fusion), kind=kCustom, calls=%fused_computation.1.clone | custom fusion | bytes 6291520 | tf_op jit(solution)/shard_map/jit(_take)/gather | solution.py:35
  112.5 4.0 %select_multiply_fusion = bf16[16,192,512]{2,1,0:T(8,128)(2,1)} fusion(bf16[16,192,512]{2,1,0:T(8,128)(2,1)} %gather_fusion.1, pred[16]{0:T(512)(128)(4,1)S(1)} %compare_and_fusion.2, bf16[16]{0:T(256)(128)(2,1)S(1)} %reshape.247), kind=kLoop, calls=%fused_computation.6 | loop fusion | flops 3145728 | bytes 6291504 | tf_op jit(solution)/shard_map/mul | solution.py:35
  116.5 29.8 %all-to-all-done = bf16[8,384,512]{2,1,0:T(8,128)(2,1)S(1)} async-done(((bf16[8,384,512]{2,1,0:T(8,128)(2,1)}), bf16[8,384,512]{2,1,0:T(8,128)(2,1)S(1)}, u32[]{:S(2)}, u32[]{:S(2)}) %all-to-all-start) | async-done | bytes 3145760 | tf_op jit(solution)/shard_map/all_to_all | solution.py:282
  146.3 4.4 %all-to-all-start.1 = ((bf16[8,384,512]{2,1,0:T(8,128)(2,1)}), bf16[8,384,512]{2,1,0:T(8,128)(2,1)}, u32[]{:S(2)}, u32[]{:S(2)}) async-start(bf16[8,384,512]{2,1,0:T(8,128)(2,1)} %bitcast.34), calls=%async_computation.1 | async-start | bytes 6291456 | tf_op jit(solution)/shard_map/all_to_all | solution.py:293
  151.9 1.9 fusion.2
  153.8 0.6 copy.52
  154.4 34.8 %all-to-all-done.1 = bf16[8,384,512]{2,1,0:T(8,128)(2,1)} async-done(((bf16[8,384,512]{2,1,0:T(8,128)(2,1)}), bf16[8,384,512]{2,1,0:T(8,128)(2,1)}, u32[]{:S(2)}, u32[]{:S(2)}) %all-to-all-start.1) | async-done | bytes 3145760 | tf_op jit(solution)/shard_map/all_to_all | solution.py:293
  189.2 3.8 %fusion = f32[4,192,512]{2,0,1:T(4,128)S(1)} fusion(bf16[16,4,1]{1,0,2:T(8,128)(2,1)S(1)} %bitcast.40, bf16[16,192,512]{2,1,0:T(8,128)(2,1)} %bitcast.13), kind=kOutput, calls=%fused_computation.2 | convolution fusion | flops 12582912 | bytes 4718720 | tf_op jit(solution)/shard_map/irb,il->rlb/dot_general | solution.py:56
  193.1 0.6 copy.53
  193.7 0.5 copy-done.1
  194.4 0.5 copy-done.4
  194.9 2.1 fusion.28
  197.1 9.4 %shard_map.130 = bf16[2048,2048]{1,0:T(8,128)(2,1)} custom-call(bf16[192,2048]{1,0:T(8,128)(2,1)} %left.1, bf16[192,2048]{1,0:T(8,128)(2,1)} %get-tuple-element.27.right), custom_call_target="tpu_custom_call" | custom-call | flops 1610612736 | bytes 9961472 | tf_op jit(solution)/shard_map/pallas_call | solution.py:213
  206.5 76.5 %all-reduce = (f32[2048]{0:T(1024)}, f32[2048]{0:T(1024)}) all-reduce(f32[2048]{0:T(1024)S(1)} %get-tuple-element.26, f32[2048]{0:T(1024)S(1)} %get-tuple-element.24), channel_id=1, replica_groups=mesh['dp'=16,'tensor'=8] {'dp'}, use_global_device_ids=true, to_apply=%region_10.12 | all-reduce | flops 4096 | bytes 32768 | tf_op jit(solution)/shard_map/psum | solution.py:317
  282.9 1.9 convert_element_type.107
  284.8 7.7 %reduce-scatter.3.cloned.1.call-done = bf16[128,2048]{1,0:T(8,128)(2,1)} async-done(((bf16[2048,2048]{1,0:T(8,128)(2,1)}), bf16[128,2048]{1,0:T(8,128)(2,1)}) %reduce-scatter.3.cloned.1.call-update) | async-done | bytes 524304 | tf_op jit(solution)/shard_map/reduce_scatter | solution.py:311
  292.5 2.1 convert_element_type.106
  (63 shorter events, 3.0 us)
Async XLA Ops:
  7.2 77.1 %all-gather.2.cloned.1.call-start = ((), (), s32[]{:S(2)}) async-start(), calls=%async_computation.4 | async-start | bytes 5570560 | tf_op jit(solution)/shard_map/all_gather | solution.py:272
  7.9 275.0 %reduce-scatter.5.cloned.1.call-start = ((), (), s32[]{:S(2)}) async-start(), calls=%async_computation.6 | async-start | bytes 5570560 | tf_op jit(solution)/shard_map/reduce_scatter | solution.py:303
  8.0 7.2 %copy-start.2 = (bf16[192,2048]{1,0:T(8,128)(2,1)S(1)}, bf16[192,2048]{1,0:T(8,128)(2,1)}, u32[]{:S(2)}) copy-start(bf16[192,2048]{1,0:T(8,128)(2,1)} %param.16) | copy-start | bytes 2359300
  15.1 1.5 copy-start
  16.6 64.8 %copy-start.5 = (s32[8,10]{1,0:T(8,128)S(1)}, s32[8,10]{1,0:T(8,128)}, u32[]{:S(2)}) copy-start(s32[8,10]{1,0:T(8,128)} %param.17) | copy-start | bytes 964
  16.6 64.8 %copy-start.6 = (s32[8,10]{1,0:T(8,128)S(1)}, s32[8,10]{1,0:T(8,128)}, u32[]{:S(2)}) copy-start(s32[8,10]{1,0:T(8,128)} %param.18) | copy-start | bytes 964
  16.6 64.8 %copy-start.8 = (s32[8]{0:T(128)S(1)}, s32[8]{0:T(128)}, u32[]{:S(2)}) copy-start(s32[8]{0:T(128)} %param.19) | copy-start | bytes 100
  104.3 42.0 %all-to-all-start = ((bf16[8,384,512]{2,1,0:T(8,128)(2,1)}), bf16[8,384,512]{2,1,0:T(8,128)(2,1)S(1)}, u32[]{:S(2)}, u32[]{:S(2)}) async-start(bf16[8,384,512]{2,1,0:T(8,128)(2,1)} %bitcast.35), calls=%async_computation | async-start | bytes 6291456 | tf_op jit(solution)/shard_map/all_to_all | solution.py:282
  146.3 42.9 %all-to-all-start.1 = ((bf16[8,384,512]{2,1,0:T(8,128)(2,1)}), bf16[8,384,512]{2,1,0:T(8,128)(2,1)}, u32[]{:S(2)}, u32[]{:S(2)}) async-start(bf16[8,384,512]{2,1,0:T(8,128)(2,1)} %bitcast.34), calls=%async_computation.1 | async-start | bytes 6291456 | tf_op jit(solution)/shard_map/all_to_all | solution.py:293
  150.8 141.8 %reduce-scatter.3.cloned.1.call-start = ((), (), s32[]{:S(2)}) async-start(), calls=%async_computation.5 | async-start | bytes 8912896 | tf_op jit(solution)/shard_map/reduce_scatter | solution.py:311
  189.2 4.5 %copy-start.7 = (f32[2048]{0:T(1024)S(1)}, f32[2048]{0:T(1024)}, u32[]{:S(2)}) copy-start(f32[2048]{0:T(1024)} %param.15) | copy-start | bytes 24580
  193.0 1.1 copy-start.1
  193.0 1.4 copy-start.3
  193.1 1.9 copy-start.4
Sparse Core Ops, SparseCore 0:
  10.1 58.9 all-gather.1
  98.5 80.8 reduce-scatter.4
  206.6 85.9 reduce-scatter.2

commit v7 on v6

--- a/solution.py
+++ b/solution.py
@@ -126,6 +126,70 @@
         ],
         compiler_params=pltpu.CompilerParams(collective_id=0, has_side_effects=True),
     )(x[:half], x[half:])
+
+
+def exchange_kernel(n, first, second, out_first, out_second, own_sem, send_sem, recv_sem):
+    me = lax.axis_index("tensor")
+    row = lax.axis_index("dp")
+    mesh_ids = pl.DeviceIdType.MESH
+    barrier = pltpu.get_barrier_semaphore()
+    for offset in range(1, n):
+        peer = lax.rem(me + offset, n)
+        pl.semaphore_signal(barrier, inc=1, device_id=(row, peer), device_id_type=mesh_ids)
+    pl.semaphore_wait(barrier, n - 1)
+    pairs = ((first, out_first), (second, out_second))
+    own = [
+        pltpu.make_async_copy(src.at[me], dst.at[me], own_sem.at[side])
+        for side, (src, dst) in enumerate(pairs)
+    ]
+    for copy in own:
+        copy.start()
+
+    def link(side, peer, slot):
+        src, dst = pairs[side]
+        return pltpu.make_async_remote_copy(
+            src_ref=src.at[peer],
+            dst_ref=dst.at[slot],
+            send_sem=send_sem.at[side, peer],
+            recv_sem=recv_sem.at[side, slot],
+            device_id=(row, peer),
+            device_id_type=mesh_ids,
+        )
+
+    sends = []
+    for offset in (1, n - 1, 2, n - 2, 3, n - 3, 4)[: n - 1]:
+        peer = lax.rem(me + offset, n)
+        for side in range(2):
+            copy = link(side, peer, me)
+            copy.start()
+            sends.append(copy)
+    for offset in range(1, n):
+        source = lax.rem(me + offset, n)
+        for side in range(2):
+            link(side, source, source).wait_recv()
+    for copy in sends:
+        copy.wait_send()
+    for copy in own:
+        copy.wait()
+
+
+def exchange(first, second, n):
+    anywhere = pl.BlockSpec(memory_space=pl.ANY)
+    return pl.pallas_call(
+        functools.partial(exchange_kernel, n),
+        out_shape=[
+            jax.ShapeDtypeStruct(first.shape, first.dtype),
+            jax.ShapeDtypeStruct(second.shape, second.dtype),
+        ],
+        in_specs=[anywhere, anywhere],
+        out_specs=[anywhere, anywhere],
+        scratch_shapes=[
+            pltpu.SemaphoreType.DMA((2,)),
+            pltpu.SemaphoreType.DMA((2, n)),
+            pltpu.SemaphoreType.DMA((2, n)),
+        ],
+        compiler_params=pltpu.CompilerParams(collective_id=1, has_side_effects=True),
+    )(first, second)
 
 
 def take_blocks(stack_a, stack_b, owner, local, me, n):
@@ -279,8 +343,11 @@
     chosen_out, filled_out = post_table(
         out_owner[mine], out_rank[mine], alive_mine, groups, capacity
     )
-    arrived_parts = lax.all_to_all(
-        pack_parts(parts, chosen_out, filled_out), "tensor", split_axis=0, concat_axis=0, tiled=True
+    chosen_in, filled_in = post_table(in_owner[mine], in_rank[mine], alive_mine, groups, capacity)
+    arrived_parts, arrived_back = exchange(
+        pack_parts(parts, chosen_out, filled_out),
+        pack_parts(back_parts, chosen_in, filled_in),
+        groups,
     )
     mixed = (
         collect_parts(
@@ -289,14 +356,6 @@
         + cross_bias
     )
     cross_out = (start_wide * mixed + start_wide).astype(jnp.bfloat16)
-    chosen_in, filled_in = post_table(in_owner[mine], in_rank[mine], alive_mine, groups, capacity)
-    arrived_back = lax.all_to_all(
-        pack_parts(back_parts, chosen_in, filled_in),
-        "tensor",
-        split_axis=0,
-        concat_axis=0,
-        tiled=True,
-    )
     grad_start = collect_parts(
         arrived_back, in_owner, in_local, in_rank, alive, mine, capacity, per_device
     )

time: 302 us -> 303 us (level)
  Pallas kernels: 88.2 us -> 161 us
  waiting for transfers between devices: 73 us -> 8.85 us
  starting transfers between devices: 8.38 us -> 0.3 us
    pallas_call x0 -> x1, Pallas kernels: none -> 72.8 us  [exchange(): pl.pallas_call(functools.partial(exchange_kernel, n), out_shape=[jax.Shap...]
    all_to_all x2 -> x0, waiting for transfers between devices: 64.6 us -> none  [the longest x1 34.8 us: on_device(): lax.all_to_all(pack_parts(back_parts, chosen_in, filled_in), 'tensor', sp...]
    all_to_all x2 -> x0, starting transfers between devices: 8.09 us -> none  [the longest x1 4.44 us: on_device(): lax.all_to_all(pack_parts(back_parts, chosen_in, filled_in), 'tensor', sp...]
  transfers between devices with their start and end apart: 5 -> 3, of which waited for: 3 -> 1; matrix products, arithmetic and copies ran while one was open for 13% -> 12% of each run, Pallas kernels for 25% -> 49%
where the time goes in v7:
time: 303 us; the launch traced here: 302 us
  Pallas kernels  161 us (53%)
  blocking collectives  76.9 us (25%)
  other arithmetic  15.9 us (5%)
  between operations  14 us (5%)
  matrix products  12.9 us (4%)
  local copies, waits for them, and re-layouts  12.5 us (4%)
  waiting for transfers between devices  8.85 us (3%)
    psum x1, blocking collectives, on_device(): lax.psum((jnp.sum(grad_pre, axis=0), jnp.sum(grad_mixed, axis=0)), 'dp')  76.9 us
    pallas_call x1, Pallas kernels, exchange(): pl.pallas_call(functools.partial(exchange_kernel, n), out_shape=[jax.Shap...  72.8 us
    pallas_call x1, Pallas kernels, ring_gather(): pl.pallas_call(functools.partial(ring_kernel, n), out_shape=[shape, shape...  64.8 us
    pallas_call x1, Pallas kernels, slot_products(): pl.pallas_call(slot_kernel, grid_spec=grid_spec, out_shape=[jax.ShapeDtyp...  14.1 us
    pallas_call x1, Pallas kernels, group_outer(): pl.pallas_call(outer_kernel, grid=(m // tile_m, n // tile_n), in_specs=[p...  9.38 us
    reduce_scatter x1, waiting for transfers between devices, on_device(): lax.psum_scatter(group_outer(taken, grad_pre_low), 'dp', scatter_dimensio...  8.13 us
    dot_general x1, matrix products, on_device(): jnp.dot(dense, bottom_weight, preferred_element_type=jnp.float32)  7.13 us
    gather x2, local copies, waits for them, and re-layouts, pack_parts(): jnp.take(parts, chosen.reshape(-1), axis=0)  6.29 us
  transfers between devices with their start and end apart: 3, of which 1 were waited for; matrix products, arithmetic and copies ran while one was open for 12% of the time, Pallas kernels for 49%

profile of v7, /device:TPU:0, one launch (start us, length us, event | category | flops | bytes accessed | tf_op | source)
XLA Modules:
  0.0 302.4 jit_solution(18078375404019510849)
XLA Ops:
  7.2 0.7 all-gather.2.cloned.1.call-update
  8.0 7.1 %fusion.8 = (f32[2048]{0:T(1024)S(1)}, bf16[192,2048]{1,0:T(8,128)(2,1)S(1)}, f32[192,2048]{1,0:T(8,128)}) fusion(bf16[192,2048]{1,0:T(8,128)(2,1)} %param.16, f32[2048]{0:T(1024)} %param.13, bf16[192,2048]{1,0:T(8,128)(2,1)} %left.1, bf16[2048,2048]{1,0:T(8,128)(2,1)} %param.12), kind=kOutput, calls=%fused_computation.21 | convolution fusion | flops 1614542848 | bytes 12337152 | tf_op jit(solution)/shard_map/dot_general | solution.py:309
  15.1 0.3 fusion.9
  15.4 1.3 pad_maximum_fusion
  16.7 64.8 %shard_map.128 = (bf16[8,96,4096]{2,1,0:T(8,128)(2,1)}, bf16[8,96,4096]{2,1,0:T(8,128)(2,1)}) custom-call(bf16[96,4096]{1,0:T(8,128)(2,1)} %get-tuple-element.44.top, bf16[96,4096]{1,0:T(8,128)(2,1)} %get-tuple-element.43.bottom), custom_call_target="tpu_custom_call" | custom-call | tf_op jit(solution)/shard_map/pallas_call | solution.py:117
  81.6 0.5 fusion.30
  82.1 0.5 fusion.20
  82.6 0.5 and_select_fusion
  83.2 0.6 and_select_fusion.1.sa_o
  83.8 0.5 and_select_fusion.3.sa_i
  84.3 14.1 %shard_map.129 = (bf16[10,192,512]{2,1,0:T(8,128)(2,1)}, bf16[10,192,512]{2,1,0:T(8,128)(2,1)}, bf16[10,512,512]{2,1,0:T(8,128)(2,1)}) custom-call(s32[10]{0:T(128)} %and_select_fusion.3.sa_i, s32[10]{0:T(128)} %get-tuple-element.49.sb_i, s32[10]{0:T(128)} %get-tuple-element.55.bi, s32[10]{0:T(128)} %and_select_fusion.1.sa_o, s32[10]{0:T(128)} %get-tuple-element.36.sb_o, ...), custom_call_target="tpu_custom_call" | custom-call | flops 3019898880 | bytes 18350080 | tf_op jit(solution)/shard_map/pallas_call | solution.py:252
  98.8 0.5 convert_reduce_fusion
  101.5 2.3 gather_fusion
  103.8 4.0 %gather_fusion.1 = bf16[16,192,512]{2,1,0:T(8,128)(2,1)} fusion(bf16[10,192,512]{2,1,0:T(8,128)(2,1)} %get-tuple-element.16, s32[1024]{0:T(1024)S(1)} %pad_clamp_fusion), kind=kCustom, calls=%fused_computation.1.clone | custom fusion | bytes 6291520 | tf_op jit(solution)/shard_map/jit(_take)/gather | solution.py:35
  107.8 2.0 select_multiply_fusion.1
  109.8 1.0 copy-done
  110.8 2.1 select_multiply_fusion
  112.9 72.8 %shard_map.130 = (bf16[8,384,512]{2,1,0:T(8,128)(2,1)}, bf16[8,384,512]{2,1,0:T(8,128)(2,1)}) custom-call(bf16[8,384,512]{2,1,0:T(8,128)(2,1)} %bitcast.33, bf16[8,384,512]{2,1,0:T(8,128)(2,1)} %bitcast.34), custom_call_target="tpu_custom_call" | custom-call | tf_op jit(solution)/shard_map/pallas_call | solution.py:178
  185.7 3.8 %fusion.2 = f32[4,192,512]{2,0,1:T(4,128)S(1)} fusion(bf16[16,4,1]{1,0,2:T(8,128)(2,1)S(1)} %bitcast.42, bf16[16,192,512]{2,1,0:T(8,128)(2,1)} %bitcast.40), kind=kOutput, calls=%fused_computation.4 | convolution fusion | flops 12582912 | bytes 4718720 | tf_op jit(solution)/shard_map/irb,il->rlb/dot_general | solution.py:56
  189.5 0.6 copy.54
  190.1 1.3 copy-done.3
  191.4 1.9 fusion
  193.4 0.6 copy.55
  194.0 0.5 copy-done.2
  194.5 0.2 copy-done.5
  194.7 0.5 copy-done.6
  195.3 2.1 fusion.28
  197.4 9.4 %shard_map.131 = bf16[2048,2048]{1,0:T(8,128)(2,1)} custom-call(bf16[192,2048]{1,0:T(8,128)(2,1)} %left.1, bf16[192,2048]{1,0:T(8,128)(2,1)} %get-tuple-element.31.right), custom_call_target="tpu_custom_call" | custom-call | flops 1610612736 | bytes 9961472 | tf_op jit(solution)/shard_map/pallas_call | solution.py:277
  206.8 76.9 %all-reduce = (f32[2048]{0:T(1024)}, f32[2048]{0:T(1024)}) all-reduce(f32[2048]{0:T(1024)S(1)} %get-tuple-element.30, f32[2048]{0:T(1024)S(1)} %get-tuple-element.28), channel_id=1, replica_groups=mesh['dp'=16,'tensor'=8] {'dp'}, use_global_device_ids=true, to_apply=%region_10.12 | all-reduce | flops 4096 | bytes 32768 | tf_op jit(solution)/shard_map/psum | solution.py:376
  283.7 1.9 convert_element_type.107
  285.6 8.1 %reduce-scatter.3.cloned.1.call-done = bf16[128,2048]{1,0:T(8,128)(2,1)} async-done(((bf16[2048,2048]{1,0:T(8,128)(2,1)}), bf16[128,2048]{1,0:T(8,128)(2,1)}) %reduce-scatter.3.cloned.1.call-update) | async-done | bytes 524304 | tf_op jit(solution)/shard_map/reduce_scatter | solution.py:370
  293.7 2.1 convert_element_type.106
  (64 shorter events, 2.7 us)
Async XLA Ops:
  7.2 77.1 %all-gather.2.cloned.1.call-start = ((), (), s32[]{:S(2)}) async-start(), calls=%async_computation.2 | async-start | bytes 5570560 | tf_op jit(solution)/shard_map/all_gather | solution.py:336
  7.9 275.8 %reduce-scatter.5.cloned.1.call-start = ((), (), s32[]{:S(2)}) async-start(), calls=%async_computation.4 | async-start | bytes 5570560 | tf_op jit(solution)/shard_map/reduce_scatter | solution.py:362
  8.0 7.2 %copy-start.4 = (bf16[192,2048]{1,0:T(8,128)(2,1)S(1)}, bf16[192,2048]{1,0:T(8,128)(2,1)}, u32[]{:S(2)}) copy-start(bf16[192,2048]{1,0:T(8,128)(2,1)} %param.16) | copy-start | bytes 2359300
  15.1 1.5 copy-start.1
  16.6 64.8 %copy-start.7 = (s32[8,10]{1,0:T(8,128)S(1)}, s32[8,10]{1,0:T(8,128)}, u32[]{:S(2)}) copy-start(s32[8,10]{1,0:T(8,128)} %param.17) | copy-start | bytes 964
  16.6 64.8 %copy-start.8 = (s32[8,10]{1,0:T(8,128)S(1)}, s32[8,10]{1,0:T(8,128)}, u32[]{:S(2)}) copy-start(s32[8,10]{1,0:T(8,128)} %param.18) | copy-start | bytes 964
  16.6 64.8 %copy-start.10 = (s32[8]{0:T(128)S(1)}, s32[8]{0:T(128)}, u32[]{:S(2)}) copy-start(s32[8]{0:T(128)} %param.19) | copy-start | bytes 100
  98.4 195.3 %reduce-scatter.3.cloned.1.call-start = ((), (), s32[]{:S(2)}) async-start(), calls=%async_computation.3 | async-start | bytes 8912896 | tf_op jit(solution)/shard_map/reduce_scatter | solution.py:370
  107.8 3.1 %copy-start = (bf16[16,192,512]{2,1,0:T(8,128)(2,1)S(1)}, bf16[16,192,512]{2,1,0:T(8,128)(2,1)}, u32[]{:S(2)}) copy-start(bf16[16,192,512]{2,1,0:T(8,128)(2,1)} %gather_fusion.1) | copy-start | bytes 9437188
  189.5 1.9 copy-start.3
  191.4 2.6 copy-start.9
  193.4 1.1 copy-start.2
  193.4 1.4 copy-start.5
  193.4 1.9 copy-start.6
Sparse Core Ops, SparseCore 0:
  10.1 58.9 all-gather.1
  98.5 80.8 reduce-scatter.4
  206.9 86.7 reduce-scatter.2

commit v8 on v7

--- a/solution.py
+++ b/solution.py
@@ -271,23 +271,118 @@
     ).astype(out.dtype)
 
 
-def group_outer(left, right, tile_m=512, tile_n=1024):
+def group_outer(left, right, core, tile_m=128, tile_n=1024):
     rows, m = left.shape
     n = right.shape[1]
-    return pl.pallas_call(
-        outer_kernel,
+
+    def place(i, j, c):
+        return ((1 - c[0]) * i + c[0] * ((i % 4) * 4 + i // 4), j)
+
+    grid_spec = pltpu.PrefetchScalarGridSpec(
+        num_scalar_prefetch=1,
         grid=(m // tile_m, n // tile_n),
         in_specs=[
-            pl.BlockSpec((rows, tile_m), lambda i, j: (0, i)),
-            pl.BlockSpec((rows, tile_n), lambda i, j: (0, j)),
-        ],
-        out_specs=pl.BlockSpec((tile_m, tile_n), lambda i, j: (i, j)),
+            pl.BlockSpec((rows, tile_m), lambda i, j, c: (0, i)),
+            pl.BlockSpec((rows, tile_n), lambda i, j, c: (0, j)),
+        ],
+        out_specs=pl.BlockSpec((tile_m, tile_n), place),
+    )
+    return pl.pallas_call(
+        lambda c, left_ref, right_ref, out_ref: outer_kernel(left_ref, right_ref, out_ref),
+        grid_spec=grid_spec,
         out_shape=jax.ShapeDtypeStruct((m, n), jnp.bfloat16),
         cost_estimate=pl.CostEstimate(
             flops=2 * rows * m * n, bytes_accessed=2 * (rows * (m + n) + m * n), transcendentals=0
         ),
-    )(left, right)
-
+    )(core.reshape(1), left, right)
+
+
+def reduce_kernel(side, part, out, send1, recv1, acc1, send2, recv2, sems1, sems2):
+    core = lax.axis_index("tensor") % 2
+    me = lax.axis_index("dp")
+    column = lax.axis_index("tensor")
+    hi, lo = me // side, me % side
+    p1 = (1 - core) * hi + core * lo
+    p2 = (1 - core) * lo + core * hi
+    mesh_ids = pl.DeviceIdType.MESH
+    half = part.shape[2] // 2
+    halves = (pl.ds(0, half), pl.ds(half, half))
+
+    def device(q1, q2):
+        q1, q2 = q1 % side, q2 % side
+        return (1 - core) * (q1 * side + q2) + core * (q2 * side + q1)
+
+    ring1 = (device(p1 + 1, p2), device(p1 - 1, p2))
+    ring2 = (device(p1, p2 + 1), device(p1, p2 - 1))
+    barrier = pltpu.get_barrier_semaphore()
+    for target in ring1 + ring2:
+        pl.semaphore_signal(barrier, inc=1, device_id=(target, column), device_id_type=mesh_ids)
+    pl.semaphore_wait(barrier, 4)
+
+    def link(send, recv, sems, d, step, target):
+        return pltpu.make_async_remote_copy(
+            src_ref=send.at[d, step],
+            dst_ref=recv.at[d, step],
+            send_sem=sems.at[0, d, step],
+            recv_sem=sems.at[1, d, step],
+            device_id=(target, column),
+            device_id_type=mesh_ids,
+        )
+
+    def own1(k, d):
+        return part[pl.ds(k * side, side), :, halves[d]].astype(jnp.float32)
+
+    def own2(k, d):
+        return acc1[k, :, halves[d]]
+
+    sends = []
+    for stage, (send, recv, sems, ring, pos, own) in enumerate(
+        ((send1, recv1, sems1, ring1, p1, own1), (send2, recv2, sems2, ring2, p2, own2))
+    ):
+        for step in range(side - 1):
+            for d, sign in ((0, 1), (1, -1)):
+                k = (pos - sign * (1 + step)) % side
+                value = own(k, d)
+                if step > 0:
+                    link(send, recv, sems, d, step - 1, ring[d]).wait_recv()
+                    value = value + recv[d, step - 1].astype(jnp.float32)
+                send[d, step] = value.astype(send.dtype)
+                copy = link(send, recv, sems, d, step, ring[d])
+                copy.start()
+                sends.append(copy)
+        for d in range(2):
+            link(send, recv, sems, d, side - 2, ring[d]).wait_recv()
+            total = own(pos, d) + recv[d, side - 2].astype(jnp.float32)
+            if stage == 0:
+                acc1[:, :, halves[d]] = total
+            else:
+                out[:, halves[d]] = total
+    for copy in sends:
+        copy.wait_send()
+
+
+def reduce_rows(part, side):
+    chunk, width = part.shape[0] // (side * side), part.shape[1]
+    part = part.reshape(side * side, chunk, width)
+    vmem = pl.BlockSpec(memory_space=pltpu.VMEM)
+    return pl.pallas_call(
+        functools.partial(reduce_kernel, side),
+        out_shape=jax.ShapeDtypeStruct((chunk, width), jnp.float32),
+        in_specs=[vmem],
+        out_specs=vmem,
+        scratch_shapes=[
+            pltpu.VMEM((2, side - 1, side, chunk, width // 2), jnp.bfloat16),
+            pltpu.VMEM((2, side - 1, side, chunk, width // 2), jnp.bfloat16),
+            pltpu.VMEM((side, chunk, width), jnp.float32),
+            pltpu.VMEM((2, side - 1, chunk, width // 2), jnp.bfloat16),
+            pltpu.VMEM((2, side - 1, chunk, width // 2), jnp.bfloat16),
+            pltpu.SemaphoreType.DMA((2, 2, side - 1)),
+            pltpu.SemaphoreType.DMA((2, 2, side - 1)),
+        ],
+        compiler_params=pltpu.CompilerParams(
+            collective_id=2, has_side_effects=True, vmem_limit_bytes=60 * 1024 * 1024
+        ),
+    )(part)
 
 def on_device(
     dense,
@@ -367,12 +462,8 @@
     grad_pre = grad_start * sigma * (1.0 + preact * (1.0 - sigma))
     grad_pre_low = grad_pre.astype(jnp.bfloat16)
     taken = dense
-    grad_bottom = lax.psum_scatter(
-        group_outer(taken, grad_pre_low),
-        "dp",
-        scatter_dimension=0,
-        tiled=True,
-    ).astype(jnp.float32)
+    side = int(round(lax.axis_size("dp") ** 0.5))
+    grad_bottom = reduce_rows(group_outer(taken, grad_pre_low, (mine % 2).astype(jnp.int32)), side)
     bias_sums = lax.psum((jnp.sum(grad_pre, axis=0), jnp.sum(grad_mixed, axis=0)), "dp")
     return (cross_out, grad_bottom, bias_sums[0], grad_blocks, bias_sums[1])
 

time: 303 us -> 376 us (1.24)
  Pallas kernels: 161 us -> 246 us
  waiting for transfers between devices: 8.85 us -> 0.7 us
  blocking collectives: 76.9 us -> 72.3 us
    pallas_call x1 -> x2, Pallas kernels: 9.38 us -> 94.2 us  [the longest x1 70.4 us: reduce_rows(): pl.pallas_call(functools.partial(reduce_kernel, side), out_shape=jax.Shap...]
    reduce_scatter x1 -> x0, waiting for transfers between devices: 8.13 us -> none  [on_device(): lax.psum_scatter(group_outer(taken, grad_pre_low), 'dp', scatter_dimensio...]
    psum x1, blocking collectives: 76.9 us -> 72.3 us  [on_device(): lax.psum((jnp.sum(grad_pre, axis=0), jnp.sum(grad_mixed, axis=0)), 'dp')]
  transfers between devices with their start and end apart: 3 -> 2, of which waited for: 1 -> 0; matrix products, arithmetic and copies ran while one was open for 12% -> 9% of each run, Pallas kernels for 49% -> 62%
where the time goes in v8:
time: 376 us; the launch traced here: 375 us
  Pallas kernels  246 us (65%)
  blocking collectives  72.3 us (19%)
  local copies, waits for them, and re-layouts  14.8 us (4%)
  between operations  14.3 us (4%)
  other arithmetic  13.8 us (4%)
  matrix products  12.9 us (3%)
    pallas_call x1, Pallas kernels, exchange(): pl.pallas_call(functools.partial(exchange_kernel, n), out_shape=[jax.Shap...  72.8 us
    psum x1, blocking collectives, on_device(): lax.psum((jnp.sum(grad_pre, axis=0), jnp.sum(grad_mixed, axis=0)), 'dp')  72.3 us
    pallas_call x1, Pallas kernels, reduce_rows(): pl.pallas_call(functools.partial(reduce_kernel, side), out_shape=jax.Shap...  70.4 us
    pallas_call x1, Pallas kernels, ring_gather(): pl.pallas_call(functools.partial(ring_kernel, n), out_shape=[shape, shape...  64.8 us
    pallas_call x1, Pallas kernels, group_outer(): pl.pallas_call(lambda c, left_ref, right_ref, out_ref: outer_kernel(left_...  23.8 us
    pallas_call x1, Pallas kernels, slot_products(): pl.pallas_call(slot_kernel, grid_spec=grid_spec, out_shape=[jax.ShapeDtyp...  14.3 us
  transfers between devices with their start and end apart: 2, of which 0 were waited for; matrix products, arithmetic and copies ran while one was open for 9% of the time, Pallas kernels for 62%

profile of v8, /device:TPU:0, one launch (start us, length us, event | category | flops | bytes accessed | tf_op | source)
XLA Modules:
  0.0 374.8 jit_solution(15543585331548768018)
XLA Ops:
  7.2 0.7 all-gather.2.cloned.1.call-update
  8.0 7.1 %fusion.8 = (f32[2048]{0:T(1024)S(1)}, bf16[192,2048]{1,0:T(8,128)(2,1)S(1)}, f32[192,2048]{1,0:T(8,128)}) fusion(bf16[192,2048]{1,0:T(8,128)(2,1)} %param.16, f32[2048]{0:T(1024)} %param.13, bf16[192,2048]{1,0:T(8,128)(2,1)} %left_ref.1, bf16[2048,2048]{1,0:T(8,128)(2,1)} %param.12), kind=kOutput, calls=%fused_computation.21 | convolution fusion | flops 1614542848 | bytes 12337152 | tf_op jit(solution)/shard_map/dot_general | solution.py:404
  15.1 0.3 fusion.9
  15.4 1.3 pad_maximum_fusion
  16.7 64.8 %shard_map.128 = (bf16[8,96,4096]{2,1,0:T(8,128)(2,1)}, bf16[8,96,4096]{2,1,0:T(8,128)(2,1)}) custom-call(bf16[96,4096]{1,0:T(8,128)(2,1)} %get-tuple-element.44.top, bf16[96,4096]{1,0:T(8,128)(2,1)} %get-tuple-element.43.bottom), custom_call_target="tpu_custom_call" | custom-call | tf_op jit(solution)/shard_map/pallas_call | solution.py:117
  81.6 0.5 fusion.30
  82.1 0.5 fusion.20
  82.6 0.5 and_select_fusion
  83.2 0.6 and_select_fusion.1.sa_o
  83.8 0.5 and_select_fusion.3.sa_i
  84.3 14.3 %shard_map.129 = (bf16[10,192,512]{2,1,0:T(8,128)(2,1)}, bf16[10,192,512]{2,1,0:T(8,128)(2,1)}, bf16[10,512,512]{2,1,0:T(8,128)(2,1)}) custom-call(s32[10]{0:T(128)} %and_select_fusion.3.sa_i, s32[10]{0:T(128)} %get-tuple-element.49.sb_i, s32[10]{0:T(128)} %get-tuple-element.55.bi, s32[10]{0:T(128)} %and_select_fusion.1.sa_o, s32[10]{0:T(128)} %get-tuple-element.36.sb_o, ...), custom_call_target="tpu_custom_call" | custom-call | flops 3019898880 | bytes 18350080 | tf_op jit(solution)/shard_map/pallas_call | solution.py:252
  98.7 0.5 convert_reduce_fusion
  101.4 2.3 gather_fusion
  103.7 4.0 %gather_fusion.1 = bf16[16,192,512]{2,1,0:T(8,128)(2,1)} fusion(bf16[10,192,512]{2,1,0:T(8,128)(2,1)} %get-tuple-element.16, s32[1024]{0:T(1024)S(1)} %pad_clamp_fusion), kind=kCustom, calls=%fused_computation.1.clone | custom fusion | bytes 6291520 | tf_op jit(solution)/shard_map/jit(_take)/gather | solution.py:35
  107.7 2.0 select_multiply_fusion.1
  109.8 1.0 copy-done
  110.8 2.1 select_multiply_fusion
  112.9 72.8 %shard_map.130 = (bf16[8,384,512]{2,1,0:T(8,128)(2,1)}, bf16[8,384,512]{2,1,0:T(8,128)(2,1)}) custom-call(bf16[8,384,512]{2,1,0:T(8,128)(2,1)} %bitcast.36, bf16[8,384,512]{2,1,0:T(8,128)(2,1)} %bitcast.37), custom_call_target="tpu_custom_call" | custom-call | tf_op jit(solution)/shard_map/pallas_call | solution.py:178
  185.7 3.8 %fusion.2 = f32[4,192,512]{2,0,1:T(4,128)S(1)} fusion(bf16[16,4,1]{1,0,2:T(8,128)(2,1)S(1)} %bitcast.45, bf16[16,192,512]{2,1,0:T(8,128)(2,1)} %bitcast.43), kind=kOutput, calls=%fused_computation.4 | convolution fusion | flops 12582912 | bytes 4718720 | tf_op jit(solution)/shard_map/irb,il->rlb/dot_general | solution.py:56
  189.5 0.6 copy.54
  190.1 1.3 copy-done.3
  191.4 1.9 fusion
  193.3 0.6 copy.55
  194.0 0.5 copy-done.2
  194.5 0.2 copy-done.5
  194.7 0.5 copy-done.6
  195.2 2.1 fusion.28
  197.3 23.8 %shard_map.131 = bf16[2048,2048]{1,0:T(8,128)(2,1)} custom-call(s32[1]{0:T(128)} %bitcast.11.c, bf16[192,2048]{1,0:T(8,128)(2,1)} %left_ref.1, bf16[192,2048]{1,0:T(8,128)(2,1)} %get-tuple-element.31.right_ref), custom_call_target="tpu_custom_call" | custom-call | flops 1610612736 | bytes 9961472 | tf_op jit(solution)/shard_map/pallas_call | solution.py:290
  221.1 70.4 %shard_map.132 = f32[128,2048]{1,0:T(8,128)} custom-call(bf16[16,128,2048]{2,1,0:T(8,128)(2,1)} %bitcast.35), custom_call_target="tpu_custom_call" | custom-call | tf_op jit(solution)/shard_map/pallas_call | solution.py:368
  291.5 72.3 %all-reduce = (f32[2048]{0:T(1024)}, f32[2048]{0:T(1024)}) all-reduce(f32[2048]{0:T(1024)S(1)} %get-tuple-element.30, f32[2048]{0:T(1024)S(1)} %get-tuple-element.28), channel_id=1, replica_groups=mesh['dp'=16,'tensor'=8] {'dp'}, use_global_device_ids=true, to_apply=%region_9.11 | all-reduce | flops 4096 | bytes 32768 | tf_op jit(solution)/shard_map/psum | solution.py:467
  363.8 1.9 convert_element_type.103
  365.7 2.3 copy.61
  (62 shorter events, 2.5 us)
Async XLA Ops:
  7.2 77.1 %all-gather.2.cloned.1.call-start = ((), (), s32[]{:S(2)}) async-start(), calls=%async_computation.1 | async-start | bytes 5570560 | tf_op jit(solution)/shard_map/all_gather | solution.py:431
  7.9 355.9 %reduce-scatter.2.cloned.1.call-start = ((), (), s32[]{:S(2)}) async-start(), calls=%async_computation.2 | async-start | bytes 5570560 | tf_op jit(solution)/shard_map/reduce_scatter | solution.py:457
  8.0 7.2 %copy-start.4 = (bf16[192,2048]{1,0:T(8,128)(2,1)S(1)}, bf16[192,2048]{1,0:T(8,128)(2,1)}, u32[]{:S(2)}) copy-start(bf16[192,2048]{1,0:T(8,128)(2,1)} %param.16) | copy-start | bytes 2359300
  15.1 1.5 copy-start.1
  16.6 64.8 %copy-start.7 = (s32[8,10]{1,0:T(8,128)S(1)}, s32[8,10]{1,0:T(8,128)}, u32[]{:S(2)}) copy-start(s32[8,10]{1,0:T(8,128)} %param.17) | copy-start | bytes 964
  16.6 64.8 %copy-start.8 = (s32[8,10]{1,0:T(8,128)S(1)}, s32[8,10]{1,0:T(8,128)}, u32[]{:S(2)}) copy-start(s32[8,10]{1,0:T(8,128)} %param.18) | copy-start | bytes 964
  16.6 64.8 %copy-start.10 = (s32[8]{0:T(128)S(1)}, s32[8]{0:T(128)}, u32[]{:S(2)}) copy-start(s32[8]{0:T(128)} %param.19) | copy-start | bytes 100
  107.7 3.1 copy-start
  189.5 1.9 copy-start.3
  191.4 2.6 copy-start.9
  193.3 1.1 copy-start.2
  193.3 1.4 copy-start.5
  193.3 1.9 copy-start.6
Sparse Core Ops, SparseCore 0:
  10.1 58.9 all-gather.1
  98.7 80.7 reduce-scatter.1

commit v9 on v8

--- a/solution.py
+++ b/solution.py
@@ -271,30 +271,22 @@
     ).astype(out.dtype)
 
 
-def group_outer(left, right, core, tile_m=128, tile_n=1024):
+def group_outer(left, right, tile_m=512, tile_n=1024):
     rows, m = left.shape
     n = right.shape[1]
-
-    def place(i, j, c):
-        return ((1 - c[0]) * i + c[0] * ((i % 4) * 4 + i // 4), j)
-
-    grid_spec = pltpu.PrefetchScalarGridSpec(
-        num_scalar_prefetch=1,
+    return pl.pallas_call(
+        outer_kernel,
         grid=(m // tile_m, n // tile_n),
         in_specs=[
-            pl.BlockSpec((rows, tile_m), lambda i, j, c: (0, i)),
-            pl.BlockSpec((rows, tile_n), lambda i, j, c: (0, j)),
-        ],
-        out_specs=pl.BlockSpec((tile_m, tile_n), place),
-    )
-    return pl.pallas_call(
-        lambda c, left_ref, right_ref, out_ref: outer_kernel(left_ref, right_ref, out_ref),
-        grid_spec=grid_spec,
+            pl.BlockSpec((rows, tile_m), lambda i, j: (0, i)),
+            pl.BlockSpec((rows, tile_n), lambda i, j: (0, j)),
+        ],
+        out_specs=pl.BlockSpec((tile_m, tile_n), lambda i, j: (i, j)),
         out_shape=jax.ShapeDtypeStruct((m, n), jnp.bfloat16),
         cost_estimate=pl.CostEstimate(
             flops=2 * rows * m * n, bytes_accessed=2 * (rows * (m + n) + m * n), transcendentals=0
         ),
-    )(core.reshape(1), left, right)
+    )(left, right)
 
 
 def reduce_kernel(side, part, out, send1, recv1, acc1, send2, recv2, sems1, sems2):
@@ -305,7 +297,7 @@
     p1 = (1 - core) * hi + core * lo
     p2 = (1 - core) * lo + core * hi
     mesh_ids = pl.DeviceIdType.MESH
-    half = part.shape[2] // 2
+    half = part.shape[3] // 2
     halves = (pl.ds(0, half), pl.ds(half, half))
 
     def device(q1, q2):
@@ -330,7 +322,9 @@
         )
 
     def own1(k, d):
-        return part[pl.ds(k * side, side), :, halves[d]].astype(jnp.float32)
+        lead = part[k, :, :, halves[d]]
+        cross = part[:, k, :, halves[d]]
+        return jnp.where(core == 0, lead, cross).astype(jnp.float32)
 
     def own2(k, d):
         return acc1[k, :, halves[d]]
@@ -363,7 +357,7 @@
 
 def reduce_rows(part, side):
     chunk, width = part.shape[0] // (side * side), part.shape[1]
-    part = part.reshape(side * side, chunk, width)
+    part = part.reshape(side, side, chunk, width)
     vmem = pl.BlockSpec(memory_space=pltpu.VMEM)
     return pl.pallas_call(
         functools.partial(reduce_kernel, side),
@@ -463,9 +457,10 @@
     grad_pre_low = grad_pre.astype(jnp.bfloat16)
     taken = dense
     side = int(round(lax.axis_size("dp") ** 0.5))
-    grad_bottom = reduce_rows(group_outer(taken, grad_pre_low, (mine % 2).astype(jnp.int32)), side)
-    bias_sums = lax.psum((jnp.sum(grad_pre, axis=0), jnp.sum(grad_mixed, axis=0)), "dp")
-    return (cross_out, grad_bottom, bias_sums[0], grad_blocks, bias_sums[1])
+    grad_bottom = reduce_rows(group_outer(taken, grad_pre_low), side)
+    grad_bias_bottom = jnp.sum(lax.all_gather(jnp.sum(grad_pre, axis=0), "dp"), axis=0)
+    grad_bias = jnp.sum(lax.all_gather(jnp.sum(grad_mixed, axis=0), "dp"), axis=0)
+    return (cross_out, grad_bottom, grad_bias_bottom, grad_blocks, grad_bias)
 
 
 def solution(mesh):

time: 376 us -> 337 us (0.90)
  blocking collectives: 72.3 us -> 48.6 us
  Pallas kernels: 246 us -> 229 us
    psum x1 -> x0, blocking collectives: 72.3 us -> none  [on_device(): lax.psum((jnp.sum(grad_pre, axis=0), jnp.sum(grad_mixed, axis=0)), 'dp')]
    all_gather x0 -> x2, blocking collectives: none -> 48.6 us  [the longest x1 25.5 us: on_device(): lax.all_gather(jnp.sum(grad_mixed, axis=0), 'dp')]
    pallas_call x1, Pallas kernels: 23.8 us -> 9.38 us  [group_outer(): pl.pallas_call(outer_kernel, grid=(m // tile_m, n // tile_n), in_specs=[p...]
  transfers between devices with their start and end apart: 2 -> 2, of which waited for: 0 -> 0; matrix products, arithmetic and copies ran while one was open for 9% -> 10% of each run, Pallas kernels for 62% -> 64%
where the time goes in v9:
time: 337 us; the launch traced here: 336 us
  Pallas kernels  229 us (68%)
  blocking collectives  48.6 us (14%)
  local copies, waits for them, and re-layouts  15.1 us (4%)
  other arithmetic  15 us (4%)
  between operations  14.3 us (4%)
  matrix products  12.9 us (4%)
    pallas_call x1, Pallas kernels, exchange(): pl.pallas_call(functools.partial(exchange_kernel, n), out_shape=[jax.Shap...  72.6 us
    pallas_call x1, Pallas kernels, reduce_rows(): pl.pallas_call(functools.partial(reduce_kernel, side), out_shape=jax.Shap...  68.6 us
    pallas_call x1, Pallas kernels, ring_gather(): pl.pallas_call(functools.partial(ring_kernel, n), out_shape=[shape, shape...  64.8 us
    all_gather x1, blocking collectives, on_device(): lax.all_gather(jnp.sum(grad_mixed, axis=0), 'dp')  25.5 us
    all_gather x1, blocking collectives, on_device(): lax.all_gather(jnp.sum(grad_pre, axis=0), 'dp')  23.1 us
    pallas_call x1, Pallas kernels, slot_products(): pl.pallas_call(slot_kernel, grid_spec=grid_spec, out_shape=[jax.ShapeDtyp...  14.1 us
    pallas_call x1, Pallas kernels, group_outer(): pl.pallas_call(outer_kernel, grid=(m // tile_m, n // tile_n), in_specs=[p...  9.38 us
    unnamed x25, local copies, waits for them, and re-layouts  7.22 us
  transfers between devices with their start and end apart: 2, of which 0 were waited for; matrix products, arithmetic and copies ran while one was open for 10% of the time, Pallas kernels for 64%

profile of v9, /device:TPU:0, one launch (start us, length us, event | category | flops | bytes accessed | tf_op | source)
XLA Modules:
  0.0 336.2 jit_solution(6397462334934564245)
XLA Ops:
  7.2 0.7 all-gather.4.cloned.1.call-update
  8.0 7.1 %fusion.8 = (f32[2048]{0:T(1024)S(1)}, bf16[192,2048]{1,0:T(8,128)(2,1)S(1)}, f32[192,2048]{1,0:T(8,128)}) fusion(bf16[192,2048]{1,0:T(8,128)(2,1)} %param.16, f32[2048]{0:T(1024)} %param.13, bf16[192,2048]{1,0:T(8,128)(2,1)} %left.1, bf16[2048,2048]{1,0:T(8,128)(2,1)} %param.12), kind=kOutput, calls=%fused_computation.21 | convolution fusion | flops 1614542848 | bytes 12337152 | tf_op jit(solution)/shard_map/dot_general | solution.py:398
  15.4 1.3 pad_maximum_fusion
  16.7 64.8 %shard_map.128 = (bf16[8,96,4096]{2,1,0:T(8,128)(2,1)}, bf16[8,96,4096]{2,1,0:T(8,128)(2,1)}) custom-call(bf16[96,4096]{1,0:T(8,128)(2,1)} %get-tuple-element.42.top, bf16[96,4096]{1,0:T(8,128)(2,1)} %get-tuple-element.41.bottom), custom_call_target="tpu_custom_call" | custom-call | tf_op jit(solution)/shard_map/pallas_call | solution.py:117
  81.6 0.5 fusion.30
  82.1 0.5 fusion.20
  82.6 0.5 and_select_fusion
  83.2 0.6 and_select_fusion.1.sa_o
  83.8 0.5 and_select_fusion.3.sa_i
  84.3 14.1 %shard_map.129 = (bf16[10,192,512]{2,1,0:T(8,128)(2,1)}, bf16[10,192,512]{2,1,0:T(8,128)(2,1)}, bf16[10,512,512]{2,1,0:T(8,128)(2,1)}) custom-call(s32[10]{0:T(128)} %and_select_fusion.3.sa_i, s32[10]{0:T(128)} %get-tuple-element.47.sb_i, s32[10]{0:T(128)} %get-tuple-element.53.bi, s32[10]{0:T(128)} %and_select_fusion.1.sa_o, s32[10]{0:T(128)} %get-tuple-element.34.sb_o, ...), custom_call_target="tpu_custom_call" | custom-call | flops 3019898880 | bytes 18350080 | tf_op jit(solution)/shard_map/pallas_call | solution.py:252
  101.2 25.5 %all-gather.1 = f32[32768]{0:T(1024)S(1)} all-gather(f32[2048]{0:T(1024)S(1)} %get-tuple-element.26), channel_id=3, replica_groups=mesh['dp'=16,'tensor'=8] {'dp'}, dimensions={0}, use_global_device_ids=true | all-gather | bytes 139264 | tf_op jit(solution)/shard_map/all_gather | solution.py:462
  126.7 0.6 reduce_sum.99
  127.4 2.3 gather_fusion
  129.7 4.0 %gather_fusion.1 = bf16[16,192,512]{2,1,0:T(8,128)(2,1)} fusion(bf16[10,192,512]{2,1,0:T(8,128)(2,1)} %get-tuple-element.16, s32[1024]{0:T(1024)S(1)} %pad_clamp_fusion), kind=kCustom, calls=%fused_computation.1.clone | custom fusion | bytes 6291520 | tf_op jit(solution)/shard_map/jit(_take)/gather | solution.py:35
  133.8 2.0 select_multiply_fusion.1
  135.8 1.2 copy-done
  136.9 2.1 select_multiply_fusion
  139.0 72.6 %shard_map.130 = (bf16[8,384,512]{2,1,0:T(8,128)(2,1)}, bf16[8,384,512]{2,1,0:T(8,128)(2,1)}) custom-call(bf16[8,384,512]{2,1,0:T(8,128)(2,1)} %bitcast.35, bf16[8,384,512]{2,1,0:T(8,128)(2,1)} %bitcast.36), custom_call_target="tpu_custom_call" | custom-call | tf_op jit(solution)/shard_map/pallas_call | solution.py:178
  211.6 3.8 %fusion.2 = f32[4,192,512]{2,0,1:T(4,128)S(1)} fusion(bf16[16,4,1]{1,0,2:T(8,128)(2,1)S(1)} %bitcast.44, bf16[16,192,512]{2,1,0:T(8,128)(2,1)} %bitcast.42), kind=kOutput, calls=%fused_computation.4 | convolution fusion | flops 12582912 | bytes 4718720 | tf_op jit(solution)/shard_map/irb,il->rlb/dot_general | solution.py:56
  215.4 0.6 copy.58
  216.0 1.3 copy-done.3
  217.3 1.9 fusion
  219.3 0.6 copy.59
  219.9 0.5 copy-done.2
  220.6 0.5 copy-done.6
  221.1 2.1 fusion.28
  223.3 23.1 %all-gather = f32[32768]{0:T(1024)S(1)} all-gather(f32[2048]{0:T(1024)S(1)} %get-tuple-element.28), channel_id=2, replica_groups=mesh['dp'=16,'tensor'=8] {'dp'}, dimensions={0}, use_global_device_ids=true | all-gather | bytes 139264 | tf_op jit(solution)/shard_map/all_gather | solution.py:461
  246.5 0.6 reduce_sum.97
  247.1 9.4 %shard_map.131 = bf16[2048,2048]{1,0:T(8,128)(2,1)} custom-call(bf16[192,2048]{1,0:T(8,128)(2,1)} %left.1, bf16[192,2048]{1,0:T(8,128)(2,1)} %get-tuple-element.29.right), custom_call_target="tpu_custom_call" | custom-call | flops 1610612736 | bytes 9961472 | tf_op jit(solution)/shard_map/pallas_call | solution.py:277
  256.5 68.6 %shard_map.132 = f32[128,2048]{1,0:T(8,128)} custom-call(bf16[4,4,128,2048]{3,2,1,0:T(8,128)(2,1)} %bitcast.34), custom_call_target="tpu_custom_call" | custom-call | tf_op jit(solution)/shard_map/pallas_call | solution.py:362
  325.1 1.9 convert_element_type.103
  327.0 2.3 copy.65
  (67 shorter events, 3.6 us)
Async XLA Ops:
  7.2 77.1 %all-gather.4.cloned.1.call-start = ((), (), s32[]{:S(2)}) async-start(), calls=%async_computation.1 | async-start | bytes 5570560 | tf_op jit(solution)/shard_map/all_gather | solution.py:425
  7.9 317.2 %reduce-scatter.2.cloned.1.call-start = ((), (), s32[]{:S(2)}) async-start(), calls=%async_computation.2 | async-start | bytes 5570560 | tf_op jit(solution)/shard_map/reduce_scatter | solution.py:451
  8.0 7.2 %copy-start.4 = (bf16[192,2048]{1,0:T(8,128)(2,1)S(1)}, bf16[192,2048]{1,0:T(8,128)(2,1)}, u32[]{:S(2)}) copy-start(bf16[192,2048]{1,0:T(8,128)(2,1)} %param.16) | copy-start | bytes 2359300
  15.1 1.5 copy-start.1
  16.6 64.8 %copy-start.7 = (s32[8,10]{1,0:T(8,128)S(1)}, s32[8,10]{1,0:T(8,128)}, u32[]{:S(2)}) copy-start(s32[8,10]{1,0:T(8,128)} %param.17) | copy-start | bytes 964
  16.6 64.8 %copy-start.8 = (s32[8,10]{1,0:T(8,128)S(1)}, s32[8,10]{1,0:T(8,128)}, u32[]{:S(2)}) copy-start(s32[8,10]{1,0:T(8,128)} %param.18) | copy-start | bytes 964
  16.6 64.8 %copy-start.10 = (s32[8]{0:T(128)S(1)}, s32[8]{0:T(128)}, u32[]{:S(2)}) copy-start(s32[8]{0:T(128)} %param.19) | copy-start | bytes 100
  133.8 3.2 copy-start
  215.4 1.9 copy-start.3
  217.3 2.6 copy-start.9
  219.2 1.1 copy-start.2
  219.2 1.4 copy-start.5
  219.3 1.9 copy-start.6
Sparse Core Ops, SparseCore 0:
  10.1 58.9 all-gather.3
  98.5 81.0 reduce-scatter.1

commit v10 on v9

--- a/solution.py
+++ b/solution.py
@@ -289,7 +289,8 @@
     )(left, right)
 
 
-def reduce_kernel(side, part, out, send1, recv1, acc1, send2, recv2, sems1, sems2):
+def reduce_kernel(side, part, bias, out, bias_out, send1, recv1, acc1, send2, recv2, sems1, sems2,
+                  bsend1, brecv1, bacc1, bsend2, brecv2, bsems1, bsems2):
     core = lax.axis_index("tensor") % 2
     me = lax.axis_index("dp")
     column = lax.axis_index("tensor")
@@ -329,41 +330,63 @@
     def own2(k, d):
         return acc1[k, :, halves[d]]
 
+    def store1(total, d):
+        acc1[:, :, halves[d]] = total
+
+    def store2(total, d):
+        out[:, halves[d]] = total
+
+    def bias1(k, d):
+        return bias[:, halves[d]]
+
+    def bias2(k, d):
+        return bacc1[:, halves[d]]
+
+    def bstore1(total, d):
+        bacc1[:, halves[d]] = total
+
+    def bstore2(total, d):
+        bias_out[:, halves[d]] = total
+
+    stages = (
+        (ring1, p1, ((send1, recv1, sems1, own1, store1), (bsend1, brecv1, bsems1, bias1, bstore1))),
+        (ring2, p2, ((send2, recv2, sems2, own2, store2), (bsend2, brecv2, bsems2, bias2, bstore2))),
+    )
     sends = []
-    for stage, (send, recv, sems, ring, pos, own) in enumerate(
-        ((send1, recv1, sems1, ring1, p1, own1), (send2, recv2, sems2, ring2, p2, own2))
-    ):
+    for ring, pos, channels in stages:
         for step in range(side - 1):
             for d, sign in ((0, 1), (1, -1)):
                 k = (pos - sign * (1 + step)) % side
-                value = own(k, d)
-                if step > 0:
-                    link(send, recv, sems, d, step - 1, ring[d]).wait_recv()
-                    value = value + recv[d, step - 1].astype(jnp.float32)
-                send[d, step] = value.astype(send.dtype)
-                copy = link(send, recv, sems, d, step, ring[d])
-                copy.start()
-                sends.append(copy)
+                for send, recv, sems, own, _ in channels:
+                    value = own(k, d)
+                    if step > 0:
+                        link(send, recv, sems, d, step - 1, ring[d]).wait_recv()
+                        value = value + recv[d, step - 1].astype(jnp.float32)
+                    send[d, step] = value.astype(send.dtype)
+                    copy = link(send, recv, sems, d, step, ring[d])
+                    copy.start()
+                    sends.append(copy)
         for d in range(2):
-            link(send, recv, sems, d, side - 2, ring[d]).wait_recv()
-            total = own(pos, d) + recv[d, side - 2].astype(jnp.float32)
-            if stage == 0:
-                acc1[:, :, halves[d]] = total
-            else:
-                out[:, halves[d]] = total
+            for send, recv, sems, own, store in channels:
+                link(send, recv, sems, d, side - 2, ring[d]).wait_recv()
+                store(own(pos, d) + recv[d, side - 2].astype(jnp.float32), d)
     for copy in sends:
         copy.wait_send()
 
 
-def reduce_rows(part, side):
+def reduce_rows(part, bias, side):
     chunk, width = part.shape[0] // (side * side), part.shape[1]
     part = part.reshape(side, side, chunk, width)
+    rows = bias.shape[0]
     vmem = pl.BlockSpec(memory_space=pltpu.VMEM)
     return pl.pallas_call(
         functools.partial(reduce_kernel, side),
-        out_shape=jax.ShapeDtypeStruct((chunk, width), jnp.float32),
-        in_specs=[vmem],
-        out_specs=vmem,
+        out_shape=[
+            jax.ShapeDtypeStruct((chunk, width), jnp.float32),
+            jax.ShapeDtypeStruct((rows, width), jnp.float32),
+        ],
+        in_specs=[vmem, vmem],
+        out_specs=[vmem, vmem],
         scratch_shapes=[
             pltpu.VMEM((2, side - 1, side, chunk, width // 2), jnp.bfloat16),
             pltpu.VMEM((2, side - 1, side, chunk, width // 2), jnp.bfloat16),
@@ -372,11 +395,18 @@
             pltpu.VMEM((2, side - 1, chunk, width // 2), jnp.bfloat16),
             pltpu.SemaphoreType.DMA((2, 2, side - 1)),
             pltpu.SemaphoreType.DMA((2, 2, side - 1)),
+            pltpu.VMEM((2, side - 1, rows, width // 2), jnp.float32),
+            pltpu.VMEM((2, side - 1, rows, width // 2), jnp.float32),
+            pltpu.VMEM((rows, width), jnp.float32),
+            pltpu.VMEM((2, side - 1, rows, width // 2), jnp.float32),
+            pltpu.VMEM((2, side - 1, rows, width // 2), jnp.float32),
+            pltpu.SemaphoreType.DMA((2, 2, side - 1)),
+            pltpu.SemaphoreType.DMA((2, 2, side - 1)),
         ],
         compiler_params=pltpu.CompilerParams(
             collective_id=2, has_side_effects=True, vmem_limit_bytes=60 * 1024 * 1024
         ),
-    )(part)
+    )(part, bias)
 
 def on_device(
     dense,
@@ -457,9 +487,11 @@
     grad_pre_low = grad_pre.astype(jnp.bfloat16)
     taken = dense
     side = int(round(lax.axis_size("dp") ** 0.5))
-    grad_bottom = reduce_rows(group_outer(taken, grad_pre_low), side)
-    grad_bias_bottom = jnp.sum(lax.all_gather(jnp.sum(grad_pre, axis=0), "dp"), axis=0)
-    grad_bias = jnp.sum(lax.all_gather(jnp.sum(grad_mixed, axis=0), "dp"), axis=0)
+    bias_rows = jnp.zeros((8, local_width), jnp.float32)
+    bias_rows = bias_rows.at[0].set(jnp.sum(grad_pre, axis=0)).at[1].set(jnp.sum(grad_mixed, axis=0))
+    grad_bottom, bias_sums = reduce_rows(group_outer(taken, grad_pre_low), bias_rows, side)
+    grad_bias_bottom = bias_sums[0]
+    grad_bias = bias_sums[1]
     return (cross_out, grad_bottom, grad_bias_bottom, grad_blocks, grad_bias)
 
 

time: 337 us -> 293 us (0.87)
  blocking collectives: 48.6 us -> 0 us
  Pallas kernels: 229 us -> 233 us
    all_gather x2 -> x0, blocking collectives: 48.6 us -> none  [the longest x1 25.5 us: on_device(): lax.all_gather(jnp.sum(grad_mixed, axis=0), 'dp')]
    unnamed x25 -> x27, local copies, waits for them, and re-layouts: 7.22 us -> 7.11 us
  transfers between devices with their start and end apart: 2 -> 2, of which waited for: 0 -> 0; matrix products, arithmetic and copies ran while one was open for 10% -> 12% of each run, Pallas kernels for 64% -> 75%
where the time goes in v10:
time: 293 us; the launch traced here: 291 us
  Pallas kernels  233 us (80%)
  local copies, waits for them, and re-layouts  16.5 us (6%)
  between operations  14.3 us (5%)
  other arithmetic  13.8 us (5%)
  matrix products  12.9 us (4%)
    pallas_call x1, Pallas kernels, exchange(): pl.pallas_call(functools.partial(exchange_kernel, n), out_shape=[jax.Shap...  72.8 us
    pallas_call x1, Pallas kernels, reduce_rows(): pl.pallas_call(functools.partial(reduce_kernel, side), out_shape=[jax.Sha...  71.6 us
    pallas_call x1, Pallas kernels, ring_gather(): pl.pallas_call(functools.partial(ring_kernel, n), out_shape=[shape, shape...  64.8 us
    pallas_call x1, Pallas kernels, slot_products(): pl.pallas_call(slot_kernel, grid_spec=grid_spec, out_shape=[jax.ShapeDtyp...  14.3 us
    pallas_call x1, Pallas kernels, group_outer(): pl.pallas_call(outer_kernel, grid=(m // tile_m, n // tile_n), in_specs=[p...  9.62 us
    dot_general x1, matrix products, on_device(): jnp.dot(dense, bottom_weight, preferred_element_type=jnp.float32)  7.13 us
    unnamed x27, local copies, waits for them, and re-layouts  7.11 us
    gather x2, local copies, waits for them, and re-layouts, pack_parts(): jnp.take(parts, chosen.reshape(-1), axis=0)  6.29 us
  transfers between devices with their start and end apart: 2, of which 0 were waited for; matrix products, arithmetic and copies ran while one was open for 12% of the time, Pallas kernels for 75%

profile of v10, /device:TPU:0, one launch (start us, length us, event | category | flops | bytes accessed | tf_op | source)
XLA Modules:
  0.0 291.4 jit_solution(11464140702758128902)
XLA Ops:
  7.2 0.7 all-gather.2.cloned.1.call-update
  8.0 7.1 %fusion.8 = (f32[2048]{0:T(1024)S(1)}, bf16[192,2048]{1,0:T(8,128)(2,1)S(1)}, f32[192,2048]{1,0:T(8,128)}) fusion(bf16[192,2048]{1,0:T(8,128)(2,1)} %param.20, f32[2048]{0:T(1024)} %param.17, bf16[192,2048]{1,0:T(8,128)(2,1)} %left.1, bf16[2048,2048]{1,0:T(8,128)(2,1)} %param.16), kind=kOutput, calls=%fused_computation.21 | convolution fusion | flops 1614542848 | bytes 12337152 | tf_op jit(solution)/shard_map/dot_general | solution.py:428
  15.1 0.3 fusion.9
  15.4 1.3 pad_maximum_fusion
  16.7 64.8 %shard_map.128 = (bf16[8,96,4096]{2,1,0:T(8,128)(2,1)}, bf16[8,96,4096]{2,1,0:T(8,128)(2,1)}) custom-call(bf16[96,4096]{1,0:T(8,128)(2,1)} %get-tuple-element.70.top, bf16[96,4096]{1,0:T(8,128)(2,1)} %get-tuple-element.69.bottom), custom_call_target="tpu_custom_call" | custom-call | tf_op jit(solution)/shard_map/pallas_call | solution.py:117
  81.6 0.5 fusion.30
  82.1 0.5 fusion.20
  82.6 0.5 and_select_fusion
  83.2 0.6 and_select_fusion.1.sa_o
  83.8 0.5 and_select_fusion.3.sa_i
  84.3 14.3 %shard_map.129 = (bf16[10,192,512]{2,1,0:T(8,128)(2,1)}, bf16[10,192,512]{2,1,0:T(8,128)(2,1)}, bf16[10,512,512]{2,1,0:T(8,128)(2,1)}) custom-call(s32[10]{0:T(128)} %and_select_fusion.3.sa_i, s32[10]{0:T(128)} %get-tuple-element.77.sb_i, s32[10]{0:T(128)} %get-tuple-element.83.bi, s32[10]{0:T(128)} %and_select_fusion.1.sa_o, s32[10]{0:T(128)} %get-tuple-element.62.sb_o, ...), custom_call_target="tpu_custom_call" | custom-call | flops 3019898880 | bytes 18350080 | tf_op jit(solution)/shard_map/pallas_call | solution.py:252
  98.7 0.5 convert_reduce_fusion
  101.4 2.3 gather_fusion
  103.7 4.0 %gather_fusion.1 = bf16[16,192,512]{2,1,0:T(8,128)(2,1)} fusion(bf16[10,192,512]{2,1,0:T(8,128)(2,1)} %get-tuple-element.42, s32[1024]{0:T(1024)S(1)} %pad_clamp_fusion), kind=kCustom, calls=%fused_computation.1.clone | custom fusion | bytes 6291520 | tf_op jit(solution)/shard_map/jit(_take)/gather | solution.py:35
  107.7 2.0 select_multiply_fusion.1
  109.8 1.0 copy-done
  110.8 2.1 select_multiply_fusion
  112.8 72.8 %shard_map.130 = (bf16[8,384,512]{2,1,0:T(8,128)(2,1)}, bf16[8,384,512]{2,1,0:T(8,128)(2,1)}) custom-call(bf16[8,384,512]{2,1,0:T(8,128)(2,1)} %bitcast.39, bf16[8,384,512]{2,1,0:T(8,128)(2,1)} %bitcast.40), custom_call_target="tpu_custom_call" | custom-call | tf_op jit(solution)/shard_map/pallas_call | solution.py:178
  185.7 3.8 %fusion.2 = f32[4,192,512]{2,0,1:T(4,128)S(1)} fusion(bf16[16,4,1]{1,0,2:T(8,128)(2,1)S(1)} %bitcast.49, bf16[16,192,512]{2,1,0:T(8,128)(2,1)} %bitcast.46), kind=kOutput, calls=%fused_computation.4 | convolution fusion | flops 12582912 | bytes 4718720 | tf_op jit(solution)/shard_map/irb,il->rlb/dot_general | solution.py:56
  189.5 0.6 copy.54
  190.1 1.3 copy-done.3
  191.4 1.9 fusion
  193.3 0.6 copy.55
  194.0 0.5 copy-done.2
  194.5 0.2 copy-done.5
  194.7 0.5 copy-done.6
  195.2 2.1 fusion.28
  197.6 9.6 %shard_map.131 = bf16[2048,2048]{1,0:T(8,128)(2,1)} custom-call(bf16[192,2048]{1,0:T(8,128)(2,1)} %left.1, bf16[192,2048]{1,0:T(8,128)(2,1)} %get-tuple-element.57.right), custom_call_target="tpu_custom_call" | custom-call | flops 1610612736 | bytes 9961472 | tf_op jit(solution)/shard_map/pallas_call | solution.py:277
  207.2 71.6 %shard_map.132 = (f32[128,2048]{1,0:T(8,128)}, f32[8,2048]{1,0:T(8,128)}) custom-call(bf16[4,4,128,2048]{3,2,1,0:T(8,128)(2,1)} %bitcast.38, f32[8,2048]{1,0:T(8,128)} %copy-done.7), custom_call_target="tpu_custom_call" | custom-call | tf_op jit(solution)/shard_map/pallas_call | solution.py:382
  278.9 1.5 fusion.33
  280.4 1.9 convert_element_type.103
  282.3 2.3 copy.62
  (66 shorter events, 2.7 us)
Async XLA Ops:
  7.2 77.1 %all-gather.2.cloned.1.call-start = ((), (), s32[]{:S(2)}) async-start(), calls=%async_computation.1 | async-start | bytes 5570560 | tf_op jit(solution)/shard_map/all_gather | solution.py:455
  7.9 272.5 %reduce-scatter.2.cloned.1.call-start = ((), (), s32[]{:S(2)}) async-start(), calls=%async_computation.2 | async-start | bytes 5570560 | tf_op jit(solution)/shard_map/reduce_scatter | solution.py:481
  8.0 7.2 %copy-start.4 = (bf16[192,2048]{1,0:T(8,128)(2,1)S(1)}, bf16[192,2048]{1,0:T(8,128)(2,1)}, u32[]{:S(2)}) copy-start(bf16[192,2048]{1,0:T(8,128)(2,1)} %param.20) | copy-start | bytes 2359300
  15.1 1.5 copy-start.1
  16.6 64.8 %copy-start.8 = (s32[8,10]{1,0:T(8,128)S(1)}, s32[8,10]{1,0:T(8,128)}, u32[]{:S(2)}) copy-start(s32[8,10]{1,0:T(8,128)} %param.21) | copy-start | bytes 964
  16.6 64.8 %copy-start.9 = (s32[8,10]{1,0:T(8,128)S(1)}, s32[8,10]{1,0:T(8,128)}, u32[]{:S(2)}) copy-start(s32[8,10]{1,0:T(8,128)} %param.22) | copy-start | bytes 964
  16.6 64.8 %copy-start.11 = (s32[8]{0:T(128)S(1)}, s32[8]{0:T(128)}, u32[]{:S(2)}) copy-start(s32[8]{0:T(128)} %param.23) | copy-start | bytes 100
  107.7 3.1 %copy-start = (bf16[16,192,512]{2,1,0:T(8,128)(2,1)S(1)}, bf16[16,192,512]{2,1,0:T(8,128)(2,1)}, u32[]{:S(2)}) copy-start(bf16[16,192,512]{2,1,0:T(8,128)(2,1)} %gather_fusion.1) | copy-start | bytes 9437188
  189.5 1.9 copy-start.3
  191.4 2.6 copy-start.10
  193.3 1.1 copy-start.2
  193.3 1.4 copy-start.5
  193.3 1.9 copy-start.6
  197.6 9.6 %copy-start.7 = (f32[8,2048]{1,0:T(8,128)}, f32[8,2048]{1,0:T(8,128)S(1)}, u32[]{:S(2)}) copy-start(f32[8,2048]{1,0:T(8,128)S(1)} %scatter.9.bias) | copy-start | bytes 196612
Sparse Core Ops, SparseCore 0:
  10.1 58.9 all-gather.1
  98.7 80.8 reduce-scatter.1

commit v11 on v10

--- a/solution.py
+++ b/solution.py
@@ -9,7 +9,7 @@
 
 BLK = 512
 SLOTS = 10
-RING_CHUNKS = 4
+RING_CHUNKS = 6
 
 
 def slot_ranks(owner, alive):

time: 293 us -> 294 us (level)
  no operation moved by 1% of the time
where the time goes in v11:
time: 294 us; the launch traced here: 292 us
  Pallas kernels  234 us (80%)
  local copies, waits for them, and re-layouts  16.5 us (6%)
  between operations  14.3 us (5%)
  other arithmetic  13.8 us (5%)
  matrix products  12.9 us (4%)
    pallas_call x1, Pallas kernels, exchange(): pl.pallas_call(functools.partial(exchange_kernel, n), out_shape=[jax.Shap...  72.8 us
    pallas_call x1, Pallas kernels, reduce_rows(): pl.pallas_call(functools.partial(reduce_kernel, side), out_shape=[jax.Sha...  71.6 us
    pallas_call x1, Pallas kernels, ring_gather(): pl.pallas_call(functools.partial(ring_kernel, n), out_shape=[shape, shape...  65.4 us
    pallas_call x1, Pallas kernels, slot_products(): pl.pallas_call(slot_kernel, grid_spec=grid_spec, out_shape=[jax.ShapeDtyp...  14.3 us
    pallas_call x1, Pallas kernels, group_outer(): pl.pallas_call(outer_kernel, grid=(m // tile_m, n // tile_n), in_specs=[p...  9.62 us
    dot_general x1, matrix products, on_device(): jnp.dot(dense, bottom_weight, preferred_element_type=jnp.float32)  7.13 us
    unnamed x27, local copies, waits for them, and re-layouts  7.11 us
    gather x2, local copies, waits for them, and re-layouts, pack_parts(): jnp.take(parts, chosen.reshape(-1), axis=0)  6.29 us
  transfers between devices with their start and end apart: 2, of which 0 were waited for; matrix products, arithmetic and copies ran while one was open for 12% of the time, Pallas kernels for 75%

profile of v11, /device:TPU:0, one launch (start us, length us, event | category | flops | bytes accessed | tf_op | source)
XLA Modules:
  0.0 292.0 jit_solution(1821903967425121309)
XLA Ops:
  7.2 0.7 all-gather.2.cloned.1.call-update
  8.0 7.1 %fusion.8 = (f32[2048]{0:T(1024)S(1)}, bf16[192,2048]{1,0:T(8,128)(2,1)S(1)}, f32[192,2048]{1,0:T(8,128)}) fusion(bf16[192,2048]{1,0:T(8,128)(2,1)} %param.20, f32[2048]{0:T(1024)} %param.17, bf16[192,2048]{1,0:T(8,128)(2,1)} %left.1, bf16[2048,2048]{1,0:T(8,128)(2,1)} %param.16), kind=kOutput, calls=%fused_computation.21 | convolution fusion | flops 1614542848 | bytes 12337152 | tf_op jit(solution)/shard_map/dot_general | solution.py:428
  15.1 0.3 fusion.9
  15.4 1.3 pad_maximum_fusion
  16.7 65.4 %shard_map.128 = (bf16[8,96,4096]{2,1,0:T(8,128)(2,1)}, bf16[8,96,4096]{2,1,0:T(8,128)(2,1)}) custom-call(bf16[96,4096]{1,0:T(8,128)(2,1)} %get-tuple-element.70.top, bf16[96,4096]{1,0:T(8,128)(2,1)} %get-tuple-element.69.bottom), custom_call_target="tpu_custom_call" | custom-call | tf_op jit(solution)/shard_map/pallas_call | solution.py:117
  82.2 0.5 fusion.30
  82.7 0.5 fusion.20
  83.3 0.5 and_select_fusion
  83.8 0.6 and_select_fusion.1.sa_o
  84.4 0.5 and_select_fusion.3.sa_i
  84.9 14.3 %shard_map.129 = (bf16[10,192,512]{2,1,0:T(8,128)(2,1)}, bf16[10,192,512]{2,1,0:T(8,128)(2,1)}, bf16[10,512,512]{2,1,0:T(8,128)(2,1)}) custom-call(s32[10]{0:T(128)} %and_select_fusion.3.sa_i, s32[10]{0:T(128)} %get-tuple-element.77.sb_i, s32[10]{0:T(128)} %get-tuple-element.83.bi, s32[10]{0:T(128)} %and_select_fusion.1.sa_o, s32[10]{0:T(128)} %get-tuple-element.62.sb_o, ...), custom_call_target="tpu_custom_call" | custom-call | flops 3019898880 | bytes 18350080 | tf_op jit(solution)/shard_map/pallas_call | solution.py:252
  99.3 0.5 convert_reduce_fusion
  102.0 2.3 gather_fusion
  104.3 4.0 %gather_fusion.1 = bf16[16,192,512]{2,1,0:T(8,128)(2,1)} fusion(bf16[10,192,512]{2,1,0:T(8,128)(2,1)} %get-tuple-element.42, s32[1024]{0:T(1024)S(1)} %pad_clamp_fusion), kind=kCustom, calls=%fused_computation.1.clone | custom fusion | bytes 6291520 | tf_op jit(solution)/shard_map/jit(_take)/gather | solution.py:35
  108.3 2.0 select_multiply_fusion.1
  110.4 1.0 copy-done
  111.4 2.1 select_multiply_fusion
  113.5 72.8 %shard_map.130 = (bf16[8,384,512]{2,1,0:T(8,128)(2,1)}, bf16[8,384,512]{2,1,0:T(8,128)(2,1)}) custom-call(bf16[8,384,512]{2,1,0:T(8,128)(2,1)} %bitcast.39, bf16[8,384,512]{2,1,0:T(8,128)(2,1)} %bitcast.40), custom_call_target="tpu_custom_call" | custom-call | tf_op jit(solution)/shard_map/pallas_call | solution.py:178
  186.3 3.8 %fusion.2 = f32[4,192,512]{2,0,1:T(4,128)S(1)} fusion(bf16[16,4,1]{1,0,2:T(8,128)(2,1)S(1)} %bitcast.49, bf16[16,192,512]{2,1,0:T(8,128)(2,1)} %bitcast.46), kind=kOutput, calls=%fused_computation.4 | convolution fusion | flops 12582912 | bytes 4718720 | tf_op jit(solution)/shard_map/irb,il->rlb/dot_general | solution.py:56
  190.1 0.6 copy.54
  190.7 1.3 copy-done.3
  192.0 1.9 fusion
  194.0 0.6 copy.55
  194.6 0.5 copy-done.2
  195.1 0.2 copy-done.5
  195.3 0.5 copy-done.6
  195.8 2.1 fusion.28
  198.2 9.6 %shard_map.131 = bf16[2048,2048]{1,0:T(8,128)(2,1)} custom-call(bf16[192,2048]{1,0:T(8,128)(2,1)} %left.1, bf16[192,2048]{1,0:T(8,128)(2,1)} %get-tuple-element.57.right), custom_call_target="tpu_custom_call" | custom-call | flops 1610612736 | bytes 9961472 | tf_op jit(solution)/shard_map/pallas_call | solution.py:277
  207.8 71.6 %shard_map.132 = (f32[128,2048]{1,0:T(8,128)}, f32[8,2048]{1,0:T(8,128)}) custom-call(bf16[4,4,128,2048]{3,2,1,0:T(8,128)(2,1)} %bitcast.38, f32[8,2048]{1,0:T(8,128)} %copy-done.7), custom_call_target="tpu_custom_call" | custom-call | tf_op jit(solution)/shard_map/pallas_call | solution.py:382
  279.5 1.5 fusion.33
  281.0 1.9 convert_element_type.103
  282.9 2.3 copy.62
  (66 shorter events, 2.7 us)
Async XLA Ops:
  7.2 77.7 %all-gather.2.cloned.1.call-start = ((), (), s32[]{:S(2)}) async-start(), calls=%async_computation.1 | async-start | bytes 5570560 | tf_op jit(solution)/shard_map/all_gather | solution.py:455
  7.9 273.1 %reduce-scatter.2.cloned.1.call-start = ((), (), s32[]{:S(2)}) async-start(), calls=%async_computation.2 | async-start | bytes 5570560 | tf_op jit(solution)/shard_map/reduce_scatter | solution.py:481
  8.0 7.2 %copy-start.4 = (bf16[192,2048]{1,0:T(8,128)(2,1)S(1)}, bf16[192,2048]{1,0:T(8,128)(2,1)}, u32[]{:S(2)}) copy-start(bf16[192,2048]{1,0:T(8,128)(2,1)} %param.20) | copy-start | bytes 2359300
  15.1 1.5 copy-start.1
  16.6 65.4 %copy-start.8 = (s32[8,10]{1,0:T(8,128)S(1)}, s32[8,10]{1,0:T(8,128)}, u32[]{:S(2)}) copy-start(s32[8,10]{1,0:T(8,128)} %param.21) | copy-start | bytes 964
  16.6 65.4 %copy-start.9 = (s32[8,10]{1,0:T(8,128)S(1)}, s32[8,10]{1,0:T(8,128)}, u32[]{:S(2)}) copy-start(s32[8,10]{1,0:T(8,128)} %param.22) | copy-start | bytes 964
  16.6 65.4 %copy-start.11 = (s32[8]{0:T(128)S(1)}, s32[8]{0:T(128)}, u32[]{:S(2)}) copy-start(s32[8]{0:T(128)} %param.23) | copy-start | bytes 100
  108.3 3.1 %copy-start = (bf16[16,192,512]{2,1,0:T(8,128)(2,1)S(1)}, bf16[16,192,512]{2,1,0:T(8,128)(2,1)}, u32[]{:S(2)}) copy-start(bf16[16,192,512]{2,1,0:T(8,128)(2,1)} %gather_fusion.1) | copy-start | bytes 9437188
  190.1 1.9 copy-start.3
  192.0 2.6 copy-start.10
  193.9 1.1 copy-start.2
  193.9 1.4 copy-start.5
  193.9 1.9 copy-start.6
  198.2 9.6 %copy-start.7 = (f32[8,2048]{1,0:T(8,128)}, f32[8,2048]{1,0:T(8,128)S(1)}, u32[]{:S(2)}) copy-start(f32[8,2048]{1,0:T(8,128)S(1)} %scatter.9.bias) | copy-start | bytes 196612
Sparse Core Ops, SparseCore 0:
  10.1 58.9 all-gather.1
  99.3 80.7 reduce-scatter.1

commit v12 on v10

--- a/solution.py
+++ b/solution.py
@@ -32,9 +32,7 @@
 
 
 def pack_parts(parts, chosen, filled):
-    picked = jnp.take(parts, chosen.reshape(-1), axis=0) * filled.reshape(-1)[:, None, None].astype(
-        parts.dtype
-    )
+    picked = jnp.take(parts, chosen.reshape(-1), axis=0)
     return picked.reshape(chosen.shape[0], chosen.shape[1] * parts.shape[1], parts.shape[2])
 
 

time: 293 us -> 292 us (level)
    mul x2 -> x0, other arithmetic: 4.09 us -> none  [pack_parts(): jnp.take(parts, chosen.reshape(-1), axis=0)]
    select_n x2 -> x4, other arithmetic: 0.01 us -> 4.08 us  [pack_parts(): picked = jnp.take(parts, chosen.reshape(-1), axis=0)]
where the time goes in v12:
time: 292 us; the launch traced here: 291 us
  Pallas kernels  233 us (80%)
  local copies, waits for them, and re-layouts  16.2 us (6%)
  between operations  14.3 us (5%)
  other arithmetic  13.6 us (5%)
  matrix products  12.9 us (4%)
    pallas_call x1, Pallas kernels, exchange(): pl.pallas_call(functools.partial(exchange_kernel, n), out_shape=[jax.Shap...  72.7 us
    pallas_call x1, Pallas kernels, reduce_rows(): pl.pallas_call(functools.partial(reduce_kernel, side), out_shape=[jax.Sha...  71.5 us
    pallas_call x1, Pallas kernels, ring_gather(): pl.pallas_call(functools.partial(ring_kernel, n), out_shape=[shape, shape...  64.8 us
    pallas_call x1, Pallas kernels, slot_products(): pl.pallas_call(slot_kernel, grid_spec=grid_spec, out_shape=[jax.ShapeDtyp...  14.2 us
    pallas_call x1, Pallas kernels, group_outer(): pl.pallas_call(outer_kernel, grid=(m // tile_m, n // tile_n), in_specs=[p...  9.63 us
    unnamed x27, local copies, waits for them, and re-layouts  7.16 us
    dot_general x1, matrix products, on_device(): jnp.dot(dense, bottom_weight, preferred_element_type=jnp.float32)  7.14 us
    gather x2, local copies, waits for them, and re-layouts, pack_parts(): picked = jnp.take(parts, chosen.reshape(-1), axis=0)  6.27 us
  transfers between devices with their start and end apart: 2, of which 0 were waited for; matrix products, arithmetic and copies ran while one was open for 12% of the time, Pallas kernels for 75%

profile of v12, /device:TPU:0, one launch (start us, length us, event | category | flops | bytes accessed | tf_op | source)
XLA Modules:
  0.0 290.7 jit_solution(171169125549421691)
XLA Ops:
  7.2 0.7 all-gather.2.cloned.1.call-update
  8.0 7.1 %fusion.8 = (f32[2048]{0:T(1024)S(1)}, bf16[192,2048]{1,0:T(8,128)(2,1)S(1)}, f32[192,2048]{1,0:T(8,128)}) fusion(bf16[192,2048]{1,0:T(8,128)(2,1)} %param.20, f32[2048]{0:T(1024)} %param.17, bf16[192,2048]{1,0:T(8,128)(2,1)} %left.1, bf16[2048,2048]{1,0:T(8,128)(2,1)} %param.16), kind=kOutput, calls=%fused_computation.21 | convolution fusion | flops 1614542848 | bytes 12337152 | tf_op jit(solution)/shard_map/dot_general | solution.py:426
  15.1 0.3 fusion.9
  15.4 1.3 pad_maximum_fusion
  16.7 64.8 %shard_map.128 = (bf16[8,96,4096]{2,1,0:T(8,128)(2,1)}, bf16[8,96,4096]{2,1,0:T(8,128)(2,1)}) custom-call(bf16[96,4096]{1,0:T(8,128)(2,1)} %get-tuple-element.68.top, bf16[96,4096]{1,0:T(8,128)(2,1)} %get-tuple-element.67.bottom), custom_call_target="tpu_custom_call" | custom-call | tf_op jit(solution)/shard_map/pallas_call | solution.py:115
  81.6 0.6 fusion.28
  82.2 0.5 fusion.18
  82.7 0.5 and_select_fusion
  83.2 0.6 and_select_fusion.1.sa_o
  83.8 0.5 and_select_fusion.3.sa_i
  84.3 14.2 %shard_map.129 = (bf16[10,192,512]{2,1,0:T(8,128)(2,1)}, bf16[10,192,512]{2,1,0:T(8,128)(2,1)}, bf16[10,512,512]{2,1,0:T(8,128)(2,1)}) custom-call(s32[10]{0:T(128)} %and_select_fusion.3.sa_i, s32[10]{0:T(128)} %get-tuple-element.75.sb_i, s32[10]{0:T(128)} %get-tuple-element.81.bi, s32[10]{0:T(128)} %and_select_fusion.1.sa_o, s32[10]{0:T(128)} %get-tuple-element.60.sb_o, ...), custom_call_target="tpu_custom_call" | custom-call | flops 3019898880 | bytes 18350080 | tf_op jit(solution)/shard_map/pallas_call | solution.py:250
  98.8 0.5 convert_reduce_fusion
  100.9 2.3 gather_fusion
  103.2 4.0 %gather_fusion.1 = bf16[16,192,512]{2,1,0:T(8,128)(2,1)} fusion(bf16[10,192,512]{2,1,0:T(8,128)(2,1)} %get-tuple-element.42, s32[1024]{0:T(1024)S(1)} %pad_clamp_fusion), kind=kCustom, calls=%fused_computation.1.clone | custom fusion | bytes 6291520 | tf_op jit(solution)/shard_map/jit(_take)/gather | solution.py:35
  107.2 2.0 broadcast_select_fusion.1
  109.2 1.1 copy-done
  110.3 2.0 broadcast_select_fusion
  112.3 72.7 %shard_map.130 = (bf16[8,384,512]{2,1,0:T(8,128)(2,1)}, bf16[8,384,512]{2,1,0:T(8,128)(2,1)}) custom-call(bf16[8,384,512]{2,1,0:T(8,128)(2,1)} %bitcast.39, bf16[8,384,512]{2,1,0:T(8,128)(2,1)} %bitcast.40), custom_call_target="tpu_custom_call" | custom-call | tf_op jit(solution)/shard_map/pallas_call | solution.py:176
  185.1 3.8 %fusion.2 = f32[4,192,512]{2,0,1:T(4,128)S(1)} fusion(bf16[16,4,1]{1,0,2:T(8,128)(2,1)S(1)} %bitcast.49, bf16[16,192,512]{2,1,0:T(8,128)(2,1)} %bitcast.46), kind=kOutput, calls=%fused_computation.4 | convolution fusion | flops 12582912 | bytes 4718720 | tf_op jit(solution)/shard_map/irb,il->rlb/dot_general | solution.py:54
  188.9 0.6 copy.50
  189.5 1.3 copy-done.3
  190.8 1.9 fusion
  192.8 0.6 copy.51
  193.4 0.5 copy-done.2
  193.9 0.2 copy-done.5
  194.1 0.5 copy-done.6
  194.6 2.1 fusion.26
  197.0 9.6 %shard_map.131 = bf16[2048,2048]{1,0:T(8,128)(2,1)} custom-call(bf16[192,2048]{1,0:T(8,128)(2,1)} %left.1, bf16[192,2048]{1,0:T(8,128)(2,1)} %get-tuple-element.55.right), custom_call_target="tpu_custom_call" | custom-call | flops 1610612736 | bytes 9961472 | tf_op jit(solution)/shard_map/pallas_call | solution.py:275
  206.6 71.5 %shard_map.132 = (f32[128,2048]{1,0:T(8,128)}, f32[8,2048]{1,0:T(8,128)}) custom-call(bf16[4,4,128,2048]{3,2,1,0:T(8,128)(2,1)} %bitcast.38, f32[8,2048]{1,0:T(8,128)} %copy-done.7), custom_call_target="tpu_custom_call" | custom-call | tf_op jit(solution)/shard_map/pallas_call | solution.py:380
  278.2 1.5 fusion.31
  279.7 1.9 convert_element_type.77
  281.6 2.3 copy.58
  (59 shorter events, 2.2 us)
Async XLA Ops:
  7.2 77.2 %all-gather.2.cloned.1.call-start = ((), (), s32[]{:S(2)}) async-start(), calls=%async_computation.1 | async-start | bytes 5570560 | tf_op jit(solution)/shard_map/all_gather | solution.py:453
  7.9 271.8 %reduce-scatter.2.cloned.1.call-start = ((), (), s32[]{:S(2)}) async-start(), calls=%async_computation.2 | async-start | bytes 5570560 | tf_op jit(solution)/shard_map/reduce_scatter | solution.py:479
  8.0 7.2 %copy-start.4 = (bf16[192,2048]{1,0:T(8,128)(2,1)S(1)}, bf16[192,2048]{1,0:T(8,128)(2,1)}, u32[]{:S(2)}) copy-start(bf16[192,2048]{1,0:T(8,128)(2,1)} %param.20) | copy-start | bytes 2359300
  15.1 1.5 copy-start.1
  16.7 64.8 %copy-start.8 = (s32[8,10]{1,0:T(8,128)S(1)}, s32[8,10]{1,0:T(8,128)}, u32[]{:S(2)}) copy-start(s32[8,10]{1,0:T(8,128)} %param.21) | copy-start | bytes 964
  16.7 64.8 %copy-start.9 = (s32[8,10]{1,0:T(8,128)S(1)}, s32[8,10]{1,0:T(8,128)}, u32[]{:S(2)}) copy-start(s32[8,10]{1,0:T(8,128)} %param.22) | copy-start | bytes 964
  16.7 64.8 %copy-start.11 = (s32[8]{0:T(128)S(1)}, s32[8]{0:T(128)}, u32[]{:S(2)}) copy-start(s32[8]{0:T(128)} %param.23) | copy-start | bytes 100
  107.2 3.1 %copy-start = (bf16[16,192,512]{2,1,0:T(8,128)(2,1)S(1)}, bf16[16,192,512]{2,1,0:T(8,128)(2,1)}, u32[]{:S(2)}) copy-start(bf16[16,192,512]{2,1,0:T(8,128)(2,1)} %gather_fusion.1) | copy-start | bytes 9437188
  188.9 1.9 copy-start.3
  190.8 2.6 copy-start.10
  192.7 1.1 copy-start.2
  192.8 1.4 copy-start.5
  192.8 1.9 copy-start.6
  197.0 9.6 %copy-start.7 = (f32[8,2048]{1,0:T(8,128)}, f32[8,2048]{1,0:T(8,128)S(1)}, u32[]{:S(2)}) copy-start(f32[8,2048]{1,0:T(8,128)S(1)} %scatter.9.bias) | copy-start | bytes 196612
Sparse Core Ops, SparseCore 0:
  10.1 58.9 all-gather.1
  98.7 80.8 reduce-scatter.1

commit v13 on v12

--- a/solution.py
+++ b/solution.py
@@ -476,8 +476,8 @@
     grad_start = collect_parts(
         arrived_back, in_owner, in_local, in_rank, alive, mine, capacity, per_device
     )
-    grad_blocks = lax.psum_scatter(block_terms, "dp", scatter_dimension=1, tiled=True).astype(
-        jnp.float32
+    grad_blocks = lax.psum_scatter(
+        block_terms.astype(jnp.float32), "dp", scatter_dimension=1, tiled=True
     )
     grad_start = grad_start + cot_wide * mixed + cot_wide
     sigma = jax.nn.sigmoid(preact)

time: 292 us -> 298 us (1.021)
  other arithmetic: 13.6 us -> 19.7 us
    convert_element_type x1, other arithmetic: 1.89 us -> 7.91 us  [on_device(): block_terms.astype(jnp.float32)]
  transfers between devices with their start and end apart: 2 -> 2, of which waited for: 0 -> 0; matrix products, arithmetic and copies ran while one was open for 12% -> 12% of each run, Pallas kernels for 75% -> 74%
where the time goes in v13:
time: 298 us; the launch traced here: 297 us
  Pallas kernels  233 us (78%)
  other arithmetic  19.7 us (7%)
  local copies, waits for them, and re-layouts  16.2 us (5%)
  between operations  14.3 us (5%)
  matrix products  13 us (4%)
    pallas_call x1, Pallas kernels, exchange(): pl.pallas_call(functools.partial(exchange_kernel, n), out_shape=[jax.Shap...  72.7 us
    pallas_call x1, Pallas kernels, reduce_rows(): pl.pallas_call(functools.partial(reduce_kernel, side), out_shape=[jax.Sha...  71.4 us
    pallas_call x1, Pallas kernels, ring_gather(): pl.pallas_call(functools.partial(ring_kernel, n), out_shape=[shape, shape...  64.8 us
    pallas_call x1, Pallas kernels, slot_products(): pl.pallas_call(slot_kernel, grid_spec=grid_spec, out_shape=[jax.ShapeDtyp...  14.3 us
    pallas_call x1, Pallas kernels, group_outer(): pl.pallas_call(outer_kernel, grid=(m // tile_m, n // tile_n), in_specs=[p...  9.6 us
    convert_element_type x1, other arithmetic, on_device(): block_terms.astype(jnp.float32)  7.91 us
    unnamed x27, local copies, waits for them, and re-layouts  7.22 us
    dot_general x1, matrix products, on_device(): jnp.dot(dense, bottom_weight, preferred_element_type=jnp.float32)  7.14 us
  transfers between devices with their start and end apart: 2, of which 0 were waited for; matrix products, arithmetic and copies ran while one was open for 12% of the time, Pallas kernels for 74%

profile of v13, /device:TPU:0, one launch (start us, length us, event | category | flops | bytes accessed | tf_op | source)
XLA Modules:
  0.0 296.7 jit_solution(15466868562178708819)
XLA Ops:
  7.2 0.7 all-gather.2.cloned.1.call-update
  8.0 7.1 %fusion.8 = (f32[2048]{0:T(1024)S(1)}, bf16[192,2048]{1,0:T(8,128)(2,1)S(1)}, f32[192,2048]{1,0:T(8,128)}) fusion(bf16[192,2048]{1,0:T(8,128)(2,1)} %param.20, f32[2048]{0:T(1024)} %param.17, bf16[192,2048]{1,0:T(8,128)(2,1)} %left.1, bf16[2048,2048]{1,0:T(8,128)(2,1)} %param.16), kind=kOutput, calls=%fused_computation.21 | convolution fusion | flops 1614542848 | bytes 12337152 | tf_op jit(solution)/shard_map/dot_general | solution.py:426
  15.1 0.3 fusion.9
  15.4 1.3 pad_maximum_fusion
  16.7 64.8 %shard_map.128 = (bf16[8,96,4096]{2,1,0:T(8,128)(2,1)}, bf16[8,96,4096]{2,1,0:T(8,128)(2,1)}) custom-call(bf16[96,4096]{1,0:T(8,128)(2,1)} %get-tuple-element.68.top, bf16[96,4096]{1,0:T(8,128)(2,1)} %get-tuple-element.67.bottom), custom_call_target="tpu_custom_call" | custom-call | tf_op jit(solution)/shard_map/pallas_call | solution.py:115
  81.6 0.6 fusion.28
  82.2 0.5 fusion.18
  82.7 0.5 and_select_fusion
  83.2 0.6 and_select_fusion.1.sa_o
  83.8 0.5 and_select_fusion.3.sa_i
  84.3 14.3 %shard_map.129 = (bf16[10,192,512]{2,1,0:T(8,128)(2,1)}, bf16[10,192,512]{2,1,0:T(8,128)(2,1)}, bf16[10,512,512]{2,1,0:T(8,128)(2,1)}) custom-call(s32[10]{0:T(128)} %and_select_fusion.3.sa_i, s32[10]{0:T(128)} %get-tuple-element.75.sb_i, s32[10]{0:T(128)} %get-tuple-element.81.bi, s32[10]{0:T(128)} %and_select_fusion.1.sa_o, s32[10]{0:T(128)} %get-tuple-element.60.sb_o, ...), custom_call_target="tpu_custom_call" | custom-call | flops 3019898880 | bytes 18350080 | tf_op jit(solution)/shard_map/pallas_call | solution.py:250
  98.6 7.9 %convert_element_type.77 = f32[10,512,512]{2,1,0:T(8,128)} convert(bf16[10,512,512]{2,1,0:T(8,128)(2,1)} %get-tuple-element.47) | non-fusion elementwise | flops 2621440 | bytes 15728640 | tf_op jit(solution)/shard_map/convert_element_type | solution.py:480
  106.7 0.5 convert_reduce_fusion
  108.8 2.3 gather_fusion
  111.1 3.9 %gather_fusion.1 = bf16[16,192,512]{2,1,0:T(8,128)(2,1)} fusion(bf16[10,192,512]{2,1,0:T(8,128)(2,1)} %get-tuple-element.42, s32[1024]{0:T(1024)S(1)} %pad_clamp_fusion), kind=kCustom, calls=%fused_computation.1.clone | custom fusion | bytes 6291520 | tf_op jit(solution)/shard_map/jit(_take)/gather | solution.py:35
  115.1 2.1 broadcast_select_fusion.1
  117.2 1.0 copy-done
  118.2 2.0 broadcast_select_fusion
  120.2 72.7 %shard_map.130 = (bf16[8,384,512]{2,1,0:T(8,128)(2,1)}, bf16[8,384,512]{2,1,0:T(8,128)(2,1)}) custom-call(bf16[8,384,512]{2,1,0:T(8,128)(2,1)} %bitcast.39, bf16[8,384,512]{2,1,0:T(8,128)(2,1)} %bitcast.40), custom_call_target="tpu_custom_call" | custom-call | tf_op jit(solution)/shard_map/pallas_call | solution.py:176
  192.9 3.9 %fusion.2 = f32[4,192,512]{2,0,1:T(4,128)S(1)} fusion(bf16[16,4,1]{1,0,2:T(8,128)(2,1)S(1)} %bitcast.49, bf16[16,192,512]{2,1,0:T(8,128)(2,1)} %bitcast.46), kind=kOutput, calls=%fused_computation.4 | convolution fusion | flops 12582912 | bytes 4718720 | tf_op jit(solution)/shard_map/irb,il->rlb/dot_general | solution.py:54
  196.8 0.6 copy.50
  197.4 1.4 copy-done.3
  198.8 1.9 fusion
  200.8 0.6 copy.51
  201.4 0.5 copy-done.2
  201.9 0.2 copy-done.5
  202.1 0.5 copy-done.6
  202.6 2.1 fusion.26
  205.0 9.6 %shard_map.131 = bf16[2048,2048]{1,0:T(8,128)(2,1)} custom-call(bf16[192,2048]{1,0:T(8,128)(2,1)} %left.1, bf16[192,2048]{1,0:T(8,128)(2,1)} %get-tuple-element.55.right), custom_call_target="tpu_custom_call" | custom-call | flops 1610612736 | bytes 9961472 | tf_op jit(solution)/shard_map/pallas_call | solution.py:275
  214.6 71.4 %shard_map.132 = (f32[128,2048]{1,0:T(8,128)}, f32[8,2048]{1,0:T(8,128)}) custom-call(bf16[4,4,128,2048]{3,2,1,0:T(8,128)(2,1)} %bitcast.38, f32[8,2048]{1,0:T(8,128)} %copy-done.7), custom_call_target="tpu_custom_call" | custom-call | tf_op jit(solution)/shard_map/pallas_call | solution.py:380
  286.1 1.5 fusion.31
  287.6 2.3 copy.58
  (59 shorter events, 2.2 us)
Async XLA Ops:
  7.2 77.2 %all-gather.2.cloned.1.call-start = ((), (), s32[]{:S(2)}) async-start(), calls=%async_computation.1 | async-start | bytes 5570560 | tf_op jit(solution)/shard_map/all_gather | solution.py:453
  7.9 279.7 %reduce-scatter.2.cloned.1.call-start = ((), (), s32[]{:S(2)}) async-start(), calls=%async_computation.2 | async-start | bytes 11141120 | tf_op jit(solution)/shard_map/reduce_scatter | solution.py:479
  8.0 7.2 %copy-start.4 = (bf16[192,2048]{1,0:T(8,128)(2,1)S(1)}, bf16[192,2048]{1,0:T(8,128)(2,1)}, u32[]{:S(2)}) copy-start(bf16[192,2048]{1,0:T(8,128)(2,1)} %param.20) | copy-start | bytes 2359300
  15.1 1.5 copy-start.1
  16.7 64.8 %copy-start.8 = (s32[8,10]{1,0:T(8,128)S(1)}, s32[8,10]{1,0:T(8,128)}, u32[]{:S(2)}) copy-start(s32[8,10]{1,0:T(8,128)} %param.21) | copy-start | bytes 964
  16.7 64.8 %copy-start.9 = (s32[8,10]{1,0:T(8,128)S(1)}, s32[8,10]{1,0:T(8,128)}, u32[]{:S(2)}) copy-start(s32[8,10]{1,0:T(8,128)} %param.22) | copy-start | bytes 964
  16.7 64.8 %copy-start.11 = (s32[8]{0:T(128)S(1)}, s32[8]{0:T(128)}, u32[]{:S(2)}) copy-start(s32[8]{0:T(128)} %param.23) | copy-start | bytes 100
  115.1 3.2 %copy-start = (bf16[16,192,512]{2,1,0:T(8,128)(2,1)S(1)}, bf16[16,192,512]{2,1,0:T(8,128)(2,1)}, u32[]{:S(2)}) copy-start(bf16[16,192,512]{2,1,0:T(8,128)(2,1)} %gather_fusion.1) | copy-start | bytes 9437188
  196.8 2.0 copy-start.3
  198.8 2.6 copy-start.10
  200.7 1.1 copy-start.2
  200.8 1.4 copy-start.5
  200.8 1.9 copy-start.6
  205.0 9.6 %copy-start.7 = (f32[8,2048]{1,0:T(8,128)}, f32[8,2048]{1,0:T(8,128)S(1)}, u32[]{:S(2)}) copy-start(f32[8,2048]{1,0:T(8,128)S(1)} %scatter.9.bias) | copy-start | bytes 196612
Sparse Core Ops, SparseCore 0:
  10.1 58.9 all-gather.1
  106.6 91.7 reduce-scatter.1

commit v14 on v12

--- a/solution.py
+++ b/solution.py
@@ -269,7 +269,7 @@
     ).astype(out.dtype)
 
 
-def group_outer(left, right, tile_m=512, tile_n=1024):
+def group_outer(left, right, tile_m=512, tile_n=2048):
     rows, m = left.shape
     n = right.shape[1]
     return pl.pallas_call(

time: 292 us -> 289 us (0.990)
  Pallas kernels: 233 us -> 230 us
where the time goes in v14:
time: 289 us; the launch traced here: 288 us
  Pallas kernels  230 us (80%)
  local copies, waits for them, and re-layouts  16.2 us (6%)
  between operations  14.3 us (5%)
  other arithmetic  13.6 us (5%)
  matrix products  12.9 us (4%)
    pallas_call x1, Pallas kernels, exchange(): pl.pallas_call(functools.partial(exchange_kernel, n), out_shape=[jax.Shap...  72.7 us
    pallas_call x1, Pallas kernels, reduce_rows(): pl.pallas_call(functools.partial(reduce_kernel, side), out_shape=[jax.Sha...  71.5 us
    pallas_call x1, Pallas kernels, ring_gather(): pl.pallas_call(functools.partial(ring_kernel, n), out_shape=[shape, shape...  64.8 us
    pallas_call x1, Pallas kernels, slot_products(): pl.pallas_call(slot_kernel, grid_spec=grid_spec, out_shape=[jax.ShapeDtyp...  14.2 us
    unnamed x27, local copies, waits for them, and re-layouts  7.16 us
    dot_general x1, matrix products, on_device(): jnp.dot(dense, bottom_weight, preferred_element_type=jnp.float32)  7.14 us
    pallas_call x1, Pallas kernels, group_outer(): pl.pallas_call(outer_kernel, grid=(m // tile_m, n // tile_n), in_specs=[p...  6.76 us
    gather x2, local copies, waits for them, and re-layouts, pack_parts(): picked = jnp.take(parts, chosen.reshape(-1), axis=0)  6.27 us
  transfers between devices with their start and end apart: 2, of which 0 were waited for; matrix products, arithmetic and copies ran while one was open for 12% of the time, Pallas kernels for 75%

profile of v14, /device:TPU:0, one launch (start us, length us, event | category | flops | bytes accessed | tf_op | source)
XLA Modules:
  0.0 287.9 jit_solution(10953489214021940260)
XLA Ops:
  7.2 0.7 all-gather.2.cloned.1.call-update
  8.0 7.1 %fusion.8 = (f32[2048]{0:T(1024)S(1)}, bf16[192,2048]{1,0:T(8,128)(2,1)S(1)}, f32[192,2048]{1,0:T(8,128)}) fusion(bf16[192,2048]{1,0:T(8,128)(2,1)} %param.20, f32[2048]{0:T(1024)} %param.17, bf16[192,2048]{1,0:T(8,128)(2,1)} %left.1, bf16[2048,2048]{1,0:T(8,128)(2,1)} %param.16), kind=kOutput, calls=%fused_computation.21 | convolution fusion | flops 1614542848 | bytes 12337152 | tf_op jit(solution)/shard_map/dot_general | solution.py:426
  15.1 0.3 fusion.9
  15.4 1.3 pad_maximum_fusion
  16.7 64.8 %shard_map.128 = (bf16[8,96,4096]{2,1,0:T(8,128)(2,1)}, bf16[8,96,4096]{2,1,0:T(8,128)(2,1)}) custom-call(bf16[96,4096]{1,0:T(8,128)(2,1)} %get-tuple-element.68.top, bf16[96,4096]{1,0:T(8,128)(2,1)} %get-tuple-element.67.bottom), custom_call_target="tpu_custom_call" | custom-call | tf_op jit(solution)/shard_map/pallas_call | solution.py:115
  81.6 0.6 fusion.28
  82.2 0.5 fusion.18
  82.7 0.5 and_select_fusion
  83.2 0.6 and_select_fusion.1.sa_o
  83.8 0.5 and_select_fusion.3.sa_i
  84.3 14.2 %shard_map.129 = (bf16[10,192,512]{2,1,0:T(8,128)(2,1)}, bf16[10,192,512]{2,1,0:T(8,128)(2,1)}, bf16[10,512,512]{2,1,0:T(8,128)(2,1)}) custom-call(s32[10]{0:T(128)} %and_select_fusion.3.sa_i, s32[10]{0:T(128)} %get-tuple-element.75.sb_i, s32[10]{0:T(128)} %get-tuple-element.81.bi, s32[10]{0:T(128)} %and_select_fusion.1.sa_o, s32[10]{0:T(128)} %get-tuple-element.60.sb_o, ...), custom_call_target="tpu_custom_call" | custom-call | flops 3019898880 | bytes 18350080 | tf_op jit(solution)/shard_map/pallas_call | solution.py:250
  98.8 0.5 convert_reduce_fusion
  100.9 2.3 gather_fusion
  103.2 4.0 %gather_fusion.1 = bf16[16,192,512]{2,1,0:T(8,128)(2,1)} fusion(bf16[10,192,512]{2,1,0:T(8,128)(2,1)} %get-tuple-element.42, s32[1024]{0:T(1024)S(1)} %pad_clamp_fusion), kind=kCustom, calls=%fused_computation.1.clone | custom fusion | bytes 6291520 | tf_op jit(solution)/shard_map/jit(_take)/gather | solution.py:35
  107.2 2.0 broadcast_select_fusion.1
  109.2 1.1 copy-done
  110.3 2.0 broadcast_select_fusion
  112.3 72.7 %shard_map.130 = (bf16[8,384,512]{2,1,0:T(8,128)(2,1)}, bf16[8,384,512]{2,1,0:T(8,128)(2,1)}) custom-call(bf16[8,384,512]{2,1,0:T(8,128)(2,1)} %bitcast.39, bf16[8,384,512]{2,1,0:T(8,128)(2,1)} %bitcast.40), custom_call_target="tpu_custom_call" | custom-call | tf_op jit(solution)/shard_map/pallas_call | solution.py:176
  185.1 3.8 %fusion.2 = f32[4,192,512]{2,0,1:T(4,128)S(1)} fusion(bf16[16,4,1]{1,0,2:T(8,128)(2,1)S(1)} %bitcast.49, bf16[16,192,512]{2,1,0:T(8,128)(2,1)} %bitcast.46), kind=kOutput, calls=%fused_computation.4 | convolution fusion | flops 12582912 | bytes 4718720 | tf_op jit(solution)/shard_map/irb,il->rlb/dot_general | solution.py:54
  188.9 0.6 copy.50
  189.5 1.3 copy-done.3
  190.8 1.9 fusion
  192.8 0.6 copy.51
  193.4 0.5 copy-done.2
  193.9 0.2 copy-done.5
  194.1 0.5 copy-done.6
  194.6 2.1 fusion.26
  197.0 6.8 %shard_map.131 = bf16[2048,2048]{1,0:T(8,128)(2,1)} custom-call(bf16[192,2048]{1,0:T(8,128)(2,1)} %left.1, bf16[192,2048]{1,0:T(8,128)(2,1)} %get-tuple-element.55.right), custom_call_target="tpu_custom_call" | custom-call | flops 1610612736 | bytes 9961472 | tf_op jit(solution)/shard_map/pallas_call | solution.py:275
  203.7 71.5 %shard_map.132 = (f32[128,2048]{1,0:T(8,128)}, f32[8,2048]{1,0:T(8,128)}) custom-call(bf16[4,4,128,2048]{3,2,1,0:T(8,128)(2,1)} %bitcast.38, f32[8,2048]{1,0:T(8,128)} %copy-done.7), custom_call_target="tpu_custom_call" | custom-call | tf_op jit(solution)/shard_map/pallas_call | solution.py:380
  275.3 1.5 fusion.31
  276.8 1.9 convert_element_type.77
  278.7 2.3 copy.58
  (59 shorter events, 2.2 us)
Async XLA Ops:
  7.2 77.2 %all-gather.2.cloned.1.call-start = ((), (), s32[]{:S(2)}) async-start(), calls=%async_computation.1 | async-start | bytes 5570560 | tf_op jit(solution)/shard_map/all_gather | solution.py:453
  7.9 268.9 %reduce-scatter.2.cloned.1.call-start = ((), (), s32[]{:S(2)}) async-start(), calls=%async_computation.2 | async-start | bytes 5570560 | tf_op jit(solution)/shard_map/reduce_scatter | solution.py:479
  8.0 7.2 %copy-start.4 = (bf16[192,2048]{1,0:T(8,128)(2,1)S(1)}, bf16[192,2048]{1,0:T(8,128)(2,1)}, u32[]{:S(2)}) copy-start(bf16[192,2048]{1,0:T(8,128)(2,1)} %param.20) | copy-start | bytes 2359300
  15.1 1.5 copy-start.1
  16.7 64.8 %copy-start.8 = (s32[8,10]{1,0:T(8,128)S(1)}, s32[8,10]{1,0:T(8,128)}, u32[]{:S(2)}) copy-start(s32[8,10]{1,0:T(8,128)} %param.21) | copy-start | bytes 964
  16.7 64.8 %copy-start.9 = (s32[8,10]{1,0:T(8,128)S(1)}, s32[8,10]{1,0:T(8,128)}, u32[]{:S(2)}) copy-start(s32[8,10]{1,0:T(8,128)} %param.22) | copy-start | bytes 964
  16.7 64.8 %copy-start.11 = (s32[8]{0:T(128)S(1)}, s32[8]{0:T(128)}, u32[]{:S(2)}) copy-start(s32[8]{0:T(128)} %param.23) | copy-start | bytes 100
  107.2 3.1 %copy-start = (bf16[16,192,512]{2,1,0:T(8,128)(2,1)S(1)}, bf16[16,192,512]{2,1,0:T(8,128)(2,1)}, u32[]{:S(2)}) copy-start(bf16[16,192,512]{2,1,0:T(8,128)(2,1)} %gather_fusion.1) | copy-start | bytes 9437188
  188.9 1.9 copy-start.3
  190.8 2.6 copy-start.10
  192.7 1.1 copy-start.2
  192.8 1.4 copy-start.5
  192.8 1.9 copy-start.6
  197.0 6.8 %copy-start.7 = (f32[8,2048]{1,0:T(8,128)}, f32[8,2048]{1,0:T(8,128)S(1)}, u32[]{:S(2)}) copy-start(f32[8,2048]{1,0:T(8,128)S(1)} %scatter.9.bias) | copy-start | bytes 196612
Sparse Core Ops, SparseCore 0:
  10.1 58.9 all-gather.1
  98.7 80.8 reduce-scatter.1

commit v15 on v14

--- a/solution.py
+++ b/solution.py
@@ -269,7 +269,7 @@
     ).astype(out.dtype)
 
 
-def group_outer(left, right, tile_m=512, tile_n=2048):
+def group_outer(left, right, tile_m=1024, tile_n=2048):
     rows, m = left.shape
     n = right.shape[1]
     return pl.pallas_call(

time: 289 us -> 288 us (level)
  no operation moved by 1% of the time
where the time goes in v15:
time: 288 us; the launch traced here: 287 us
  Pallas kernels  229 us (80%)
  local copies, waits for them, and re-layouts  16.2 us (6%)
  between operations  14.3 us (5%)
  other arithmetic  13.6 us (5%)
  matrix products  12.9 us (4%)
    pallas_call x1, Pallas kernels, exchange(): pl.pallas_call(functools.partial(exchange_kernel, n), out_shape=[jax.Shap...  72.7 us
    pallas_call x1, Pallas kernels, reduce_rows(): pl.pallas_call(functools.partial(reduce_kernel, side), out_shape=[jax.Sha...  71.5 us
    pallas_call x1, Pallas kernels, ring_gather(): pl.pallas_call(functools.partial(ring_kernel, n), out_shape=[shape, shape...  64.8 us
    pallas_call x1, Pallas kernels, slot_products(): pl.pallas_call(slot_kernel, grid_spec=grid_spec, out_shape=[jax.ShapeDtyp...  14.2 us
    unnamed x27, local copies, waits for them, and re-layouts  7.16 us
    dot_general x1, matrix products, on_device(): jnp.dot(dense, bottom_weight, preferred_element_type=jnp.float32)  7.14 us
    gather x2, local copies, waits for them, and re-layouts, pack_parts(): picked = jnp.take(parts, chosen.reshape(-1), axis=0)  6.27 us
    pallas_call x1, Pallas kernels, group_outer(): pl.pallas_call(outer_kernel, grid=(m // tile_m, n // tile_n), in_specs=[p...  6.06 us
  transfers between devices with their start and end apart: 2, of which 0 were waited for; matrix products, arithmetic and copies ran while one was open for 12% of the time, Pallas kernels for 75%

profile of v15, /device:TPU:0, one launch (start us, length us, event | category | flops | bytes accessed | tf_op | source)
XLA Modules:
  0.0 287.1 jit_solution(203504738353678736)
XLA Ops:
  7.2 0.7 all-gather.2.cloned.1.call-update
  8.0 7.1 %fusion.8 = (f32[2048]{0:T(1024)S(1)}, bf16[192,2048]{1,0:T(8,128)(2,1)S(1)}, f32[192,2048]{1,0:T(8,128)}) fusion(bf16[192,2048]{1,0:T(8,128)(2,1)} %param.20, f32[2048]{0:T(1024)} %param.17, bf16[192,2048]{1,0:T(8,128)(2,1)} %left.1, bf16[2048,2048]{1,0:T(8,128)(2,1)} %param.16), kind=kOutput, calls=%fused_computation.21 | convolution fusion | flops 1614542848 | bytes 12337152 | tf_op jit(solution)/shard_map/dot_general | solution.py:426
  15.1 0.3 fusion.9
  15.4 1.3 pad_maximum_fusion
  16.7 64.8 %shard_map.128 = (bf16[8,96,4096]{2,1,0:T(8,128)(2,1)}, bf16[8,96,4096]{2,1,0:T(8,128)(2,1)}) custom-call(bf16[96,4096]{1,0:T(8,128)(2,1)} %get-tuple-element.68.top, bf16[96,4096]{1,0:T(8,128)(2,1)} %get-tuple-element.67.bottom), custom_call_target="tpu_custom_call" | custom-call | tf_op jit(solution)/shard_map/pallas_call | solution.py:115
  81.6 0.6 fusion.28
  82.2 0.5 fusion.18
  82.7 0.5 and_select_fusion
  83.2 0.6 and_select_fusion.1.sa_o
  83.8 0.5 and_select_fusion.3.sa_i
  84.3 14.2 %shard_map.129 = (bf16[10,192,512]{2,1,0:T(8,128)(2,1)}, bf16[10,192,512]{2,1,0:T(8,128)(2,1)}, bf16[10,512,512]{2,1,0:T(8,128)(2,1)}) custom-call(s32[10]{0:T(128)} %and_select_fusion.3.sa_i, s32[10]{0:T(128)} %get-tuple-element.75.sb_i, s32[10]{0:T(128)} %get-tuple-element.81.bi, s32[10]{0:T(128)} %and_select_fusion.1.sa_o, s32[10]{0:T(128)} %get-tuple-element.60.sb_o, ...), custom_call_target="tpu_custom_call" | custom-call | flops 3019898880 | bytes 18350080 | tf_op jit(solution)/shard_map/pallas_call | solution.py:250
  98.8 0.5 convert_reduce_fusion
  100.9 2.3 gather_fusion
  103.2 4.0 %gather_fusion.1 = bf16[16,192,512]{2,1,0:T(8,128)(2,1)} fusion(bf16[10,192,512]{2,1,0:T(8,128)(2,1)} %get-tuple-element.42, s32[1024]{0:T(1024)S(1)} %pad_clamp_fusion), kind=kCustom, calls=%fused_computation.1.clone | custom fusion | bytes 6291520 | tf_op jit(solution)/shard_map/jit(_take)/gather | solution.py:35
  107.2 2.0 broadcast_select_fusion.1
  109.2 1.1 copy-done
  110.3 2.0 broadcast_select_fusion
  112.3 72.7 %shard_map.130 = (bf16[8,384,512]{2,1,0:T(8,128)(2,1)}, bf16[8,384,512]{2,1,0:T(8,128)(2,1)}) custom-call(bf16[8,384,512]{2,1,0:T(8,128)(2,1)} %bitcast.39, bf16[8,384,512]{2,1,0:T(8,128)(2,1)} %bitcast.40), custom_call_target="tpu_custom_call" | custom-call | tf_op jit(solution)/shard_map/pallas_call | solution.py:176
  185.1 3.8 %fusion.2 = f32[4,192,512]{2,0,1:T(4,128)S(1)} fusion(bf16[16,4,1]{1,0,2:T(8,128)(2,1)S(1)} %bitcast.49, bf16[16,192,512]{2,1,0:T(8,128)(2,1)} %bitcast.46), kind=kOutput, calls=%fused_computation.4 | convolution fusion | flops 12582912 | bytes 4718720 | tf_op jit(solution)/shard_map/irb,il->rlb/dot_general | solution.py:54
  188.9 0.6 copy.50
  189.5 1.3 copy-done.3
  190.8 1.9 fusion
  192.8 0.6 copy.51
  193.4 0.5 copy-done.2
  193.9 0.2 copy-done.5
  194.1 0.5 copy-done.6
  194.6 2.1 fusion.26
  197.0 6.1 %shard_map.131 = bf16[2048,2048]{1,0:T(8,128)(2,1)} custom-call(bf16[192,2048]{1,0:T(8,128)(2,1)} %left.1, bf16[192,2048]{1,0:T(8,128)(2,1)} %get-tuple-element.55.right), custom_call_target="tpu_custom_call" | custom-call | flops 1610612736 | bytes 9961472 | tf_op jit(solution)/shard_map/pallas_call | solution.py:275
  203.1 71.5 %shard_map.132 = (f32[128,2048]{1,0:T(8,128)}, f32[8,2048]{1,0:T(8,128)}) custom-call(bf16[4,4,128,2048]{3,2,1,0:T(8,128)(2,1)} %bitcast.38, f32[8,2048]{1,0:T(8,128)} %copy-done.7), custom_call_target="tpu_custom_call" | custom-call | tf_op jit(solution)/shard_map/pallas_call | solution.py:380
  274.6 1.5 fusion.31
  276.1 1.9 convert_element_type.77
  278.0 2.3 copy.58
  (59 shorter events, 2.2 us)
Async XLA Ops:
  7.2 77.2 %all-gather.2.cloned.1.call-start = ((), (), s32[]{:S(2)}) async-start(), calls=%async_computation.1 | async-start | bytes 5570560 | tf_op jit(solution)/shard_map/all_gather | solution.py:453
  7.9 268.2 %reduce-scatter.2.cloned.1.call-start = ((), (), s32[]{:S(2)}) async-start(), calls=%async_computation.2 | async-start | bytes 5570560 | tf_op jit(solution)/shard_map/reduce_scatter | solution.py:479
  8.0 7.2 %copy-start.4 = (bf16[192,2048]{1,0:T(8,128)(2,1)S(1)}, bf16[192,2048]{1,0:T(8,128)(2,1)}, u32[]{:S(2)}) copy-start(bf16[192,2048]{1,0:T(8,128)(2,1)} %param.20) | copy-start | bytes 2359300
  15.1 1.5 copy-start.1
  16.7 64.8 %copy-start.8 = (s32[8,10]{1,0:T(8,128)S(1)}, s32[8,10]{1,0:T(8,128)}, u32[]{:S(2)}) copy-start(s32[8,10]{1,0:T(8,128)} %param.21) | copy-start | bytes 964
  16.7 64.8 %copy-start.9 = (s32[8,10]{1,0:T(8,128)S(1)}, s32[8,10]{1,0:T(8,128)}, u32[]{:S(2)}) copy-start(s32[8,10]{1,0:T(8,128)} %param.22) | copy-start | bytes 964
  16.7 64.8 %copy-start.11 = (s32[8]{0:T(128)S(1)}, s32[8]{0:T(128)}, u32[]{:S(2)}) copy-start(s32[8]{0:T(128)} %param.23) | copy-start | bytes 100
  107.2 3.1 %copy-start = (bf16[16,192,512]{2,1,0:T(8,128)(2,1)S(1)}, bf16[16,192,512]{2,1,0:T(8,128)(2,1)}, u32[]{:S(2)}) copy-start(bf16[16,192,512]{2,1,0:T(8,128)(2,1)} %gather_fusion.1) | copy-start | bytes 9437188
  188.9 1.9 copy-start.3
  190.8 2.6 copy-start.10
  192.7 1.1 copy-start.2
  192.8 1.4 copy-start.5
  192.8 1.9 copy-start.6
  197.0 6.1 %copy-start.7 = (f32[8,2048]{1,0:T(8,128)}, f32[8,2048]{1,0:T(8,128)S(1)}, u32[]{:S(2)}) copy-start(f32[8,2048]{1,0:T(8,128)S(1)} %scatter.9.bias) | copy-start | bytes 196612
Sparse Core Ops, SparseCore 0:
  10.1 58.9 all-gather.1
  98.7 80.8 reduce-scatter.1
